TPU v7x, 32 devices: a whole 2x2x4 slice. The times are simulated.
32 devices in a mesh: dp: 8 (over z, y), mp: 4 (over x, core).
Axes of the slice: x: 2, y: 2, z: 4, core: 2. Of those that a mesh axis runs over, the one named last changes fastest.
Arguments:
- hidden_in: bfloat16 [16384, 768], P('dp'), may hold values from -6 to 6
- cotangent: bfloat16 [16384, 768], P('dp'), may hold values from -6 to 6
- w_query: bfloat16 [768, 768], P('dp', 'mp'), may hold values from -0.3125 to 0.3125
- w_key: bfloat16 [768, 768], P('dp', 'mp'), may hold values from -0.21875 to 0.21875
- w_value: bfloat16 [768, 768], P('dp', 'mp'), may hold values from -0.21875 to 0.21875
- w_output: bfloat16 [768, 768], P('mp', 'dp'), may hold values from -0.4375 to 0.4375
- w_inner: bfloat16 [768, 3072], P('dp', 'mp'), may hold values from -0.21875 to 0.21875
- w_outer: bfloat16 [3072, 768], P('mp', 'dp'), may hold values from -0.109375 to 0.109375
- biases: bfloat16 [4, 768], P(None, 'dp'), may hold values from -3 to 3
- gains: bfloat16 [2, 768], P(None, 'dp'), may hold values from 0.5 to 1.5
- shifts: bfloat16 [2, 768], P(None, 'dp'), may hold values from -2 to 2
- inner_bias: bfloat16 [3072], P('dp'), may hold values from -3 to 3
- lengths: int32 [10], replicated, may hold values from 1024 to 2048, as said below
- padding: int32 [16384], P('dp'), may hold values from 0 to 1, as said below
- cluster_perm: int32 [12, 16384], P('mp', 'dp'), may hold values from 0 to 16383, as said below
Outputs:
- hidden_out: bfloat16 [16384, 768], P('dp')
- grad_hidden: bfloat16 [16384, 768], P('dp')
- grad_query: float32 [768, 768], P('dp', 'mp')
- grad_key: float32 [768, 768], P('dp', 'mp')
- grad_value: float32 [768, 768], P('dp', 'mp')
- grad_output: float32 [768, 768], P('mp', 'dp')
- grad_inner: float32 [768, 3072], P('dp', 'mp')
- grad_outer: float32 [3072, 768], P('mp', 'dp')
- grad_biases: float32 [4, 768], P(None, 'dp')
- grad_gains: float32 [2, 768], P(None, 'dp')
- grad_shifts: float32 [2, 768], P(None, 'dp')
- grad_inner_bias: float32 [3072], P('dp')
Inputs may be any that keep to these rules, and one draw needn't show every extreme that they name: In each run of 8 indices of dp, 10 lengths that, each rounded up to a multiple of 128, sum to 16384; in each run one of them is exactly 2048. `padding`: A row that is the p-th of its document's rows on its device, on index d of dp, is 1 exactly when p * 8 + (d mod 8) is under the document's length. `cluster_perm`: for each head a permutation of the token numbers; each cluster holds tokens of one document only, 16 from each device of its run; of the tokens held by one index of dp, exactly 256 have slots among those of each index r of dp (slots r * 2048 to (r + 1) * 2048 - 1).
All inputs are finite; a program needn't handle non-finite values.
Results may differ from a plain program's by a relative error of at most 0.015.
Values may be sent and summed in bfloat16 or wider, within the bound.
No kernel may reach another device: no remote copies, remote signals or barrier semaphores. Data moves between devices by JAX's collectives and lax.ppermute only.
A program may use at most 128 MiB of HBM per device.

v0:
```python
from functools import partial
import math

import jax
import jax.numpy as jnp
from jax import lax
from jax.experimental import pallas as pl
from jax.experimental.pallas import tpu as pltpu
from jax.sharding import PartitionSpec as P

D = 768
HEAD_DIM = 64
FF = 3072
CLUSTER = 128
LANES = 128
EPSILON = 1e-05
MASKED = -1e30
SCALE = 1.0 / math.sqrt(HEAD_DIM)

bf16 = jnp.bfloat16
f32 = jnp.float32
i32 = jnp.int32

VMEM = 60 * 1024 * 1024


def cost(us):
    return pl.CostEstimate(flops=int(1e9 * us), bytes_accessed=int(3e6 * us), transcendentals=0)


QUICK = cost(0.001)
ATTEND_US = 46
COLLECT_US = 30
COLLECT_ROWS = 512
SPREAD_US = 3
HEAD_GRADS_US = 4
SORT_US = 80


def nn(a, b):
    return lax.dot_general(a, b, (((1,), (0,)), ((), ())), preferred_element_type=f32)


def nt(a, b):
    return lax.dot_general(a, b, (((1,), (1,)), ((), ())), preferred_element_type=f32)


def tn(a, b):
    return lax.dot_general(a, b, (((0,), (0,)), ((), ())), preferred_element_type=f32)


def lane_iota(rows, lanes=LANES):
    return lax.broadcasted_iota(i32, (rows, lanes), 1)


def sublane_iota(rows, lanes=LANES):
    return lax.broadcasted_iota(i32, (rows, lanes), 0)


def as_column(row):
    parts = [
        jnp.broadcast_to(row[:, i * LANES : (i + 1) * LANES], (LANES, LANES)).T
        for i in range(row.shape[1] // LANES)
    ]
    return parts[0] if len(parts) == 1 else jnp.concatenate(parts, axis=0)


def loop(count):
    def run(step):
        def body(i, carry):
            step(i)
            return carry

        lax.fori_loop(0, count, body, 0)

    return run


class Layout:
    def __init__(self, peers, tokens, heads):
        self.peers, self.tokens, self.heads = peers, tokens, heads
        self.stripe = min(16, peers)
        self.runs = peers // self.stripe
        self.per_dev = CLUSTER // self.stripe
        self.rows_peer = tokens // peers
        self.half_rows = self.rows_peer // 2
        self.pairs = self.half_rows // self.per_dev
        self.packed = tokens // 2
        self.clusters = peers * tokens // CLUSTER
        self.data_rows = 9 * self.half_rows
        self.direct = self.half_rows == LANES
        self.arrays = peers if self.direct else 1

    def peer(self, me, s):
        return (me ^ s) if self.direct else s

    def shapes(self, rows, dtype=bf16):
        lead = () if self.direct else (self.peers,)
        return [jax.ShapeDtypeStruct(lead + (rows, LANES), dtype)] * self.arrays

    def specs(self, rows, at):
        if self.direct:
            return [pl.BlockSpec((rows, LANES), lambda *g: (at(*g), 0))] * self.arrays
        return [pl.BlockSpec((self.peers, rows, LANES), lambda *g: (0, at(*g), 0))]

    def view(self, refs, s):
        return refs[s] if self.direct else refs[0].at[s]


def only(at):
    return lambda *g: at


def place_kernel(lay, perm_ref, code_ref):
    groups = lay.clusters
    shift = CLUSTER.bit_length() - 1
    blocks = lay.tokens // LANES
    before = sublane_iota(LANES, 2 * LANES)
    after = lane_iota(LANES, 2 * LANES)
    ahead_of = jnp.where((before < after) | (after >= LANES), 1.0, 0.0).astype(bf16)

    def members(h, b):
        row = lax.shift_right_logical(perm_ref[h : h + 1, b * LANES : (b + 1) * LANES], shift)
        return jnp.broadcast_to(row, (groups, LANES)) == sublane_iota(groups)

    for h in range(lay.heads):
        if lay.runs == 1:
            carry = (sublane_iota(groups) * lay.per_dev).astype(f32)
        else:
            counts = jnp.zeros((groups, LANES), f32)
            for b in range(blocks):
                member = jnp.where(members(h, b), 1.0, 0.0).astype(bf16)
                counts = counts + nn(member, ahead_of)[:, LANES:]
            lower = jnp.where(
                sublane_iota(groups, groups) > lane_iota(groups, groups), 1.0, 0.0
            ).astype(bf16)
            carry = nn(lower, counts.astype(bf16))
        for b in range(blocks):
            member = members(h, b)
            found = nn(jnp.where(member, 1.0, 0.0).astype(bf16), ahead_of)
            rank = jnp.sum(jnp.where(member, found[:, :LANES] + carry, 0.0), axis=0, keepdims=True)
            carry = carry + found[:, LANES:]
            rank = rank.astype(i32)
            peer = lax.shift_right_logical(rank, lay.rows_peer.bit_length() - 1)
            rest = rank & (lay.rows_peer - 1)
            half = lax.shift_right_logical(rest, lay.half_rows.bit_length() - 1)
            packed = peer * lay.half_rows + (rest & (lay.half_rows - 1))
            at = slice(b * LANES, (b + 1) * LANES)
            code_ref[h, 0:1, at] = packed
            code_ref[h, 1:2, at] = half


def place_tokens(lay, perm):
    return pl.pallas_call(
        partial(place_kernel, lay),
        out_shape=jax.ShapeDtypeStruct((lay.heads, 8, lay.tokens), i32),
        name="place_tokens",
        cost_estimate=QUICK,
    )(perm)


def one_hot(equal):
    return jnp.where(equal, 1.0, 0.0).astype(bf16)


def scatter_matrix(lay, me, packed, s, blocks):
    rows = blocks * lay.half_rows
    if lay.direct:
        parts = [
            one_hot(
                jnp.broadcast_to(packed, (lay.half_rows, lay.tokens))
                == sublane_iota(lay.half_rows, lay.tokens) + lay.peer(me, s + i) * lay.half_rows
            )
            for i in range(blocks)
        ]
        return jnp.concatenate(parts, axis=0)
    wanted = sublane_iota(rows, lay.tokens) + s * lay.half_rows
    return one_hot(jnp.broadcast_to(packed, (rows, lay.tokens)) == wanted)


def gather_matrix(lay, me, column):
    lane = lane_iota(column.shape[0])
    parts = [
        one_hot(column == lane + lay.peer(me, k) * LANES) for k in range(lay.packed // LANES)
    ]
    return jnp.concatenate(parts, axis=1)


def block_rows(lay, refs, first):
    at = slice(first, first + lay.half_rows)
    if lay.direct:
        return jnp.concatenate([refs[s][at, :] for s in range(lay.peers)], axis=0)
    return refs[0][:, at, :].astype(f32).reshape(lay.packed, LANES).astype(bf16)


def put_blocks(lay, refs, s, blocks, first, rows):
    at = slice(first, first + lay.half_rows) if isinstance(first, int) else pl.ds(first, lay.half_rows)
    if lay.direct:
        for i in range(blocks):
            refs[s + i][at, :] = rows[i * LANES : (i + 1) * LANES].astype(bf16)
    else:
        rows = rows.astype(f32).reshape(blocks, lay.half_rows, LANES).astype(bf16)
        refs[0][s : s + blocks, at, :] = rows


ROWS = 512
COUNT = 4


def project_kernel(lay, steps, place_ref, x_ref, w_ref, bias_ref, code_ref, pad_ref, *rest):
    outs = rest[: lay.arrays]
    rows_ref, flag_ref = rest[lay.arrays :]
    step = pl.program_id(0)
    me = place_ref[0]
    width = 4 * LANES

    @pl.when(step < steps)
    def _():
        at = pl.ds(pl.multiple_of(step * ROWS, ROWS), ROWS)
        values = nn(x_ref[...], w_ref[...]) + bias_ref[0:1, :]
        low = lane_iota(ROWS) < HEAD_DIM
        lane_half = jnp.where(low, 0, 1)
        live = as_column(pad_ref[0:1, at])
        tiles = [values[:, i * LANES : (i + 1) * LANES] for i in range(values.shape[1] // LANES)]
        turned = [pltpu.roll(tile, HEAD_DIM, 1) for tile in tiles]
        for h in range(lay.heads):
            half = as_column(code_ref[h, 1:2, at])
            keep = half == lane_half
            v, side = lay.heads + h // 2, h % 2
            planes = (
                jnp.where(low, tiles[h], turned[h]),
                jnp.where(low, turned[h], tiles[h]),
                jnp.where(low, tiles[v], turned[v]) if side == 0 else jnp.where(low, turned[v], tiles[v]),
            )
            for x, plane in enumerate(planes):
                rows_ref[h, at, x * LANES : (x + 1) * LANES] = jnp.where(keep, plane, 0.0).astype(bf16)
            flags = jnp.where((lane_iota(ROWS) == half) & (live == 1), 1.0, 0.0)
            rows_ref[h, at, 3 * LANES :] = flags.astype(bf16)

    count = COUNT if lay.direct else 32

    @pl.when(step >= steps)
    def _():
        h = step - steps
        for s in range(0, lay.peers, count):
            chosen = scatter_matrix(lay, me, code_ref[h, 0:1, :], s, count)
            moved = nn(chosen, rows_ref[h])
            for x in range(3):
                first = pl.multiple_of((h * 3 + x) * lay.half_rows, 16)
                put_blocks(lay, outs, s, count, first, moved[:, x * LANES : (x + 1) * LANES])
            for i in range(count * lay.half_rows // LANES):
                at = slice(s * lay.half_rows + i * LANES, s * lay.half_rows + (i + 1) * LANES)
                flag_ref[h, :, at] = moved[i * LANES : (i + 1) * LANES, 3 * LANES :].T[:8]

    @pl.when(step == steps + lay.heads - 1)
    def _():
        for s in range(lay.peers):
            at = slice(s * lay.half_rows, (s + 1) * lay.half_rows)
            rows = [flag_ref[k, 0:2, at] for k in range(lay.heads)]
            block = jnp.concatenate(rows + [jnp.zeros((16 - 2 * lay.heads, lay.half_rows), f32)], axis=0)
            if lay.half_rows < LANES:
                block = jnp.concatenate(
                    [block, jnp.zeros((16, LANES - lay.half_rows), f32)], axis=1
                )
            lay.view(outs, s)[lay.data_rows : lay.data_rows + 16, :] = block.astype(bf16)


def project_rows(lay, places, x, weights, bias, code, pad):
    width = weights.shape[1]
    steps = lay.tokens // ROWS
    spec = pltpu.PrefetchScalarGridSpec(
        num_scalar_prefetch=1,
        grid=(steps + lay.heads,),
        in_specs=[
            pl.BlockSpec((ROWS, D), lambda s, _: (jnp.minimum(s, steps - 1), 0)),
            pl.BlockSpec((D, width), lambda s, _: (0, 0)),
            pl.BlockSpec((8, width), lambda s, _: (0, 0)),
            pl.BlockSpec((lay.heads, 8, lay.tokens), lambda s, _: (0, 0, 0)),
            pl.BlockSpec((1, lay.tokens), lambda s, _: (0, 0)),
        ],
        out_specs=lay.specs(lay.data_rows + 16, only(0)),
        scratch_shapes=[
            pltpu.VMEM((lay.heads, lay.tokens, 4 * LANES), bf16),
            pltpu.VMEM((lay.heads, 8, lay.packed), f32),
        ],
    )
    return pl.pallas_call(
        partial(project_kernel, lay, steps),
        grid_spec=spec,
        out_shape=lay.shapes(lay.data_rows + 16),
        compiler_params=pltpu.CompilerParams(vmem_limit_bytes=VMEM),
        name="project_rows",
        cost_estimate=QUICK,
    )(places, x, weights, bias, code, pad)


def pair_rows(lay, refs, first, run, p):
    at = slice(first + p * lay.per_dev, first + (p + 1) * lay.per_dev)
    if lay.direct:
        return jnp.concatenate([refs[s][at, :] for s in range(lay.stripe)], axis=0)
    block = refs[0][run * lay.stripe : (run + 1) * lay.stripe, first : first + lay.half_rows, :]
    block = block.astype(f32)[:, p * lay.per_dev : (p + 1) * lay.per_dev, :]
    return block.reshape(CLUSTER, LANES).astype(bf16)


def put_pair(lay, refs, first, run, p, rows):
    at = slice(first + p * lay.per_dev, first + (p + 1) * lay.per_dev)
    for s in range(lay.stripe):
        part = rows[s * lay.per_dev : (s + 1) * lay.per_dev]
        lay.view(refs, run * lay.stripe + s)[at, :] = part.astype(bf16)


def live_columns(lay, flags, h):
    pick = one_hot(sublane_iota(16, 2 * LANES) == 2 * h + lane_iota(16, 2 * LANES) // LANES)
    return [tn(lay.view(flags, s)[...], pick) for s in range(lay.peers)]


def allowed_pair(lay, columns, run, p):
    at = slice(p * lay.per_dev, (p + 1) * lay.per_dev)
    live = jnp.concatenate([columns[run * lay.stripe + s][at] for s in range(lay.stripe)], axis=0)
    live = jnp.concatenate([live[:, :LANES], live[:, LANES:]], axis=0)
    same = sublane_iota(2 * CLUSTER) % CLUSTER == lane_iota(2 * CLUSTER)
    return (live > 0.5) | same


def stack_halves(rows):
    low = lane_iota(rows.shape[0], rows.shape[1]) < HEAD_DIM
    zero = jnp.zeros_like(rows)
    return jnp.concatenate([jnp.where(low, rows, zero), jnp.where(low, zero, rows)], axis=0)


def each_half(fold, rows):
    one, two = (
        jnp.broadcast_to(fold(part, axis=0, keepdims=True), part.shape)
        for part in (rows[:CLUSTER], rows[CLUSTER:])
    )
    return jnp.concatenate([one, two], axis=0)


def inverse_sum(rows, axis, keepdims):
    return 1.0 / jnp.sum(rows, axis=axis, keepdims=keepdims)


def soft_weights(queries, keys, allowed):
    scores = jnp.where(allowed, nt(keys, queries) * SCALE, MASKED)
    grown = jnp.exp(scores - each_half(jnp.max, scores))
    return grown * each_half(inverse_sum, grown)


def attend_kernel(lay, *refs):
    rows, flags, outs = (refs[i * lay.arrays : (i + 1) * lay.arrays] for i in range(3))
    live = live_columns(lay, flags, pl.program_id(0))
    for run in range(lay.runs):
        for p in range(lay.pairs):
            q, k, v = (pair_rows(lay, rows, x * lay.half_rows, run, p) for x in range(3))
            soft = soft_weights(q, stack_halves(k), allowed_pair(lay, live, run, p))
            put_pair(lay, outs, 0, run, p, tn(soft.astype(bf16), stack_halves(v)))


def attend(lay, arrived):
    head = lambda h: h
    return pl.pallas_call(
        partial(attend_kernel, lay),
        grid=(lay.heads,),
        in_specs=lay.specs(3 * lay.half_rows, head) + lay.specs(16, only(lay.data_rows // 16)),
        out_specs=lay.specs(lay.half_rows, head),
        out_shape=lay.shapes(lay.heads * lay.half_rows),
        name="attend",
        cost_estimate=cost(ATTEND_US),
    )(*arrived, *arrived)


def attend_back_kernel(lay, *refs):
    rows, flags, grads, outs = (refs[i * lay.arrays : (i + 1) * lay.arrays] for i in range(4))
    sum_ref = refs[-1]
    live = live_columns(lay, flags, pl.program_id(0))
    low = lane_iota(CLUSTER) < HEAD_DIM
    sums = [jnp.zeros((1, LANES), f32)] * 2
    for run in range(lay.runs):
        for p in range(lay.pairs):
            q, k, v = (pair_rows(lay, rows, x * lay.half_rows, run, p) for x in range(3))
            g = pair_rows(lay, grads, 0, run, p)
            keys = stack_halves(k)
            soft = soft_weights(q, keys, allowed_pair(lay, live, run, p))
            grad_soft = nt(stack_halves(v), g)
            delta = each_half(jnp.sum, soft * grad_soft)
            grad = (soft * (grad_soft - delta)).astype(bf16)
            grad_q = (tn(grad, keys) * SCALE).astype(bf16)
            part = nn(grad, q)
            grad_k = (jnp.where(low, part[:CLUSTER], part[CLUSTER:]) * SCALE).astype(bf16)
            part = nn(soft.astype(bf16), g)
            grad_v = jnp.where(low, part[:CLUSTER], part[CLUSTER:]).astype(bf16)
            for x, part in enumerate((grad_q, grad_k, grad_v)):
                put_pair(lay, outs, x * lay.half_rows, run, p, part)
            sums[0] = sums[0] + jnp.sum(grad_q.astype(f32), axis=0, keepdims=True)
            sums[1] = sums[1] + jnp.sum(grad_v.astype(f32), axis=0, keepdims=True)
    sum_ref[0] = jnp.concatenate(sums + [jnp.zeros((6, LANES), f32)], axis=0)


def attend_back(lay, arrived, grads):
    head = lambda h: h
    three = lay.specs(3 * lay.half_rows, head)
    out = pl.pallas_call(
        partial(attend_back_kernel, lay),
        grid=(lay.heads,),
        in_specs=three
        + lay.specs(16, only(lay.data_rows // 16))
        + lay.specs(lay.half_rows, head),
        out_specs=three + [pl.BlockSpec((1, 8, LANES), lambda h: (h, 0, 0))],
        out_shape=lay.shapes(lay.data_rows)
        + [jax.ShapeDtypeStruct((lay.heads, 8, LANES), f32)],
        name="attend_back",
        cost_estimate=QUICK,
    )(*arrived, *arrived, *grads)
    return list(out[:-1]), out[-1]


def side_rows(quarter, side):
    return pl.ds(pl.multiple_of(quarter * 512 + side * 256, 256), 256)


def unsort_kernel(lay, place_ref, *refs):
    rows_refs, code_ref, outs = refs[: lay.arrays], refs[lay.arrays], refs[lay.arrays + 1 :]
    rows = block_rows(lay, rows_refs, 0)
    low = lane_iota(256) < HEAD_DIM
    me, place = place_ref[0], place_ref[1]

    for t in range(4):
        sides = []
        for side in range(2):
            at = side_rows(place ^ t, side)
            column = as_column(code_ref[0, 0:1, at])
            half = as_column(code_ref[0, 1:2, at])
            found = nn(gather_matrix(lay, me, column), rows)
            sides.append(jnp.where(half == side, found, pltpu.roll(found, HEAD_DIM, 1)))
        outs[t][...] = jnp.where(low, sides[0], sides[1]).astype(bf16)


def unsort_rows(lay, places, returned, code):
    spec = pltpu.PrefetchScalarGridSpec(
        num_scalar_prefetch=1,
        grid=(lay.heads,),
        in_specs=lay.specs(lay.half_rows, lambda h, _: h)
        + [pl.BlockSpec((1, 8, lay.tokens), lambda h, _: (h, 0, 0))],
        out_specs=[pl.BlockSpec((256, LANES), lambda h, _: (0, h))] * 4,
    )
    return pl.pallas_call(
        partial(unsort_kernel, lay),
        grid_spec=spec,
        out_shape=[jax.ShapeDtypeStruct((256, lay.heads * LANES), bf16)] * 4,
        name="unsort_rows",
        cost_estimate=QUICK,
    )(places, *returned, code)


def sort_kernel(lay, place_ref, *refs):
    grads, code_ref, outs, rows_ref = refs[:4], refs[4], refs[5:-1], refs[-1]
    low = lane_iota(256) < HEAD_DIM
    lane_half = jnp.where(low, 0, 1)
    me, place = place_ref[0], place_ref[1]

    for t in range(4):
        block = grads[t][...].astype(f32)
        turned = pltpu.roll(block, HEAD_DIM, 1)
        for side in range(2):
            at = side_rows(place ^ t, side)
            half = as_column(code_ref[0, 1:2, at])
            both = jnp.where(low, block, turned) if side == 0 else jnp.where(low, turned, block)
            rows_ref[at, :] = jnp.where(half == lane_half, both, 0.0).astype(bf16)

    count = 4 if lay.direct else 32
    for s in range(0, lay.peers, count):
        chosen = scatter_matrix(lay, me, code_ref[0, 0:1, :], s, count)
        put_blocks(lay, outs, s, count, 0, nn(chosen, rows_ref[...]))


def sort_rows(lay, places, grads, code):
    spec = pltpu.PrefetchScalarGridSpec(
        num_scalar_prefetch=1,
        grid=(lay.heads,),
        in_specs=[pl.BlockSpec((256, LANES), lambda h, _: (0, h))] * 4
        + [pl.BlockSpec((1, 8, lay.tokens), lambda h, _: (h, 0, 0))],
        out_specs=lay.specs(lay.half_rows, lambda h, _: h),
        scratch_shapes=[pltpu.VMEM((lay.tokens, LANES), bf16)],
    )
    return pl.pallas_call(
        partial(sort_kernel, lay),
        grid_spec=spec,
        out_shape=lay.shapes(lay.heads * lay.half_rows),
        name="sort_rows",
        cost_estimate=cost(SORT_US),
    )(places, *grads, code)


def pack_kernel(
    query_ref, key_ref, value_ref, output_ref, inner_ref, outer_ref,
    bias_ref, gain_ref, shift_ref, inner_bias_ref, piece_ref, shard_ref,
):
    depth, width = query_ref.shape
    heads = width // HEAD_DIM
    query, key, value = (ref[...].astype(f32) for ref in (query_ref, key_ref, value_ref))
    cut = [slice(h * HEAD_DIM, (h + 1) * HEAD_DIM) for h in range(heads)]
    columns = [part for at in cut for part in (query[:, at], key[:, at])] + [value]
    have = 3 * width
    fill = -have % LANES
    if fill:
        columns.append(jnp.zeros((depth, fill), f32))
    columns = jnp.concatenate(columns, axis=1).astype(bf16)
    piece_ref[:depth, : have + fill] = columns
    inner_bias = inner_bias_ref[...].astype(f32)
    vectors = jnp.concatenate(
        [ref[...].astype(f32) for ref in (bias_ref, gain_ref, shift_ref)]
        + [inner_bias[:, i * depth : (i + 1) * depth] for i in range(4)]
        + [jnp.zeros((4, depth), f32)],
        axis=0,
    )
    if depth < LANES:
        vectors = jnp.concatenate([vectors, jnp.zeros((16, LANES - depth), f32)], axis=1)
    piece_ref[:16, have + fill :] = vectors.astype(bf16)
    shard_ref[:, :D] = inner_ref[...]
    turned = output_ref[...].astype(f32).T
    shard_ref[:, D : 2 * D] = outer_ref[...]
    shard_ref[:, 2 * D :] = jnp.concatenate(
        [turned[:, at] for at in cut for _ in range(2)], axis=1
    ).astype(bf16)


def pack_weights(*arrays):
    depth, width = arrays[0].shape
    columns = -(-3 * width // LANES) * LANES
    return pl.pallas_call(
        pack_kernel,
        out_shape=[
            jax.ShapeDtypeStruct((max(depth, 16), columns + LANES), bf16),
            jax.ShapeDtypeStruct((depth, 2 * D + 2 * width), bf16),
        ],
        name="pack_weights",
        cost_estimate=QUICK,
    )(*arrays)


def assemble_kernel(lay, place_ref, *refs):
    pieces, (weight_ref, bias_ref, par_ref, part_ref) = refs[: lay.peers], refs[lay.peers :]
    me, place = place_ref[0], place_ref[1]
    depth = D // lay.peers
    for s in range(lay.peers):
        d = me ^ s
        at = pl.ds(pl.multiple_of(d * depth, 16), depth)
        columns = weight_ref.shape[1]
        weight_ref[at, :] = pieces[s][:, :columns]
        part_ref[d] = pieces[s][:16, columns:].astype(f32)

    def whole(row, rows=1, peers=range(lay.peers)):
        return jnp.concatenate(
            [part_ref[d, row + i : row + i + 1, :depth] for d in peers for i in range(rows)], axis=1
        )

    vectors = [whole(r) for r in range(8)]
    each = lay.peers // 4
    vectors += [whole(8, 4, range(j * each, (j + 1) * each)) for j in range(4)]
    par_ref[...] = jnp.concatenate(vectors + [jnp.zeros((4, D), f32)], axis=0)
    width = lay.heads * HEAD_DIM

    def own(vector):
        out = vector[:, :width]
        for p in range(1, D // width):
            out = jnp.where(place == p, vector[:, p * width : (p + 1) * width], out)
        return out

    query = own(vectors[0])
    zero = jnp.zeros((1, HEAD_DIM), f32)
    columns = [
        part for h in range(lay.heads) for part in (query[:, h * HEAD_DIM : (h + 1) * HEAD_DIM], zero)
    ] + [own(vectors[1])]
    fill = bias_ref.shape[1] - 3 * width
    if fill:
        columns.append(jnp.zeros((1, fill), f32))
    bias_ref[...] = jnp.broadcast_to(jnp.concatenate(columns, axis=1), bias_ref.shape)


def assemble_weights(lay, places, pieces):
    columns = pieces[0].shape[1] - LANES
    vmem = pl.BlockSpec(memory_space=pltpu.VMEM)
    return pl.pallas_call(
        partial(assemble_kernel, lay),
        in_specs=[pl.BlockSpec(memory_space=pltpu.SMEM)] + [vmem] * lay.peers,
        out_specs=[vmem] * 3,
        out_shape=[
            jax.ShapeDtypeStruct((D, columns), bf16),
            jax.ShapeDtypeStruct((8, columns), f32),
            jax.ShapeDtypeStruct((16, D), f32),
        ],
        scratch_shapes=[pltpu.VMEM((lay.peers, 16, LANES), f32)],
        name="assemble_weights",
        cost_estimate=QUICK,
    )(places, *pieces)


def mean_rows(v):
    return jnp.sum(v, axis=1, keepdims=True) * (1.0 / D)


def norm_forward(rows):
    centred = rows - mean_rows(rows)
    inv = lax.rsqrt(mean_rows(centred * centred) + EPSILON)
    return centred * inv, inv


def norm_backward(scaled, normed, inv):
    return inv * (scaled - mean_rows(scaled) - normed * mean_rows(scaled * normed))


TALL = 512


def middle_kernel(
    place_ref,
    att0,
    att1,
    att2,
    att3,
    hidden_ref,
    cot_ref,
    par_ref,
    w0,
    w1,
    w2,
    w3,
    out_ref,
    act_ref,
    pre_ref,
    low_ref,
    ffn_grad_ref,
    branch_grad_ref,
    h1_ref,
    grad0,
    grad1,
    grad2,
    grad3,
    vec_ref,
    first_ref,
    normed_ref,
    inv_ref,
    slope_ref,
    sum_ref,
    h2_ref,
    weight_ref,
    sems,
):
    step = pl.program_id(0)
    place = place_ref[1]
    project = slice(2 * D, None)

    def fetch(t, part):
        width = att0.shape[1]
        at = (pl.ds(2 * D, width), pl.ds(0, 2 * D))[part]
        source = (w0, w1, w2, w3)[t]
        return pltpu.make_async_copy(source.at[:, at], weight_ref.at[t, :, at], sems.at[part, t])

    for t in range(4):

        @pl.when(step == t + 1)
        def _():
            fetch(t, 1).wait()

    @pl.when(step == 0)
    def _():
        for t in range(4):
            fetch(t, 0).start()
        for t in range(4):
            fetch(t, 1).start()
        for t in range(4):
            fetch(t, 0).wait()
        vec_ref[...] = jnp.zeros_like(vec_ref)

        @loop(2)
        def _(side):
            branch = jnp.zeros((256, D), f32)
            for t, att_ref in enumerate((att0, att1, att2, att3)):
                att = att_ref[...]
                lane = lane_iota(256, att.shape[1]) % LANES
                own = (lane >= HEAD_DIM).astype(i32) == side
                branch = branch + nt(jnp.where(own, att, jnp.zeros_like(att)), weight_ref[t, :, project])
            at = pl.ds(pl.multiple_of(side * 256, 256), 256)
            rows = hidden_ref[at, :].astype(f32) + (branch + par_ref[2:3, :])
            normed, inv = norm_forward(rows)
            first = normed * par_ref[4:5, :] + par_ref[6:7, :]
            first_ref[at, :] = first
            normed_ref[at, :] = normed
            inv_ref[at, :] = jnp.broadcast_to(inv, (256, LANES))
            low_ref[at, :] = first.astype(bf16)

        sum_ref[...] = jnp.zeros_like(sum_ref)

    @pl.when((step >= 1) & (step <= 4))
    def _():
        j = step - 1

        @loop(512 // TALL)
        def _(side):
            at = pl.ds(pl.multiple_of(side * TALL, TALL), TALL)
            pre = nn(low_ref[at, :], weight_ref[j, :, :D]) + par_ref[pl.ds(8 + (place ^ j), 1), :]
            cdf = 0.5 * (1.0 + lax.erf(pre * (1.0 / math.sqrt(2.0))))
            slope_ref[j, at, :] = cdf + pre * jnp.exp(-0.5 * pre * pre) * (1.0 / math.sqrt(2.0 * math.pi))
            act = (pre * cdf).astype(bf16)
            act_ref[at, :] = act
            sum_ref[at, :] += nt(act, weight_ref[j, :, D : 2 * D])

    @pl.when(step == 4)
    def _():

        @loop(4)
        def _(side):
            at = pl.ds(pl.multiple_of(side * 128, 128), 128)
            rows = first_ref[at, :] + (sum_ref[at, :] + par_ref[3:4, :])
            normed, inv = norm_forward(rows)
            out_ref[at, :] = (normed * par_ref[5:6, :] + par_ref[7:8, :]).astype(bf16)
            cot = cot_ref[at, :].astype(f32)
            grad = norm_backward(cot * par_ref[5:6, :], normed, inv)
            grad_low = grad.astype(bf16)
            h2_ref[at, :] = grad
            ffn_grad_ref[at, :] = grad_low
            vec_ref[3:4, :] += jnp.sum(grad_low.astype(f32), axis=0, keepdims=True)
            vec_ref[5:6, :] += jnp.sum(cot * normed, axis=0, keepdims=True)
            vec_ref[7:8, :] += jnp.sum(cot, axis=0, keepdims=True)

        sum_ref[...] = jnp.zeros_like(sum_ref)

    @pl.when(step >= 5)
    def _():
        j = 8 - step
        vec_ref[pl.ds(8 + (place ^ j), 1), :] = jnp.zeros((1, D), f32)

        @loop(512 // TALL)
        def _(side):
            at = pl.ds(pl.multiple_of(side * TALL, TALL), TALL)
            grad_act = nn(ffn_grad_ref[at, :], weight_ref[j, :, D : 2 * D])
            grad_pre = (grad_act * slope_ref[j, at, :]).astype(bf16)
            pre_ref[at, :] = grad_pre
            vec_ref[pl.ds(8 + (place ^ j), 1), :] += jnp.sum(grad_pre.astype(f32), axis=0, keepdims=True)
            sum_ref[at, :] += nt(grad_pre, weight_ref[j, :, :D])

    @pl.when(step == 8)
    def _():

        @loop(4)
        def _(side):
            at = pl.ds(pl.multiple_of(side * 128, 128), 128)
            grad_first = h2_ref[at, :] + sum_ref[at, :]
            normed = normed_ref[at, :]
            grad = norm_backward(grad_first * par_ref[4:5, :], normed, inv_ref[at, 0:1])
            grad_low = grad.astype(bf16)
            h1_ref[at, :] = grad
            branch_grad_ref[at, :] = grad_low
            vec_ref[2:3, :] += jnp.sum(grad_low.astype(f32), axis=0, keepdims=True)
            vec_ref[4:5, :] += jnp.sum(grad_first * normed, axis=0, keepdims=True)
            vec_ref[6:7, :] += jnp.sum(grad_first, axis=0, keepdims=True)

        for t, grad_ref in enumerate((grad0, grad1, grad2, grad3)):
            both = nn(branch_grad_ref[...], weight_ref[t, :, project])
            lane = lane_iota(256, both.shape[1]) % LANES
            grad_ref[...] = jnp.where(lane < HEAD_DIM, both[:256], both[256:]).astype(bf16)


def middle(places, att, hidden, cotangent, params, weights):
    width = att[0].shape[1]
    rows = 512

    def up(s, q):
        return (0, jnp.clip(s - 1, 0, 3))

    def down(s, q):
        return (0, jnp.clip(8 - s, 0, 3))

    def whole(rank):
        return lambda s, q: (0,) * rank

    square = pl.BlockSpec((rows, D), whole(2))
    exchanged = pl.BlockSpec((256, width), whole(2))
    spec = pltpu.PrefetchScalarGridSpec(
        num_scalar_prefetch=1,
        grid=(9,),
        in_specs=[exchanged] * 4
        + [
            pl.BlockSpec((rows, D), lambda s, q: (q[1], 0)),
            pl.BlockSpec((rows, D), lambda s, q: (q[1], 0)),
            pl.BlockSpec((16, D), whole(2)),
        ]
        + [pl.BlockSpec(memory_space=pl.ANY)] * 4,
        out_specs=[
            square,
            pl.BlockSpec((rows, D), up),
            pl.BlockSpec((rows, D), down),
            square,
            square,
            square,
            square,
        ]
        + [exchanged] * 4
        + [pl.BlockSpec((16, D), whole(2))],
        scratch_shapes=[
            pltpu.VMEM((rows, D), f32),
            pltpu.VMEM((rows, D), f32),
            pltpu.VMEM((rows, LANES), f32),
            pltpu.VMEM((4, rows, D), f32),
            pltpu.VMEM((rows, D), f32),
            pltpu.VMEM((rows, D), f32),
            pltpu.VMEM((4, D, 2 * D + width), bf16),
            pltpu.SemaphoreType.DMA((2, 4)),
        ],
    )
    out = pl.pallas_call(
        middle_kernel,
        grid_spec=spec,
        out_shape=[
            jax.ShapeDtypeStruct((rows, D), bf16),
            jax.ShapeDtypeStruct((rows, FF), bf16),
            jax.ShapeDtypeStruct((rows, FF), bf16),
            jax.ShapeDtypeStruct((rows, D), bf16),
            jax.ShapeDtypeStruct((rows, D), bf16),
            jax.ShapeDtypeStruct((rows, D), bf16),
            jax.ShapeDtypeStruct((rows, D), f32),
        ]
        + [jax.ShapeDtypeStruct((256, width), bf16)] * 4
        + [jax.ShapeDtypeStruct((16, D), f32)],
        compiler_params=pltpu.CompilerParams(vmem_limit_bytes=50 * 1024 * 1024),
        name="middle",
        cost_estimate=QUICK,
    )(places, *att, hidden, cotangent, params, *weights)
    return out[:7], out[7:11], out[11]


def weight_grad_kernel(chunks, adds, place_ref, act_ref, pre_ref, low_ref, ffn_ref, branch_ref, *refs):
    att_refs, add_refs, out_ref = refs[:chunks], refs[chunks : chunks + adds], refs[-1]

    def put(at, part):
        for ref in add_refs:
            part = part + ref[:, at].astype(f32)
        out_ref[:, at] = part.astype(bf16)

    put(slice(0, D), tn(low_ref[...], pre_ref[...]))
    put(slice(D, 2 * D), tn(ffn_ref[...], act_ref[...]))
    for i in range(chunks):

        @pl.when(pl.program_id(0) == i)
        def _():
            att = att_refs[i][...]
            low = lane_iota(256, att.shape[1]) % LANES < HEAD_DIM
            zero = jnp.zeros_like(att)
            both = jnp.concatenate([jnp.where(low, att, zero), jnp.where(low, zero, att)], axis=0)
            put(slice(2 * D, 2 * D + att.shape[1]), tn(branch_ref[...], both))


def weight_grads(places, saved, att, first, chunks, adds):
    act, pre, low, ffn_grad, branch_grad = saved
    rows = act.shape[0]
    width = att[0].shape[1]
    total = 2 * D + width
    cut = D // 2

    def chunk(s, i, q):
        return (0, first - 2 * s)

    part = pl.BlockSpec((rows, cut), lambda s, i, q: (0, i))
    spec = pltpu.PrefetchScalarGridSpec(
        num_scalar_prefetch=1,
        grid=(chunks, 2),
        in_specs=[pl.BlockSpec((rows, D), chunk)] * 2
        + [part] * 3
        + [pl.BlockSpec((256, width), lambda s, i, q: (0, 0))] * chunks
        + [pl.BlockSpec((cut, total), lambda s, i, q, k=k: (2 * k + i, 0)) for _, k in adds],
        out_specs=pl.BlockSpec((cut, total), lambda s, i, q: (2 * s + i, 0)),
    )
    return pl.pallas_call(
        partial(weight_grad_kernel, chunks, len(adds)),
        grid_spec=spec,
        out_shape=jax.ShapeDtypeStruct((chunks * D, total), bf16),
        compiler_params=pltpu.CompilerParams(vmem_limit_bytes=VMEM),
        name="weight_grads",
        cost_estimate=QUICK,
    )(
        places, act, pre, low, ffn_grad, branch_grad,
        *[att[first - 2 * s] for s in range(chunks)], *[a for a, _ in adds],
    )


def collect_kernel(lay, place_ref, *refs):
    rows_refs = refs[: lay.arrays]
    code_ref, dense_ref = refs[lay.arrays :]
    me = place_ref[0]
    tokens = dense_ref.shape[0]
    low = lane_iota(tokens) < HEAD_DIM
    firsts, seconds = [], []
    for h in range(lay.heads):
        column = as_column(code_ref[h, 0:1, :])
        half = as_column(code_ref[h, 1:2, :])
        planes = [block_rows(lay, rows_refs, (h * 3 + x) * lay.half_rows) for x in range(3)]
        found = nn(gather_matrix(lay, me, column), jnp.concatenate(planes, axis=1))
        one, two = [], []
        for x in range(3):
            part = found[:, x * LANES : (x + 1) * LANES]
            turned = pltpu.roll(part, HEAD_DIM, 1)
            one.append(jnp.where(half == 0, part, turned))
            two.append(jnp.where(half == 1, part, turned))
        firsts.append(one)
        seconds.append(two)
    tiles = [jnp.where(low, firsts[h][0], seconds[h][1]) for h in range(lay.heads)]
    for h in range(0, lay.heads, 2):
        right = seconds[h + 1][2] if h + 1 < lay.heads else jnp.zeros((tokens, LANES), f32)
        tiles.append(jnp.where(low, firsts[h][2], right))
    dense_ref[...] = jnp.concatenate(tiles, axis=1).astype(bf16)


def collect(lay, places, returned, code, width):
    tokens = COLLECT_ROWS
    spec = pltpu.PrefetchScalarGridSpec(
        num_scalar_prefetch=1,
        grid=(lay.tokens // tokens,),
        in_specs=lay.specs(lay.data_rows, only(0))
        + [pl.BlockSpec((lay.heads, 8, tokens), lambda c, q: (0, 0, c))],
        out_specs=pl.BlockSpec((tokens, width), lambda c, q: (c, 0)),
    )
    return pl.pallas_call(
        partial(collect_kernel, lay),
        grid_spec=spec,
        out_shape=jax.ShapeDtypeStruct((lay.tokens, width), bf16),
        compiler_params=pltpu.CompilerParams(vmem_limit_bytes=VMEM),
        name="collect",
        cost_estimate=cost(COLLECT_US),
    )(places, *returned, code)


def half_rows_at(g, s, place):
    core = place % 2
    return jnp.where(s == 0, 1 - core, core) * 2 + g


def spread_kernel(g, place_ref, dense_ref, w_ref, h1_ref, other_ref, mine_ref):
    step, place = pl.program_id(0), place_ref[1]
    own = (half_rows_at(g, step, place) == place).astype(f32)
    part = nt(dense_ref[...], w_ref[...]) + own * h1_ref[...]

    @pl.when(step == 0)
    def _():
        other_ref[...] = part.astype(bf16)

    @pl.when(step == 1)
    def _():
        mine_ref[...] = part.astype(bf16)


def spread_grads(g, places, dense, weights, grad_h1):
    width = weights.shape[1]
    whole = lambda s, q: (0, 0)
    spec = pltpu.PrefetchScalarGridSpec(
        num_scalar_prefetch=1,
        grid=(2,),
        in_specs=[
            pl.BlockSpec((512, width), lambda s, q: (half_rows_at(g, s, q[1]), 0)),
            pl.BlockSpec((D, width), whole),
            pl.BlockSpec((512, D), whole),
        ],
        out_specs=[pl.BlockSpec((512, D), whole)] * 2,
    )
    return pl.pallas_call(
        partial(spread_kernel, g),
        grid_spec=spec,
        out_shape=[jax.ShapeDtypeStruct((512, D), bf16)] * 2,
        compiler_params=pltpu.CompilerParams(vmem_limit_bytes=VMEM),
        name="spread_grads",
        cost_estimate=cost(SPREAD_US),
    )(places, dense, weights, grad_h1)


def head_grad_kernel(lay, place_ref, x_ref, dense_ref, vec_ref, *refs):
    out_ref, total_ref = refs
    step = pl.program_id(0)

    @pl.when(step == 0)
    def _():
        total_ref[...] = tn(x_ref[...], dense_ref[...])

    @pl.when(step > 0)
    def _():
        total_ref[...] += tn(x_ref[...], dense_ref[...])

    @pl.when(step == 3)
    def _():
        depth = D // lay.peers
        if not lay.direct:
            out_ref[...] = total_ref[...].astype(bf16)
            return
        for d in range(lay.peers):
            out_ref[d, :depth, :] = total_ref[d * depth : (d + 1) * depth, :].astype(bf16)
            vector = vec_ref[d]
            high = vector.astype(bf16).astype(f32)
            width = total_ref.shape[1]
            out_ref[d, depth:, :] = jnp.concatenate(
                [high, vector - high, jnp.zeros((16, width - 2 * LANES), f32)], axis=1
            ).astype(bf16)


def head_grads(lay, places, x, dense, vec):
    width = dense.shape[1]
    depth = D // lay.peers
    shape = (lay.peers, depth + 16, width) if lay.direct else (D, width)
    spec = pltpu.PrefetchScalarGridSpec(
        num_scalar_prefetch=1,
        grid=(4,),
        in_specs=[
            pl.BlockSpec((512, D), lambda s, q: (s, 0)),
            pl.BlockSpec((512, width), lambda s, q: (s, 0)),
            pl.BlockSpec(vec.shape, lambda s, q: (0, 0, 0)),
        ],
        out_specs=pl.BlockSpec(shape, lambda s, q: (0,) * len(shape)),
        scratch_shapes=[pltpu.VMEM((D, width), f32)],
    )
    return pl.pallas_call(
        partial(head_grad_kernel, lay),
        grid_spec=spec,
        out_shape=jax.ShapeDtypeStruct(shape, bf16),
        compiler_params=pltpu.CompilerParams(vmem_limit_bytes=VMEM),
        name="head_grads",
        cost_estimate=cost(HEAD_GRADS_US),
    )(places, x, dense, vec)


def finish_heads_kernel(*refs):
    parts, outs = refs[0], refs[1:]
    depth, width = outs[0].shape
    heads = width // HEAD_DIM
    total = parts[0].astype(f32)
    for d in range(1, parts.shape[0]):
        total = total + parts[d].astype(f32)
    grads = total[:depth]
    cut = [slice(h * LANES, h * LANES + HEAD_DIM) for h in range(heads)]
    outs[0][...] = jnp.concatenate([grads[:, at] for at in cut], axis=1)
    cut = [slice(h * LANES + HEAD_DIM, (h + 1) * LANES) for h in range(heads)]
    outs[1][...] = jnp.concatenate([grads[:, at] for at in cut], axis=1)
    outs[2][...] = grads[:, 2 * width : 3 * width]
    outs[3][...] = total[depth:, :LANES] + total[depth:, LANES : 2 * LANES]


def finish_heads(parts, depth, width):
    shapes = [(depth, width)] * 3 + [(16, LANES)]
    return pl.pallas_call(
        finish_heads_kernel,
        out_shape=[jax.ShapeDtypeStruct(s, f32) for s in shapes],
        name="finish_heads",
        cost_estimate=QUICK,
    )(parts)


def finish_vectors_kernel(depth, own_ref, other_ref, bias_ref, gain_ref, shift_ref, inner_ref):
    total = (own_ref[...] + other_ref[...])[:, :depth]
    bias_ref[...] = total[:4]
    gain_ref[...] = total[4:6]
    shift_ref[...] = total[6:8]
    inner_ref[...] = total[8:12]


def finish_vectors(own, other, depth):
    return pl.pallas_call(
        partial(finish_vectors_kernel, depth),
        out_shape=[jax.ShapeDtypeStruct((n, depth), f32) for n in (4, 2, 2, 4)],
        name="finish_vectors",
        cost_estimate=QUICK,
    )(own, other)


def finish_middle_kernel(grad_ref, inner_ref, outer_ref, output_ref):
    inner_ref[...] = grad_ref[:, :D].astype(f32)
    outer_ref[...] = grad_ref[:, D : 2 * D].astype(f32)
    rest = grad_ref[:, 2 * D :].astype(f32)
    planes = [rest[:, i * LANES : (i + 1) * LANES] for i in range(rest.shape[1] // LANES)]
    folded = [p[:, :HEAD_DIM] + p[:, HEAD_DIM:] for p in planes]
    output_ref[...] = jnp.concatenate(folded, axis=1).T


def finish_middle(grads):
    depth, total = grads.shape
    return pl.pallas_call(
        finish_middle_kernel,
        out_shape=[
            jax.ShapeDtypeStruct((depth, D), f32),
            jax.ShapeDtypeStruct((depth, D), f32),
            jax.ShapeDtypeStruct(((total - 2 * D) // 2, depth), f32),
        ],
        name="finish_middle",
        cost_estimate=QUICK,
    )(grads)


def order_kernel(place_ref, *refs):
    parts, out_ref, rows_ref, sems = refs[:4], refs[4], refs[5], refs[6]
    rows = rows_ref.shape[1]

    def take(i):
        return pltpu.make_async_copy(parts[i], rows_ref.at[i], sems.at[0, i])

    def put(i):
        at = pl.ds(pl.multiple_of(place_ref[i] * rows, rows), rows)
        return pltpu.make_async_copy(rows_ref.at[i], out_ref.at[at, :], sems.at[1, i])

    for i in range(4):
        take(i).start()
    for i in range(4):
        take(i).wait()
        put(i).start()
    for i in range(4):
        put(i).wait()


def order_quarters(order, quarters):
    rows, width = quarters[0].shape
    dtype = quarters[0].dtype
    return pl.pallas_call(
        order_kernel,
        in_specs=[pl.BlockSpec(memory_space=pltpu.SMEM)]
        + [pl.BlockSpec(memory_space=pl.ANY)] * 4,
        out_specs=pl.BlockSpec(memory_space=pl.ANY),
        out_shape=jax.ShapeDtypeStruct((4 * rows, width), dtype),
        scratch_shapes=[pltpu.VMEM((4, rows, width), dtype), pltpu.SemaphoreType.DMA((2, 4))],
        name="order_quarters",
        cost_estimate=QUICK,
    )(order, *quarters)


def over_rows(lay, blocks, near_first=False):
    if not lay.direct:
        return [lax.all_to_all(blocks[0], "dp", split_axis=0, concat_axis=0, tiled=True)]
    out = [blocks[0]]
    for s in range(1, lay.peers):
        rows = blocks[s]
        if near_first and s >= lay.peers - 2:
            rows = after(rows, out[s - lay.peers + 3])
        out.append(lax.ppermute(rows, "dp", [(i, i ^ s) for i in range(lay.peers)]))
    return out


def in_hbm(rows):
    return pltpu.with_memory_space_constraint(rows, pltpu.HBM)


def share_pieces(lay, piece):
    def flip(rows, s):
        return lax.ppermute(rows, "dp", [(i, i ^ s) for i in range(lay.peers)])

    half = lay.peers // 2
    far = flip(piece, half)
    near = [piece] + [flip(piece, s) for s in range(1, half)]
    return near + [far] + [flip(far, s) for s in range(1, half)]


def after(value, *others):
    return lax.optimization_barrier((value, *others))[0]


def swap(rows, flip):
    return lax.ppermute(rows, "mp", [(i, i ^ flip) for i in range(4)])


def over_heads(blocks):
    return [blocks[0]] + [swap(blocks[t], t) for t in range(1, 4)]


def on_device(
    hidden_in,
    cotangent,
    w_query,
    w_key,
    w_value,
    w_output,
    w_inner,
    w_outer,
    biases,
    gains,
    shifts,
    inner_bias,
    lengths,
    padding,
    cluster_perm,
):
    peers = lax.axis_size("dp")
    tokens = hidden_in.shape[0]
    heads = cluster_perm.shape[0]
    lay = Layout(peers, tokens, heads)
    place = lax.axis_index("mp")
    me = lax.axis_index("dp")
    places = jnp.stack([me, place]).astype(i32)
    hidden_in = in_hbm(hidden_in)
    depth = w_query.shape[0]
    width = heads * HEAD_DIM

    piece, shard = pack_weights(
        w_query, w_key, w_value, w_output, w_inner, w_outer.T,
        biases, gains, shifts, inner_bias.reshape(1, -1),
    )
    own_w = lax.all_gather(shard, "dp", axis=0, tiled=True)
    far_w = swap(own_w, 2)
    if lay.direct:
        weights, bias, params = assemble_weights(lay, places, share_pieces(lay, piece))
    else:
        weights, bias, params = gather_weights(lay, place, piece)

    weights = in_hbm(weights)
    code = in_hbm(place_tokens(lay, cluster_perm))
    sent = project_rows(lay, places, hidden_in, weights, bias, code, padding.reshape(1, tokens))
    arrived = over_rows(lay, sent, near_first=True)
    mixed = over_rows(lay, attend(lay, arrived))
    found = unsort_rows(lay, places, mixed, code)
    att = over_heads(found)
    far_w = after(far_w, found[0])
    middle_w = [own_w, swap(own_w, 1), far_w, swap(far_w, 1)]
    saved, att_grad, vec = middle(places, att, hidden_in, cotangent, params, middle_w)
    out_quarter, act, pre_grad, first_low, ffn_grad, branch_grad, grad_h1 = saved
    saved = tuple(in_hbm(a) for a in (act, pre_grad, first_low, ffn_grad, branch_grad))
    att = [in_hbm(a) for a in att]

    got = over_heads(att_grad)
    from_core = swap(weight_grads(places, saved, att, 3, 2, []), 1)
    grads = sort_rows(lay, places, got, code)
    ready = (after(act, grads[0]),) + saved[1:]
    from_far = swap(weight_grads(places, ready, att, 2, 1, [(from_core, 0)]), 2)
    grads = over_rows(lay, grads)
    slot_grads, bias_sums = attend_back(lay, arrived, grads)

    summed = weight_grads(places, saved, att, 0, 1, [(from_core, 1), (from_far, 0)])
    returned = over_rows(lay, slot_grads)
    head_sums = bias_sums[:, :2].reshape(heads, 2, 2, HEAD_DIM).sum(axis=2)
    head_sums = head_sums.transpose(1, 0, 2).reshape(2, width)
    vec = lax.dynamic_update_slice(vec[:12], head_sums, (0, place * width))
    vec = jnp.concatenate(
        [vec[:8].reshape(8, peers, depth).transpose(1, 0, 2), vec[8:].reshape(peers, 4, depth)],
        axis=1,
    )
    spread = jnp.pad(vec, ((0, 0), (0, 4), (0, (-depth) % LANES)))
    reduced = lax.psum_scatter(after(summed, *returned), "dp", scatter_dimension=0, tiled=True)
    far = swap(after(out_quarter, summed), 2)
    dense = collect(lay, places, returned, code, weights.shape[1])
    terms = head_grads(lay, places, hidden_in, dense, spread)
    dense = after(dense, terms, far)
    groups = [spread_grads(g, places, dense, weights, grad_h1) for g in range(2)]
    chips = [
        (mine.astype(f32) + swap(other, 1).astype(f32)).astype(bf16) for other, mine in groups
    ]
    hidden_out = order_quarters(
        jnp.stack([place, place ^ 2, place ^ 1, place ^ 3]).astype(i32),
        [out_quarter, far, swap(out_quarter, 1), swap(far, 1)],
    )
    if lay.direct:
        terms = lax.all_to_all(terms, "dp", split_axis=0, concat_axis=0, tiled=True)
        ends = finish_heads(terms, depth, width)
    else:
        ends = reduce_heads(terms, vec, depth, width)
    ready = [
        (after(chip, ends[0]).astype(f32) + swap(chip, 2).astype(f32)).astype(bf16)
        for chip in chips
    ]
    core = place % 2
    grad_hidden = order_quarters(
        jnp.stack([2 * core, 2 * core + 1, 2 - 2 * core, 3 - 2 * core]).astype(i32),
        ready + [swap(part, 1) for part in ready],
    )

    small = ends[3] + swap(ends[3], 1)
    small = finish_vectors(small, swap(small, 2), depth)
    grad_inner, grad_outer, grad_output = finish_middle(reduced)
    return (
        hidden_out,
        grad_hidden,
        ends[0],
        ends[1],
        ends[2],
        grad_output,
        grad_inner,
        grad_outer.T,
        small[0],
        small[1],
        small[2],
        small[3].reshape(-1),
    )


def gather_weights(lay, place, piece):
    depth = D // lay.peers
    width = lay.heads * HEAD_DIM
    got = lax.all_gather(piece, "dp", axis=0, tiled=False)
    columns = piece.shape[1] - LANES
    weights = got[:, :depth, :columns].reshape(D, columns)
    vectors = got[:, :12, columns : columns + depth].astype(f32)
    params = vectors[:, :8].transpose(1, 0, 2).reshape(8, D)
    params = jnp.concatenate([params, vectors[:, 8:].reshape(4, D), jnp.zeros((4, D), f32)], axis=0)
    own = lax.dynamic_slice_in_dim(params[:2], place * width, width, 1)
    query = own[0].reshape(lay.heads, HEAD_DIM)
    query = jnp.concatenate([query, jnp.zeros_like(query)], axis=1).reshape(-1)
    row = jnp.concatenate([query, own[1], jnp.zeros(weights.shape[1] - 3 * width, f32)])
    return weights, jnp.broadcast_to(row[None], (8, row.shape[0])), params


def reduce_heads(grads, vec, depth, width):
    total = lax.psum_scatter(grads, "dp", scatter_dimension=0, tiled=True).astype(f32)
    pairs = total[:, : 2 * width].reshape(depth, -1, 2, HEAD_DIM)
    small = lax.psum_scatter(vec, "dp", scatter_dimension=0, tiled=False)
    small = jnp.pad(small, ((0, 4), (0, LANES - depth)))
    return (
        pairs[:, :, 0].reshape(depth, width),
        pairs[:, :, 1].reshape(depth, width),
        total[:, 2 * width : 3 * width],
        small,
    )


def solution(mesh):
    placed = (
        P("dp", None),
        P("dp", None),
        P("dp", "mp"),
        P("dp", "mp"),
        P("dp", "mp"),
        P("mp", "dp"),
        P("dp", "mp"),
        P("mp", "dp"),
        P(None, "dp"),
        P(None, "dp"),
        P(None, "dp"),
        P("dp"),
        P(),
        P("dp"),
        P("mp", "dp"),
    )
    return jax.shard_map(
        on_device,
        mesh=mesh,
        in_specs=placed,
        out_specs=(
            P("dp", None),
            P("dp", None),
            P("dp", "mp"),
            P("dp", "mp"),
            P("dp", "mp"),
            P("mp", "dp"),
            P("dp", "mp"),
            P("mp", "dp"),
            P(None, "dp"),
            P(None, "dp"),
            P(None, "dp"),
            P("dp"),
        ),
        check_vma=False,
    )
```

profile of v0, /device:TPU:0, one launch (start us, length us, event | category | flops | bytes accessed | tf_op | source)
XLA Modules:
  0.0 429.0 jit_solution(13880999450925204162)
XLA Ops:
  10.6 4.1 collective-permute-start.3
  18.2 3.8 collective-permute-done.3.refs_4_
  28.7 4.5 %collective-permute-done.2.refs_3_ = bf16[96,768]{1,0:T(8,128)(2,1)S(1)} collective-permute-done((bf16[96,768]{1,0:T(8,128)(2,1)}, bf16[96,768]{1,0:T(8,128)(2,1)S(1)}, u32[]{:S(2)}, u32[]{:S(2)}) %collective-permute-start.2) | collective-permute-done | bytes 147488 | tf_op jit(solution)/shard_map/ppermute | solution.py:1147
  33.2 8.3 %collective-permute-done.5.refs_6_ = bf16[96,768]{1,0:T(8,128)(2,1)S(1)} collective-permute-done((bf16[96,768]{1,0:T(8,128)(2,1)S(1)}, bf16[96,768]{1,0:T(8,128)(2,1)S(1)}, u32[]{:S(2)}, u32[]{:S(2)}) %collective-permute-start.5) | collective-permute-done | bytes 147488 | tf_op jit(solution)/shard_map/ppermute | solution.py:1147
  48.2 15.1 %project_rows.1 = (bf16[1168,128]{1,0:T(8,128)(2,1)}, bf16[1168,128]{1,0:T(8,128)(2,1)}, bf16[1168,128]{1,0:T(8,128)(2,1)}, bf16[1168,128]{1,0:T(8,128)(2,1)}, b...) custom-call(s32[2]{0:T(128)} %pad_add_fusion.1.place_ref, ...), custom_call_target="tpu_custom_call" | custom-call | flops 1000000 | bytes 3000 | tf_op jit(solution)/shard_map/project_rows/pallas_call | solution.py:287
  76.6 17.9 %collective-permute-done.8.refs_2_.refs_10_ = bf16[1168,128]{1,0:T(8,128)(2,1)S(1)} collective-permute-done((bf16[1168,128]{1,0:T(8,128)(2,1)}, bf16[1168,128]{1,0:T(8,128)(2,1)S(1)}, u32[]{:S(2)}, u32[]{:S(2)}) %collective-permute-start.8) | collective-permute-done | bytes 299040 | tf_op jit(solution)/shard_map/ppermute | solution.py:1137
  96.2 3.7 collective-permute-done.9.refs_3_.refs_11_
  101.3 17.6 %collective-permute-done.11.refs_5_.refs_13_ = bf16[1168,128]{1,0:T(8,128)(2,1)S(1)} collective-permute-done((bf16[1168,128]{1,0:T(8,128)(2,1)}, bf16[1168,128]{1,0:T(8,128)(2,1)S(1)}, u32[]{:S(2)}, u32[]{:S(2)}) %collective-permute-start.11) | collective-permute-done | bytes 299040 | tf_op jit(solution)/shard_map/ppermute | solution.py:1137
  119.8 5.1 %attend.1 = (bf16[384,128]{1,0:T(8,128)(2,1)}, bf16[384,128]{1,0:T(8,128)(2,1)}, bf16[384,128]{1,0:T(8,128)(2,1)}, bf16[384,128]{1,0:T(8,128)(2,1)}, bf16[384,12...) custom-call(bf16[1168,128]{1,0:T(8,128)(2,1)} %get-tuple-element.93.refs_0_.refs_, ...), custom_call_target="tpu_custom_call" | custom-call | flops 46000001024 | bytes 138000000 | tf_op jit(solution)/shard_map/attend/pallas_call | solution.py:362
  125.4 10.6 %collective-permute-start.15 = (bf16[384,128]{1,0:T(8,128)(2,1)}, bf16[384,128]{1,0:T(8,128)(2,1)S(1)}, u32[]{:S(2)}, u32[]{:S(2)}) collective-permute-start(bf16[384,128]{1,0:T(8,128)(2,1)} %get-tuple-element.105), channel_id=1, source_target_pairs={{0,8},{4,12},{8,0},{12,4},{16,24},{20,28},{24,16},{28,20},{1,9},{5... | collective-permute-start | bytes 294920 | tf_op jit(solution)/shard_map/ppermute | solution.py:1137
  145.5 4.8 %collective-permute-done.17.refs_4_ = bf16[384,128]{1,0:T(8,128)(2,1)S(1)} collective-permute-done((bf16[384,128]{1,0:T(8,128)(2,1)}, bf16[384,128]{1,0:T(8,128)(2,1)S(1)}, u32[]{:S(2)}, u32[]{:S(2)}) %collective-permute-start.17) | collective-permute-done | bytes 98336 | tf_op jit(solution)/shard_map/ppermute | solution.py:1137
  153.4 6.6 %unsort_rows.1 = (bf16[256,384]{1,0:T(8,128)(2,1)}, bf16[256,384]{1,0:T(8,128)(2,1)}, bf16[256,384]{1,0:T(8,128)(2,1)}, bf16[256,384]{1,0:T(8,128)(2,1)}) custom-call(s32[2]{0:T(128)} %pad_add_fusion.1.place_ref, bf16[384,128]{1,0:T(8,128)(2,1)} %get-tuple-element.103.refs_0_, bf16[384,128]{1,0:T(8,128)(2,1)} %copy-done.34, bf16[384,128]{1,0:T(8,128)(2,1)} %copy-done.35, ...), custom_call_target="tpu_custom_call" | custom-call | flops 1000000 | bytes 3000 | tf_op jit(solution)/shard_map/unsort_rows/pallas_call | solution.py:447
  160.1 5.3 %collective-permute-done.25.w2 = bf16[768,1920]{1,0:T(8,128)(2,1)} collective-permute-done((bf16[768,1920]{1,0:T(8,128)(2,1)}, bf16[768,1920]{1,0:T(8,128)(2,1)}, u32[]{:S(2)}, u32[]{:S(2)}) %collective-permute-start.25) | collective-permute-done | bytes 2949152 | tf_op jit(solution)/shard_map/ppermute | solution.py:1160
  167.3 4.0 collective-permute-done.21.att1.refs_1_
  179.8 27.1 %middle.1 = (bf16[512,768]{1,0:T(8,128)(2,1)S(1)}, bf16[512,3072]{1,0:T(8,128)(2,1)}, bf16[512,3072]{1,0:T(8,128)(2,1)}, bf16[512,768]{1,0:T(8,128)(2,1)S(1)}, b...) custom-call(s32[2]{0:T(128)S(1)} %copy-done.8, ...), custom_call_target="tpu_custom_call" | custom-call | flops 1000000 | bytes 3000 | tf_op jit(solution)/shard_map/middle/pallas_call | solution.py:812
  211.5 10.0 %weight_grads.3 = bf16[1536,1920]{1,0:T(8,128)(2,1)} custom-call(s32[2]{0:T(128)} %pad_add_fusion.1.place_ref, bf16[512,3072]{1,0:T(8,128)(2,1)} %get-tuple-element.129.act_ref, bf16[512,3072]{1,0:T(8,128)(2,1)} %get-tuple-element.120.pre_ref, bf16[512,768]{1,0:T(8,128)(2,1)} %copy-done, bf16[512,768]{1,0:T(8,128)(2,1)} %copy-done.1, ...), custom_call_target="tpu_custom_call" | custom-call | flops 1000000 | bytes 3000 | tf_op jit(solution)/shard_map/weight_grads/pallas_call | solution.py:874
  223.1 7.4 %sort_rows.1 = (bf16[384,128]{1,0:T(8,128)(2,1)}, bf16[384,128]{1,0:T(8,128)(2,1)}, bf16[384,128]{1,0:T(8,128)(2,1)}, bf16[384,128]{1,0:T(8,128)(2,1)}, bf16[384...) custom-call(s32[2]{0:T(128)} %pad_add_fusion.1.place_ref, ...), custom_call_target="tpu_custom_call" | custom-call | flops 80000000000 | bytes 240000000 | tf_op jit(solution)/shard_map/sort_rows/pallas_call | solution.py:486
  231.9 6.2 %weight_grads.4 = bf16[768,1920]{1,0:T(8,128)(2,1)} custom-call(s32[2]{0:T(128)} %pad_add_fusion.1.place_ref, bf16[512,3072]{1,0:T(8,128)(2,1)} %get-tuple-element.129.act_ref, bf16[512,3072]{1,0:T(8,128)(2,1)} %get-tuple-element.120.pre_ref, bf16[512,768]{1,0:T(8,128)(2,1)} %copy-done, bf16[512,768]{1,0:T(8,128)(2,1)} %copy-done.1, ...), custom_call_target="tpu_custom_call" | custom-call | flops 1000000 | bytes 3000 | tf_op jit(solution)/shard_map/weight_grads/pallas_call | solution.py:874
  251.6 5.5 %collective-permute-done.38.refs_20_ = bf16[384,128]{1,0:T(8,128)(2,1)S(1)} collective-permute-done((bf16[384,128]{1,0:T(8,128)(2,1)S(1)}, bf16[384,128]{1,0:T(8,128)(2,1)S(1)}, u32[]{:S(2)}, u32[]{:S(2)}) %collective-permute-start.38) | collective-permute-done | bytes 98336 | tf_op jit(solution)/shard_map/ppermute | solution.py:1137
  261.3 10.6 %attend_back.1 = (bf16[1152,128]{1,0:T(8,128)(2,1)}, bf16[1152,128]{1,0:T(8,128)(2,1)}, bf16[1152,128]{1,0:T(8,128)(2,1)}, bf16[1152,128]{1,0:T(8,128)(2,1)}, bf...) custom-call(bf16[1168,128]{1,0:T(8,128)(2,1)} %get-tuple-element.93., ...), custom_call_target="tpu_custom_call" | custom-call | flops 1000000 | bytes 3000 | tf_op jit(solution)/shard_map/attend_back/pallas_call | solution.py:403
  279.1 6.2 %collective-permute-start.46 = (bf16[1152,128]{1,0:T(8,128)(2,1)}, bf16[1152,128]{1,0:T(8,128)(2,1)S(1)}, u32[]{:S(2)}, u32[]{:S(2)}) collective-permute-start(bf16[1152,128]{1,0:T(8,128)(2,1)} %get-tuple-element.143), channel_id=1, source_target_pairs={{0,20},{4,16},{8,28},{12,24},{16,4},{20,0},{24,12},{28,8},{1,21},{... | collective-permute-start | bytes 884744 | tf_op jit(solution)/shard_map/ppermute | solution.py:1137
  285.3 10.5 %collective-permute-done.43.refs_2_ = bf16[1152,128]{1,0:T(8,128)(2,1)S(1)} collective-permute-done((bf16[1152,128]{1,0:T(8,128)(2,1)}, bf16[1152,128]{1,0:T(8,128)(2,1)S(1)}, u32[]{:S(2)}, u32[]{:S(2)}) %collective-permute-start.43) | collective-permute-done | bytes 294944 | tf_op jit(solution)/shard_map/ppermute | solution.py:1137
  297.4 7.2 %collective-permute-done.31.refs_2_ = bf16[768,1920]{1,0:T(8,128)(2,1)} collective-permute-done((bf16[768,1920]{1,0:T(8,128)(2,1)}, bf16[768,1920]{1,0:T(8,128)(2,1)}, u32[]{:S(2)}, u32[]{:S(2)}) %collective-permute-start.31) | collective-permute-done | bytes 2949152 | tf_op jit(solution)/shard_map/ppermute | solution.py:1160
  309.2 7.3 %weight_grads.5 = bf16[768,1920]{1,0:T(8,128)(2,1)} custom-call(s32[2]{0:T(128)} %pad_add_fusion.1.place_ref, bf16[512,3072]{1,0:T(8,128)(2,1)} %get-tuple-element.129.act_ref, bf16[512,3072]{1,0:T(8,128)(2,1)} %get-tuple-element.120.pre_ref, bf16[512,768]{1,0:T(8,128)(2,1)} %copy-done, bf16[512,768]{1,0:T(8,128)(2,1)} %copy-done.1, ...), custom_call_target="tpu_custom_call" | custom-call | flops 1000000 | bytes 3000 | tf_op jit(solution)/shard_map/weight_grads/pallas_call | solution.py:874
  319.0 10.9 %collect.1.dense_ref = bf16[2048,640]{1,0:T(8,128)(2,1)} custom-call(s32[2]{0:T(128)} %pad_add_fusion.1.place_ref, bf16[1152,128]{1,0:T(8,128)(2,1)} %get-tuple-element.138.refs_0_, bf16[1152,128]{1,0:T(8,128)(2,1)} %copy-done.51, bf16[1152,128]{1,0:T(8,128)(2,1)} %copy-done.52, bf16[1152,128]{1,0:T(8,128)(2,1)} %copy-done.53, bf16[1152,128]{1,0:T(8,128)(2,1)} %copy-done.54, ...), custom_call_target="tpu_custom_call" | custom-call | flops 30000001024 | bytes 90000000 | tf_op jit(solution)/shard_map/collect/pallas_call | solution.py:923
  329.9 7.1 %head_grads.1 = bf16[8,112,640]{2,1,0:T(8,128)(2,1)} custom-call(s32[2]{0:T(128)} %pad_add_fusion.1.place_ref, bf16[2048,768]{1,0:T(8,128)(2,1)} %x_ref.3, bf16[2048,640]{1,0:T(8,128)(2,1)} %collect.1.dense_ref, f32[8,16,128]{2,1,0:T(8,128)} %select_maximum_fusion.vec_ref), custom_call_target="tpu_custom_call" | custom-call | flops 4000000000 | bytes 12000000 | tf_op jit(solution)/shard_map/head_grads/pallas_call | solution.py:1018
  337.0 14.0 %all-to-all-start = ((bf16[8,112,640]{2,1,0:T(8,128)(2,1)}), bf16[8,112,640]{2,1,0:T(8,128)(2,1)S(1)}, u32[]{:S(2)}, u32[]{:S(2)}) async-start(bf16[8,112,640]{2,1,0:T(8,128)(2,1)} %head_grads.1), calls=%async_computation | async-start | bytes 2293760 | tf_op jit(solution)/shard_map/all_to_all | solution.py:1252
  351.0 5.6 %spread_grads.2 = (bf16[512,768]{1,0:T(8,128)(2,1)}, bf16[512,768]{1,0:T(8,128)(2,1)}) custom-call(s32[2]{0:T(128)} %pad_add_fusion.1.place_ref, bf16[2048,640]{1,0:T(8,128)(2,1)} %collect.1.dense_ref, bf16[768,640]{1,0:T(8,128)(2,1)} %get-tuple-element.91.w_ref, f32[512,768]{1,0:T(8,128)} %get-tuple-element.149.h1_ref), custom_call_target="tpu_custom_call" | custom-call | flops 3000000000 | bytes 9000000 | tf_op jit(solution)/shard_map/spread_grads/pallas_call | solution.py:965
  356.6 5.8 %spread_grads.3 = (bf16[512,768]{1,0:T(8,128)(2,1)}, bf16[512,768]{1,0:T(8,128)(2,1)}) custom-call(s32[2]{0:T(128)} %pad_add_fusion.1.place_ref, bf16[2048,640]{1,0:T(8,128)(2,1)} %collect.1.dense_ref, bf16[768,640]{1,0:T(8,128)(2,1)} %get-tuple-element.91.w_ref, f32[512,768]{1,0:T(8,128)} %get-tuple-element.149.h1_ref), custom_call_target="tpu_custom_call" | custom-call | flops 3000000000 | bytes 9000000 | tf_op jit(solution)/shard_map/spread_grads/pallas_call | solution.py:965
  367.3 19.7 %all-to-all-done.refs_0_ = bf16[8,112,640]{2,1,0:T(8,128)(2,1)S(1)} async-done(((bf16[8,112,640]{2,1,0:T(8,128)(2,1)}), bf16[8,112,640]{2,1,0:T(8,128)(2,1)S(1)}, u32[]{:S(2)}, u32[]{:S(2)}) %all-to-all-start) | async-done | bytes 1146912 | tf_op jit(solution)/shard_map/all_to_all | solution.py:1252
  392.0 9.6 %collective-permute-done.52 = bf16[512,768]{1,0:T(8,128)(2,1)} collective-permute-done((bf16[512,768]{1,0:T(8,128)(2,1)S(1)}, bf16[512,768]{1,0:T(8,128)(2,1)}, u32[]{:S(2)}, u32[]{:S(2)}) %collective-permute-start.52) | collective-permute-done | bytes 786464 | tf_op jit(solution)/shard_map/ppermute | solution.py:1160
  412.2 3.5 order_quarters.2
  (265 shorter events, 128.7 us)
Async XLA Ops:
  7.2 92.8 %all-gather.2.cloned.1.call-start = ((), (), s32[]{:S(2)}) async-start(), calls=%async_computation.2 | async-start | bytes 3317760 | tf_op jit(solution)/shard_map/all_gather | solution.py:1199
  10.5 409.7 %reduce-scatter.2.cloned.1.call-start = ((), (), s32[]{:S(2)}) async-start(), calls=%async_computation.3 | async-start | bytes 3317760 | tf_op jit(solution)/shard_map/reduce_scatter | solution.py:1238
  17.8 15.4 %collective-permute-start.2 = (bf16[96,768]{1,0:T(8,128)(2,1)}, bf16[96,768]{1,0:T(8,128)(2,1)S(1)}, u32[]{:S(2)}, u32[]{:S(2)}) collective-permute-start(bf16[96,768]{1,0:T(8,128)(2,1)} %get-tuple-element.90.refs_0_), channel_id=1, source_target_pairs={{0,12},{4,8},{8,4},{12,0},{16,28},{20,24},{24,20},{28,16},{1,13},{... | collective-permute-start | bytes 442376 | tf_op jit(solution)/shard_map/ppermute | solution.py:1147
  23.6 17.9 %collective-permute-start.5 = (bf16[96,768]{1,0:T(8,128)(2,1)S(1)}, bf16[96,768]{1,0:T(8,128)(2,1)S(1)}, u32[]{:S(2)}, u32[]{:S(2)}) collective-permute-start(bf16[96,768]{1,0:T(8,128)(2,1)S(1)} %collective-permute-done.3.refs_4_), channel_id=1, source_target_pairs={{0,8},{4,12},{8,0},{12,4},{16,24},{20,28},{24,16},{28,20},{1,9},{5... | collective-permute-start | bytes 442376 | tf_op jit(solution)/shard_map/ppermute | solution.py:1147
  24.3 20.5 %collective-permute-start.6 = (bf16[96,768]{1,0:T(8,128)(2,1)S(1)}, bf16[96,768]{1,0:T(8,128)(2,1)S(1)}, u32[]{:S(2)}, u32[]{:S(2)}) collective-permute-start(bf16[96,768]{1,0:T(8,128)(2,1)S(1)} %collective-permute-done.3.refs_4_), channel_id=1, source_target_pairs={{0,12},{4,8},{8,4},{12,0},{16,28},{20,24},{24,20},{28,16},{1,13},{... | collective-permute-start | bytes 442376 | tf_op jit(solution)/shard_map/ppermute | solution.py:1147
  64.9 29.5 %collective-permute-start.8 = (bf16[1168,128]{1,0:T(8,128)(2,1)}, bf16[1168,128]{1,0:T(8,128)(2,1)S(1)}, u32[]{:S(2)}, u32[]{:S(2)}) collective-permute-start(bf16[1168,128]{1,0:T(8,128)(2,1)} %get-tuple-element.95), channel_id=1, source_target_pairs={{0,8},{4,12},{8,0},{12,4},{16,24},{20,28},{24,16},{28,20},{1,9},{5... | collective-permute-start | bytes 897032 | tf_op jit(solution)/shard_map/ppermute | solution.py:1137
  64.9 35.0 %collective-permute-start.9 = (bf16[1168,128]{1,0:T(8,128)(2,1)}, bf16[1168,128]{1,0:T(8,128)(2,1)S(1)}, u32[]{:S(2)}, u32[]{:S(2)}) collective-permute-start(bf16[1168,128]{1,0:T(8,128)(2,1)} %get-tuple-element.96), channel_id=1, source_target_pairs={{0,12},{4,8},{8,4},{12,0},{16,28},{20,24},{24,20},{28,16},{1,13},{... | collective-permute-start | bytes 897032 | tf_op jit(solution)/shard_map/ppermute | solution.py:1137
  66.8 34.5 %collective-permute-start.10 = (bf16[1168,128]{1,0:T(8,128)(2,1)}, bf16[1168,128]{1,0:T(8,128)(2,1)S(1)}, u32[]{:S(2)}, u32[]{:S(2)}) collective-permute-start(bf16[1168,128]{1,0:T(8,128)(2,1)} %get-tuple-element.97), channel_id=1, source_target_pairs={{0,16},{4,20},{8,24},{12,28},{16,0},{20,4},{24,8},{28,12},{1,17},{... | collective-permute-start | bytes 897032 | tf_op jit(solution)/shard_map/ppermute | solution.py:1137
  67.7 51.2 %collective-permute-start.11 = (bf16[1168,128]{1,0:T(8,128)(2,1)}, bf16[1168,128]{1,0:T(8,128)(2,1)S(1)}, u32[]{:S(2)}, u32[]{:S(2)}) collective-permute-start(bf16[1168,128]{1,0:T(8,128)(2,1)} %get-tuple-element.98), channel_id=1, source_target_pairs={{0,20},{4,16},{8,28},{12,24},{16,4},{20,0},{24,12},{28,8},{1,21},{... | collective-permute-start | bytes 897032 | tf_op jit(solution)/shard_map/ppermute | solution.py:1137
  73.3 45.6 %collective-permute-start.12 = (bf16[1168,128]{1,0:T(8,128)(2,1)}, bf16[1168,128]{1,0:T(8,128)(2,1)S(1)}, u32[]{:S(2)}, u32[]{:S(2)}) collective-permute-start(bf16[1168,128]{1,0:T(8,128)(2,1)} %get-tuple-element.100), channel_id=1, source_target_pairs={{0,24},{4,28},{8,16},{12,20},{16,8},{20,12},{24,0},{28,4},{1,25},{... | collective-permute-start | bytes 897032 | tf_op jit(solution)/shard_map/ppermute | solution.py:1137
  94.4 24.5 %collective-permute-start.13 = (bf16[1168,128]{1,0:T(8,128)(2,1)}, bf16[1168,128]{1,0:T(8,128)(2,1)S(1)}, u32[]{:S(2)}, u32[]{:S(2)}) collective-permute-start(bf16[1168,128]{1,0:T(8,128)(2,1)} %get-tuple-element.102), channel_id=1, source_target_pairs={{0,28},{4,24},{8,20},{12,16},{16,12},{20,8},{24,4},{28,0},{1,29},{... | collective-permute-start | bytes 897032 | tf_op jit(solution)/shard_map/ppermute | solution.py:1137
  99.9 65.4 %collective-permute-start.25 = (bf16[768,1920]{1,0:T(8,128)(2,1)}, bf16[768,1920]{1,0:T(8,128)(2,1)}, u32[]{:S(2)}, u32[]{:S(2)}) collective-permute-start(bf16[768,1920]{1,0:T(8,128)(2,1)} %all-gather.2.cloned.1.call-done.w0), channel_id=1, source_target_pairs={{0,2},{1,3},{2,0},{3,1},{4,6},{5,7},{6,4},{7,5},{8,10},{9,11},{10,... | collective-permute-start | bytes 8847368 | tf_op jit(solution)/shard_map/ppermute | solution.py:1160
  124.9 14.3 %collective-permute-start.14 = (bf16[384,128]{1,0:T(8,128)(2,1)}, bf16[384,128]{1,0:T(8,128)(2,1)S(1)}, u32[]{:S(2)}, u32[]{:S(2)}) collective-permute-start(bf16[384,128]{1,0:T(8,128)(2,1)} %get-tuple-element.104), channel_id=1, source_target_pairs={{0,4},{4,0},{8,12},{12,8},{16,20},{20,16},{24,28},{28,24},{1,5},{5... | collective-permute-start | bytes 294920 | tf_op jit(solution)/shard_map/ppermute | solution.py:1137
  125.4 15.2 %collective-permute-start.15 = (bf16[384,128]{1,0:T(8,128)(2,1)}, bf16[384,128]{1,0:T(8,128)(2,1)S(1)}, u32[]{:S(2)}, u32[]{:S(2)}) collective-permute-start(bf16[384,128]{1,0:T(8,128)(2,1)} %get-tuple-element.105), channel_id=1, source_target_pairs={{0,8},{4,12},{8,0},{12,4},{16,24},{20,28},{24,16},{28,20},{1,9},{5... | collective-permute-start | bytes 294920 | tf_op jit(solution)/shard_map/ppermute | solution.py:1137
  136.7 13.6 %collective-permute-start.17 = (bf16[384,128]{1,0:T(8,128)(2,1)}, bf16[384,128]{1,0:T(8,128)(2,1)S(1)}, u32[]{:S(2)}, u32[]{:S(2)}) collective-permute-start(bf16[384,128]{1,0:T(8,128)(2,1)} %get-tuple-element.107), channel_id=1, source_target_pairs={{0,16},{4,20},{8,24},{12,28},{16,0},{20,4},{24,8},{28,12},{1,17},{... | collective-permute-start | bytes 294920 | tf_op jit(solution)/shard_map/ppermute | solution.py:1137
  160.0 16.2 %collective-permute-start.24 = (bf16[768,1920]{1,0:T(8,128)(2,1)}, bf16[768,1920]{1,0:T(8,128)(2,1)S(1)}, u32[]{:S(2)}, u32[]{:S(2)}) collective-permute-start(bf16[768,1920]{1,0:T(8,128)(2,1)} %all-gather.2.cloned.1.call-done.w0), channel_id=1, source_target_pairs={{0,1},{1,0},{2,3},{3,2},{4,5},{5,4},{6,7},{7,6},{8,9},{9,8},{10,11... | collective-permute-start | bytes 8847368 | tf_op jit(solution)/shard_map/ppermute | solution.py:1160
  238.1 66.5 %collective-permute-start.31 = (bf16[768,1920]{1,0:T(8,128)(2,1)}, bf16[768,1920]{1,0:T(8,128)(2,1)}, u32[]{:S(2)}, u32[]{:S(2)}) collective-permute-start(bf16[768,1920]{1,0:T(8,128)(2,1)} %weight_grads.4), channel_id=1, source_target_pairs={{0,2},{1,3},{2,0},{3,1},{4,6},{5,7},{6,4},{7,5},{8,10},{9,11},{10,... | collective-permute-start | bytes 8847368 | tf_op jit(solution)/shard_map/ppermute | solution.py:1160
  242.9 14.3 %collective-permute-start.38 = (bf16[384,128]{1,0:T(8,128)(2,1)S(1)}, bf16[384,128]{1,0:T(8,128)(2,1)S(1)}, u32[]{:S(2)}, u32[]{:S(2)}) collective-permute-start(bf16[384,128]{1,0:T(8,128)(2,1)S(1)} %copy-done.62), channel_id=1, source_target_pairs={{0,16},{4,20},{8,24},{12,28},{16,0},{20,4},{24,8},{28,12},{1,17},{... | collective-permute-start | bytes 294920 | tf_op jit(solution)/shard_map/ppermute | solution.py:1137
  244.1 15.8 %collective-permute-start.39 = (bf16[384,128]{1,0:T(8,128)(2,1)S(1)}, bf16[384,128]{1,0:T(8,128)(2,1)S(1)}, u32[]{:S(2)}, u32[]{:S(2)}) collective-permute-start(bf16[384,128]{1,0:T(8,128)(2,1)S(1)} %copy-done.61), channel_id=1, source_target_pairs={{0,20},{4,16},{8,28},{12,24},{16,4},{20,0},{24,12},{28,8},{1,21},{... | collective-permute-start | bytes 294920 | tf_op jit(solution)/shard_map/ppermute | solution.py:1137
  272.7 23.1 %collective-permute-start.43 = (bf16[1152,128]{1,0:T(8,128)(2,1)}, bf16[1152,128]{1,0:T(8,128)(2,1)S(1)}, u32[]{:S(2)}, u32[]{:S(2)}) collective-permute-start(bf16[1152,128]{1,0:T(8,128)(2,1)} %get-tuple-element.140), channel_id=1, source_target_pairs={{0,8},{4,12},{8,0},{12,4},{16,24},{20,28},{24,16},{28,20},{1,9},{5... | collective-permute-start | bytes 884744 | tf_op jit(solution)/shard_map/ppermute | solution.py:1137
  276.0 40.5 %collective-permute-start.44 = (bf16[1152,128]{1,0:T(8,128)(2,1)}, bf16[1152,128]{1,0:T(8,128)(2,1)S(1)}, u32[]{:S(2)}, u32[]{:S(2)}) collective-permute-start(bf16[1152,128]{1,0:T(8,128)(2,1)} %get-tuple-element.141), channel_id=1, source_target_pairs={{0,12},{4,8},{8,4},{12,0},{16,28},{20,24},{24,20},{28,16},{1,13},{... | collective-permute-start | bytes 884744 | tf_op jit(solution)/shard_map/ppermute | solution.py:1137
  276.5 41.6 %collective-permute-start.45 = (bf16[1152,128]{1,0:T(8,128)(2,1)}, bf16[1152,128]{1,0:T(8,128)(2,1)S(1)}, u32[]{:S(2)}, u32[]{:S(2)}) collective-permute-start(bf16[1152,128]{1,0:T(8,128)(2,1)} %get-tuple-element.142), channel_id=1, source_target_pairs={{0,16},{4,20},{8,24},{12,28},{16,0},{20,4},{24,8},{28,12},{1,17},{... | collective-permute-start | bytes 884744 | tf_op jit(solution)/shard_map/ppermute | solution.py:1137
  279.1 39.2 %collective-permute-start.46 = (bf16[1152,128]{1,0:T(8,128)(2,1)}, bf16[1152,128]{1,0:T(8,128)(2,1)S(1)}, u32[]{:S(2)}, u32[]{:S(2)}) collective-permute-start(bf16[1152,128]{1,0:T(8,128)(2,1)} %get-tuple-element.143), channel_id=1, source_target_pairs={{0,20},{4,16},{8,28},{12,24},{16,4},{20,0},{24,12},{28,8},{1,21},{... | collective-permute-start | bytes 884744 | tf_op jit(solution)/shard_map/ppermute | solution.py:1137
  295.8 22.5 %collective-permute-start.47 = (bf16[1152,128]{1,0:T(8,128)(2,1)}, bf16[1152,128]{1,0:T(8,128)(2,1)}, u32[]{:S(2)}, u32[]{:S(2)}) collective-permute-start(bf16[1152,128]{1,0:T(8,128)(2,1)} %get-tuple-element.144), channel_id=1, source_target_pairs={{0,24},{4,28},{8,16},{12,20},{16,8},{20,12},{24,0},{28,4},{1,25},{... | collective-permute-start | bytes 884744 | tf_op jit(solution)/shard_map/ppermute | solution.py:1137
  304.6 13.7 %collective-permute-start.48 = (bf16[1152,128]{1,0:T(8,128)(2,1)}, bf16[1152,128]{1,0:T(8,128)(2,1)}, u32[]{:S(2)}, u32[]{:S(2)}) collective-permute-start(bf16[1152,128]{1,0:T(8,128)(2,1)} %get-tuple-element.145), channel_id=1, source_target_pairs={{0,28},{4,24},{8,20},{12,16},{16,12},{20,8},{24,4},{28,0},{1,29},{... | collective-permute-start | bytes 884744 | tf_op jit(solution)/shard_map/ppermute | solution.py:1137
  316.5 34.5 %collective-permute-start.32 = (bf16[512,768]{1,0:T(8,128)(2,1)S(1)}, bf16[512,768]{1,0:T(8,128)(2,1)S(1)}, u32[]{:S(2)}, u32[]{:S(2)}) collective-permute-start(bf16[512,768]{1,0:T(8,128)(2,1)S(1)} %get-tuple-element.130.refs_0_), channel_id=1, source_target_pairs={{0,2},{1,3},{2,0},{3,1},{4,6},{5,7},{6,4},{7,5},{8,10},{9,11},{10,... | collective-permute-start | bytes 2359304 | tf_op jit(solution)/shard_map/ppermute | solution.py:1160
  337.0 50.0 %all-to-all-start = ((bf16[8,112,640]{2,1,0:T(8,128)(2,1)}), bf16[8,112,640]{2,1,0:T(8,128)(2,1)S(1)}, u32[]{:S(2)}, u32[]{:S(2)}) async-start(bf16[8,112,640]{2,1,0:T(8,128)(2,1)} %head_grads.1), calls=%async_computation | async-start | bytes 2293760 | tf_op jit(solution)/shard_map/all_to_all | solution.py:1252
  365.0 25.2 %collective-permute-start.50 = (bf16[512,768]{1,0:T(8,128)(2,1)S(1)}, bf16[512,768]{1,0:T(8,128)(2,1)}, u32[]{:S(2)}, u32[]{:S(2)}) collective-permute-start(bf16[512,768]{1,0:T(8,128)(2,1)S(1)} %add_convert_fusion.3), channel_id=1, source_target_pairs={{0,2},{1,3},{2,0},{3,1},{4,6},{5,7},{6,4},{7,5},{8,10},{9,11},{10,... | collective-permute-start | bytes 2359304 | tf_op jit(solution)/shard_map/ppermute | solution.py:1160
  365.6 35.9 %collective-permute-start.52 = (bf16[512,768]{1,0:T(8,128)(2,1)S(1)}, bf16[512,768]{1,0:T(8,128)(2,1)}, u32[]{:S(2)}, u32[]{:S(2)}) collective-permute-start(bf16[512,768]{1,0:T(8,128)(2,1)S(1)} %add_convert_fusion.1), channel_id=1, source_target_pairs={{0,2},{1,3},{2,0},{3,1},{4,6},{5,7},{6,4},{7,5},{8,10},{9,11},{10,... | collective-permute-start | bytes 2359304 | tf_op jit(solution)/shard_map/ppermute | solution.py:1160
  367.3 44.9 %collective-permute-start.33 = (bf16[512,768]{1,0:T(8,128)(2,1)S(1)}, bf16[512,768]{1,0:T(8,128)(2,1)}, u32[]{:S(2)}, u32[]{:S(2)}) collective-permute-start(bf16[512,768]{1,0:T(8,128)(2,1)S(1)} %get-tuple-element.130.refs_0_), channel_id=1, source_target_pairs={{0,1},{1,0},{2,3},{3,2},{4,5},{5,4},{6,7},{7,6},{8,9},{9,8},{10,11... | collective-permute-start | bytes 2359304 | tf_op jit(solution)/shard_map/ppermute | solution.py:1160
  390.1 22.1 %collective-permute-start.34 = (bf16[512,768]{1,0:T(8,128)(2,1)}, bf16[512,768]{1,0:T(8,128)(2,1)}, u32[]{:S(2)}, u32[]{:S(2)}) collective-permute-start(bf16[512,768]{1,0:T(8,128)(2,1)} %copy-done.22), channel_id=1, source_target_pairs={{0,1},{1,0},{2,3},{3,2},{4,5},{5,4},{6,7},{7,6},{8,9},{9,8},{10,11... | collective-permute-start | bytes 2359304 | tf_op jit(solution)/shard_map/ppermute | solution.py:1160
  391.4 24.3 %collective-permute-start.53 = (bf16[512,768]{1,0:T(8,128)(2,1)S(1)}, bf16[512,768]{1,0:T(8,128)(2,1)}, u32[]{:S(2)}, u32[]{:S(2)}) collective-permute-start(bf16[512,768]{1,0:T(8,128)(2,1)S(1)} %add_convert_fusion.2.refs_0_), channel_id=1, source_target_pairs={{0,1},{1,0},{2,3},{3,2},{4,5},{5,4},{6,7},{7,6},{8,9},{9,8},{10,11... | collective-permute-start | bytes 2359304 | tf_op jit(solution)/shard_map/ppermute | solution.py:1160
  (94 other events, 1144.8 us)
Sparse Core Ops, SparseCore 0:
  10.8 82.0 all-gather.1
  318.4 95.8 reduce-scatter.1
where the time goes:
time: 430 us; the launch traced here: 429 us
  waiting for transfers between devices  145 us (34%)
  Pallas kernels  144 us (33%)
  starting transfers between devices  99.7 us (23%)
  local copies, waits for them, and re-layouts  18.6 us (4%)
  between operations  14.7 us (3%)
  other arithmetic  6.64 us (2%)
    ppermute x28, waiting for transfers between devices, over_rows(): out.append(lax.ppermute(rows, 'dp', [(i, i ^ s) for i in range(lay.peers)]))  69.2 us
    ppermute x28, starting transfers between devices, over_rows(): out.append(lax.ppermute(rows, 'dp', [(i, i ^ s) for i in range(lay.peers)]))  61.4 us
    ppermute x22, waiting for transfers between devices, swap(): return lax.ppermute(rows, 'mp', [(i, i ^ flip) for i in range(4)])  36.1 us
    pallas_call x1, Pallas kernels, middle(): pl.pallas_call(middle_kernel, grid_spec=spec, out_shape=[jax.ShapeDtypeSt...  27.1 us
    pallas_call x3, Pallas kernels, weight_grads(): pl.pallas_call(partial(weight_grad_kernel, chunks, len(adds)), grid_spec=...  23.5 us
    ppermute x7, waiting for transfers between devices, flip(): return lax.ppermute(rows, 'dp', [(i, i ^ s) for i in range(lay.peers)])  20 us
    all_to_all x1, waiting for transfers between devices, on_device(): terms = lax.all_to_all(terms, 'dp', split_axis=0, concat_axis=0, tiled=True)  19.7 us
    pallas_call x1, Pallas kernels, project_rows(): pl.pallas_call(partial(project_kernel, lay, steps), grid_spec=spec, out_s...  15.1 us
  transfers between devices with their start and end apart: 60, of which 27 were waited for; matrix products, arithmetic and copies ran while one was open for 2% of the time, Pallas kernels for 25%

commit v1 on v0

--- a/solution.py
+++ b/solution.py
@@ -35,6 +35,7 @@
 SPREAD_US = 3
 HEAD_GRADS_US = 4
 SORT_US = 80
+ATTEND_BACK_US = 40
 
 
 def nn(a, b):
@@ -410,7 +411,7 @@
         out_shape=lay.shapes(lay.data_rows)
         + [jax.ShapeDtypeStruct((lay.heads, 8, LANES), f32)],
         name="attend_back",
-        cost_estimate=QUICK,
+        cost_estimate=cost(ATTEND_BACK_US),
     )(*arrived, *arrived, *grads)
     return list(out[:-1]), out[-1]
 
@@ -823,7 +824,7 @@
         ]
         + [jax.ShapeDtypeStruct((256, width), bf16)] * 4
         + [jax.ShapeDtypeStruct((16, D), f32)],
-        compiler_params=pltpu.CompilerParams(vmem_limit_bytes=50 * 1024 * 1024),
+        compiler_params=pltpu.CompilerParams(vmem_limit_bytes=VMEM),
         name="middle",
         cost_estimate=QUICK,
     )(places, *att, hidden, cotangent, params, *weights)
@@ -1211,7 +1212,7 @@
     found = unsort_rows(lay, places, mixed, code)
     att = over_heads(found)
     far_w = after(far_w, found[0])
-    middle_w = [own_w, swap(own_w, 1), far_w, swap(far_w, 1)]
+    middle_w = [own_w, in_hbm(swap(own_w, 1)), far_w, in_hbm(swap(far_w, 1))]
     saved, att_grad, vec = middle(places, att, hidden_in, cotangent, params, middle_w)
     out_quarter, act, pre_grad, first_low, ffn_grad, branch_grad, grad_h1 = saved
     saved = tuple(in_hbm(a) for a in (act, pre_grad, first_low, ffn_grad, branch_grad))
@@ -1225,8 +1226,9 @@
     grads = over_rows(lay, grads)
     slot_grads, bias_sums = attend_back(lay, arrived, grads)
 
-    summed = weight_grads(places, saved, att, 0, 1, [(from_core, 1), (from_far, 0)])
     returned = over_rows(lay, slot_grads)
+    ready = (after(act, *returned[1:4]),) + saved[1:]
+    summed = weight_grads(places, ready, att, 0, 1, [(from_core, 1), (from_far, 0)])
     head_sums = bias_sums[:, :2].reshape(heads, 2, 2, HEAD_DIM).sum(axis=2)
     head_sums = head_sums.transpose(1, 0, 2).reshape(2, width)
     vec = lax.dynamic_update_slice(vec[:12], head_sums, (0, place * width))
@@ -1244,6 +1246,7 @@
     chips = [
         (mine.astype(f32) + swap(other, 1).astype(f32)).astype(bf16) for other, mine in groups
     ]
+    others = [swap(chip, 2) for chip in chips]
     hidden_out = order_quarters(
         jnp.stack([place, place ^ 2, place ^ 1, place ^ 3]).astype(i32),
         [out_quarter, far, swap(out_quarter, 1), swap(far, 1)],
@@ -1253,18 +1256,19 @@
         ends = finish_heads(terms, depth, width)
     else:
         ends = reduce_heads(terms, vec, depth, width)
+    small = ends[3] + swap(ends[3], 1)
+    small = finish_vectors(small, swap(small, 2), depth)
+    chips[1] = after(chips[1], ends[0], hidden_out)
     ready = [
-        (after(chip, ends[0]).astype(f32) + swap(chip, 2).astype(f32)).astype(bf16)
-        for chip in chips
+        (chip.astype(f32) + part.astype(f32)).astype(bf16) for chip, part in zip(chips, others)
     ]
     core = place % 2
+    order = jnp.stack([2 * core, 2 * core + 1, 2 - 2 * core, 3 - 2 * core]).astype(i32)
     grad_hidden = order_quarters(
-        jnp.stack([2 * core, 2 * core + 1, 2 - 2 * core, 3 - 2 * core]).astype(i32),
+        after(order, small[0]),
         ready + [swap(part, 1) for part in ready],
     )
 
-    small = ends[3] + swap(ends[3], 1)
-    small = finish_vectors(small, swap(small, 2), depth)
     grad_inner, grad_outer, grad_output = finish_middle(reduced)
     return (
         hidden_out,

time: 430 us -> 419 us (0.974)
  waiting for transfers between devices: 145 us -> 136 us
    all_to_all x1, starting transfers between devices: 14 us -> 3.57 us  [on_device(): terms = lax.all_to_all(terms, 'dp', split_axis=0, concat_axis=0, tiled=True)]
    ppermute x28, waiting for transfers between devices: 69.2 us -> 60.1 us  [over_rows(): out.append(lax.ppermute(rows, 'dp', [(i, i ^ s) for i in range(lay.peers)]))]
    ppermute x28, starting transfers between devices: 61.4 us -> 67.4 us  [over_rows(): out.append(lax.ppermute(rows, 'dp', [(i, i ^ s) for i in range(lay.peers)]))]
    unnamed x132 -> x94, local copies, waits for them, and re-layouts: 14.5 us -> 13.3 us
  transfers between devices with their start and end apart: 60 -> 60, of which waited for: 27 -> 23; matrix products, arithmetic and copies ran while one was open for 2% -> 2% of each run, Pallas kernels for 25% -> 27%
where the time goes in v1:
time: 419 us; the launch traced here: 417 us
  Pallas kernels  146 us (35%)
  waiting for transfers between devices  136 us (32%)
  starting transfers between devices  96.3 us (23%)
  local copies, waits for them, and re-layouts  17.4 us (4%)
  between operations  14.5 us (3%)
  other arithmetic  6.61 us (2%)
    ppermute x28, starting transfers between devices, over_rows(): out.append(lax.ppermute(rows, 'dp', [(i, i ^ s) for i in range(lay.peers)]))  67.4 us
    ppermute x28, waiting for transfers between devices, over_rows(): out.append(lax.ppermute(rows, 'dp', [(i, i ^ s) for i in range(lay.peers)]))  60.1 us
    ppermute x22, waiting for transfers between devices, swap(): return lax.ppermute(rows, 'mp', [(i, i ^ flip) for i in range(4)])  39.1 us
    pallas_call x1, Pallas kernels, middle(): pl.pallas_call(middle_kernel, grid_spec=spec, out_shape=[jax.ShapeDtypeSt...  28.8 us
    pallas_call x3, Pallas kernels, weight_grads(): pl.pallas_call(partial(weight_grad_kernel, chunks, len(adds)), grid_spec=...  23.4 us
    ppermute x7, waiting for transfers between devices, flip(): return lax.ppermute(rows, 'dp', [(i, i ^ s) for i in range(lay.peers)])  20 us
    all_to_all x1, waiting for transfers between devices, on_device(): terms = lax.all_to_all(terms, 'dp', split_axis=0, concat_axis=0, tiled=True)  17.1 us
    pallas_call x1, Pallas kernels, project_rows(): pl.pallas_call(partial(project_kernel, lay, steps), grid_spec=spec, out_s...  15.1 us
  transfers between devices with their start and end apart: 60, of which 23 were waited for; matrix products, arithmetic and copies ran while one was open for 2% of the time, Pallas kernels for 27%

profile of v1, /device:TPU:0, one launch (start us, length us, event | category | flops | bytes accessed | tf_op | source)
XLA Modules:
  0.0 417.3 jit_solution(16688858506616200594)
XLA Ops:
  10.6 4.1 collective-permute-start.3
  18.2 3.8 collective-permute-done.3.refs_4_
  28.7 4.5 %collective-permute-done.2.refs_3_ = bf16[96,768]{1,0:T(8,128)(2,1)S(1)} collective-permute-done((bf16[96,768]{1,0:T(8,128)(2,1)}, bf16[96,768]{1,0:T(8,128)(2,1)S(1)}, u32[]{:S(2)}, u32[]{:S(2)}) %collective-permute-start.2) | collective-permute-done | bytes 147488 | tf_op jit(solution)/shard_map/ppermute | solution.py:1148
  33.2 8.3 %collective-permute-done.5.refs_6_ = bf16[96,768]{1,0:T(8,128)(2,1)S(1)} collective-permute-done((bf16[96,768]{1,0:T(8,128)(2,1)S(1)}, bf16[96,768]{1,0:T(8,128)(2,1)S(1)}, u32[]{:S(2)}, u32[]{:S(2)}) %collective-permute-start.5) | collective-permute-done | bytes 147488 | tf_op jit(solution)/shard_map/ppermute | solution.py:1148
  48.2 15.1 %project_rows.1 = (bf16[1168,128]{1,0:T(8,128)(2,1)}, bf16[1168,128]{1,0:T(8,128)(2,1)}, bf16[1168,128]{1,0:T(8,128)(2,1)}, bf16[1168,128]{1,0:T(8,128)(2,1)}, b...) custom-call(s32[2]{0:T(128)} %pad_add_fusion.1.place_ref, ...), custom_call_target="tpu_custom_call" | custom-call | flops 1000000 | bytes 3000 | tf_op jit(solution)/shard_map/project_rows/pallas_call | solution.py:288
  70.7 17.3 %collective-permute-done.8.refs_2_.refs_10_ = bf16[1168,128]{1,0:T(8,128)(2,1)S(1)} collective-permute-done((bf16[1168,128]{1,0:T(8,128)(2,1)}, bf16[1168,128]{1,0:T(8,128)(2,1)S(1)}, u32[]{:S(2)}, u32[]{:S(2)}) %collective-permute-start.8) | collective-permute-done | bytes 299040 | tf_op jit(solution)/shard_map/ppermute | solution.py:1138
  98.5 5.5 %collective-permute-done.11.refs_5_.refs_13_ = bf16[1168,128]{1,0:T(8,128)(2,1)S(1)} collective-permute-done((bf16[1168,128]{1,0:T(8,128)(2,1)}, bf16[1168,128]{1,0:T(8,128)(2,1)S(1)}, u32[]{:S(2)}, u32[]{:S(2)}) %collective-permute-start.11) | collective-permute-done | bytes 299040 | tf_op jit(solution)/shard_map/ppermute | solution.py:1138
  104.0 6.9 %collective-permute-done.13.refs_7_.refs_15_ = bf16[1168,128]{1,0:T(8,128)(2,1)S(1)} collective-permute-done((bf16[1168,128]{1,0:T(8,128)(2,1)}, bf16[1168,128]{1,0:T(8,128)(2,1)S(1)}, u32[]{:S(2)}, u32[]{:S(2)}) %collective-permute-start.13) | collective-permute-done | bytes 299040 | tf_op jit(solution)/shard_map/ppermute | solution.py:1138
  110.9 5.0 %collective-permute-done.12.refs_6_.refs_14_ = bf16[1168,128]{1,0:T(8,128)(2,1)S(1)} collective-permute-done((bf16[1168,128]{1,0:T(8,128)(2,1)}, bf16[1168,128]{1,0:T(8,128)(2,1)S(1)}, u32[]{:S(2)}, u32[]{:S(2)}) %collective-permute-start.12) | collective-permute-done | bytes 299040 | tf_op jit(solution)/shard_map/ppermute | solution.py:1138
  116.6 5.2 %attend.1 = (bf16[384,128]{1,0:T(8,128)(2,1)}, bf16[384,128]{1,0:T(8,128)(2,1)}, bf16[384,128]{1,0:T(8,128)(2,1)}, bf16[384,128]{1,0:T(8,128)(2,1)}, bf16[384,12...) custom-call(bf16[1168,128]{1,0:T(8,128)(2,1)} %get-tuple-element.94.refs_0_.refs_, ...), custom_call_target="tpu_custom_call" | custom-call | flops 46000001024 | bytes 138000000 | tf_op jit(solution)/shard_map/attend/pallas_call | solution.py:363
  124.6 10.5 %collective-permute-start.15 = (bf16[384,128]{1,0:T(8,128)(2,1)}, bf16[384,128]{1,0:T(8,128)(2,1)S(1)}, u32[]{:S(2)}, u32[]{:S(2)}) collective-permute-start(bf16[384,128]{1,0:T(8,128)(2,1)} %get-tuple-element.106), channel_id=1, source_target_pairs={{0,8},{4,12},{8,0},{12,4},{16,24},{20,28},{24,16},{28,20},{1,9},{5... | collective-permute-start | bytes 294920 | tf_op jit(solution)/shard_map/ppermute | solution.py:1138
  145.0 5.5 %collective-permute-done.17.refs_4_ = bf16[384,128]{1,0:T(8,128)(2,1)S(1)} collective-permute-done((bf16[384,128]{1,0:T(8,128)(2,1)}, bf16[384,128]{1,0:T(8,128)(2,1)S(1)}, u32[]{:S(2)}, u32[]{:S(2)}) %collective-permute-start.17) | collective-permute-done | bytes 98336 | tf_op jit(solution)/shard_map/ppermute | solution.py:1138
  153.2 6.6 %unsort_rows.1 = (bf16[256,384]{1,0:T(8,128)(2,1)}, bf16[256,384]{1,0:T(8,128)(2,1)}, bf16[256,384]{1,0:T(8,128)(2,1)}, bf16[256,384]{1,0:T(8,128)(2,1)}) custom-call(s32[2]{0:T(128)} %pad_add_fusion.1.place_ref, bf16[384,128]{1,0:T(8,128)(2,1)} %get-tuple-element.104.refs_0_, bf16[384,128]{1,0:T(8,128)(2,1)} %copy-done.23, bf16[384,128]{1,0:T(8,128)(2,1)} %copy-done.24, ...), custom_call_target="tpu_custom_call" | custom-call | flops 1000000 | bytes 3000 | tf_op jit(solution)/shard_map/unsort_rows/pallas_call | solution.py:448
  162.3 7.7 %collective-permute-done.21.att1.refs_1_ = bf16[256,384]{1,0:T(8,128)(2,1)S(1)} collective-permute-done((bf16[256,384]{1,0:T(8,128)(2,1)}, bf16[256,384]{1,0:T(8,128)(2,1)S(1)}, u32[]{:S(2)}, u32[]{:S(2)}) %collective-permute-start.21) | collective-permute-done | bytes 196640 | tf_op jit(solution)/shard_map/ppermute | solution.py:1161
  175.1 28.8 %middle.1 = (bf16[512,768]{1,0:T(8,128)(2,1)}, bf16[512,3072]{1,0:T(8,128)(2,1)}, bf16[512,3072]{1,0:T(8,128)(2,1)}, bf16[512,768]{1,0:T(8,128)(2,1)}, bf16[512,...) custom-call(s32[2]{0:T(128)} %pad_add_fusion.1.place_ref, ...), custom_call_target="tpu_custom_call" | custom-call | flops 1000000 | bytes 3000 | tf_op jit(solution)/shard_map/middle/pallas_call | solution.py:813
  205.8 10.0 %weight_grads.3 = bf16[1536,1920]{1,0:T(8,128)(2,1)} custom-call(s32[2]{0:T(128)} %pad_add_fusion.1.place_ref, bf16[512,3072]{1,0:T(8,128)(2,1)} %get-tuple-element.141.act_ref, bf16[512,3072]{1,0:T(8,128)(2,1)} %get-tuple-element.137.pre_ref, bf16[512,768]{1,0:T(8,128)(2,1)} %get-tuple-element.138.low_ref, bf16[512,768]{1,0:T(8,128)(2,1)} %get-tuple-element.139.ffn_ref, ...), custom_call_target="tpu_custom_call" | custom-call | flops 1000000 | bytes 3000 | tf_op jit(solution)/shard_map/weight_grads/pallas_call | solution.py:875
  217.2 7.4 %sort_rows.1 = (bf16[384,128]{1,0:T(8,128)(2,1)}, bf16[384,128]{1,0:T(8,128)(2,1)}, bf16[384,128]{1,0:T(8,128)(2,1)}, bf16[384,128]{1,0:T(8,128)(2,1)}, bf16[384...) custom-call(s32[2]{0:T(128)} %pad_add_fusion.1.place_ref, ...), custom_call_target="tpu_custom_call" | custom-call | flops 80000000000 | bytes 240000000 | tf_op jit(solution)/shard_map/sort_rows/pallas_call | solution.py:487
  237.8 6.2 %weight_grads.4 = bf16[768,1920]{1,0:T(8,128)(2,1)} custom-call(s32[2]{0:T(128)} %pad_add_fusion.1.place_ref, bf16[512,3072]{1,0:T(8,128)(2,1)} %get-tuple-element.141.act_ref, bf16[512,3072]{1,0:T(8,128)(2,1)} %get-tuple-element.137.pre_ref, bf16[512,768]{1,0:T(8,128)(2,1)} %get-tuple-element.138.low_ref, bf16[512,768]{1,0:T(8,128)(2,1)} %get-tuple-element.139.ffn_ref, ...), custom_call_target="tpu_custom_call" | custom-call | flops 1000000 | bytes 3000 | tf_op jit(solution)/shard_map/weight_grads/pallas_call | solution.py:875
  246.6 10.7 %attend_back.1 = (bf16[1152,128]{1,0:T(8,128)(2,1)}, bf16[1152,128]{1,0:T(8,128)(2,1)}, bf16[1152,128]{1,0:T(8,128)(2,1)}, bf16[1152,128]{1,0:T(8,128)(2,1)}, bf...) custom-call(bf16[1168,128]{1,0:T(8,128)(2,1)} %get-tuple-element.94., ...), custom_call_target="tpu_custom_call" | custom-call | flops 40000000000 | bytes 120000000 | tf_op jit(solution)/shard_map/attend_back/pallas_call | solution.py:404
  258.3 3.8 collective-permute-start.38
  265.2 6.6 %collective-permute-start.46 = (bf16[1152,128]{1,0:T(8,128)(2,1)}, bf16[1152,128]{1,0:T(8,128)(2,1)}, u32[]{:S(2)}, u32[]{:S(2)}) collective-permute-start(bf16[1152,128]{1,0:T(8,128)(2,1)} %get-tuple-element.145), channel_id=1, source_target_pairs={{0,20},{4,16},{8,28},{12,24},{16,4},{20,0},{24,12},{28,8},{1,21},{... | collective-permute-start | bytes 884744 | tf_op jit(solution)/shard_map/ppermute | solution.py:1138
  271.9 10.1 %collective-permute-done.38.refs_2_ = bf16[1152,128]{1,0:T(8,128)(2,1)} collective-permute-done((bf16[1152,128]{1,0:T(8,128)(2,1)}, bf16[1152,128]{1,0:T(8,128)(2,1)}, u32[]{:S(2)}, u32[]{:S(2)}) %collective-permute-start.38) | collective-permute-done | bytes 294944 | tf_op jit(solution)/shard_map/ppermute | solution.py:1138
  291.6 16.9 %collective-permute-done.41.refs_2_ = bf16[768,1920]{1,0:T(8,128)(2,1)S(1)} collective-permute-done((bf16[768,1920]{1,0:T(8,128)(2,1)}, bf16[768,1920]{1,0:T(8,128)(2,1)S(1)}, u32[]{:S(2)}, u32[]{:S(2)}) %collective-permute-start.41) | collective-permute-done | bytes 2949152 | tf_op jit(solution)/shard_map/ppermute | solution.py:1161
  310.1 7.2 %weight_grads.5 = bf16[768,1920]{1,0:T(8,128)(2,1)} custom-call(s32[2]{0:T(128)} %pad_add_fusion.1.place_ref, bf16[512,3072]{1,0:T(8,128)(2,1)} %get-tuple-element.141.act_ref, bf16[512,3072]{1,0:T(8,128)(2,1)} %get-tuple-element.137.pre_ref, bf16[512,768]{1,0:T(8,128)(2,1)} %get-tuple-element.138.low_ref, bf16[512,768]{1,0:T(8,128)(2,1)} %get-tuple-element.139.ffn_ref, ...), custom_call_target="tpu_custom_call" | custom-call | flops 1000000 | bytes 3000 | tf_op jit(solution)/shard_map/weight_grads/pallas_call | solution.py:875
  320.0 10.9 %collect.1.dense_ref = bf16[2048,640]{1,0:T(8,128)(2,1)} custom-call(s32[2]{0:T(128)} %pad_add_fusion.1.place_ref, bf16[1152,128]{1,0:T(8,128)(2,1)} %get-tuple-element.143.refs_0_, bf16[1152,128]{1,0:T(8,128)(2,1)} %copy-done.39, bf16[1152,128]{1,0:T(8,128)(2,1)} %collective-permute-done.38.refs_2_, bf16[1152,128]{1,0:T(8,128)(2,1)} %collective-permute-done.39.refs_3_, ...), custom_call_target="tpu_custom_call" | custom-call | flops 30000001024 | bytes 90000000 | tf_op jit(solution)/shard_map/collect/pallas_call | solution.py:924
  330.9 7.0 %head_grads.1 = bf16[8,112,640]{2,1,0:T(8,128)(2,1)} custom-call(s32[2]{0:T(128)} %pad_add_fusion.1.place_ref, bf16[2048,768]{1,0:T(8,128)(2,1)} %x_ref.3, bf16[2048,640]{1,0:T(8,128)(2,1)} %collect.1.dense_ref, f32[8,16,128]{2,1,0:T(8,128)} %select_maximum_fusion.vec_ref), custom_call_target="tpu_custom_call" | custom-call | flops 4000000000 | bytes 12000000 | tf_op jit(solution)/shard_map/head_grads/pallas_call | solution.py:1019
  337.9 3.6 all-to-all-start
  341.5 5.6 %spread_grads.3 = (bf16[512,768]{1,0:T(8,128)(2,1)}, bf16[512,768]{1,0:T(8,128)(2,1)}) custom-call(s32[2]{0:T(128)} %pad_add_fusion.1.place_ref, bf16[2048,640]{1,0:T(8,128)(2,1)} %collect.1.dense_ref, bf16[768,640]{1,0:T(8,128)(2,1)} %get-tuple-element.92.w_ref, f32[512,768]{1,0:T(8,128)} %get-tuple-element.154.h1_ref), custom_call_target="tpu_custom_call" | custom-call | flops 3000000000 | bytes 9000000 | tf_op jit(solution)/shard_map/spread_grads/pallas_call | solution.py:966
  347.1 5.7 %spread_grads.2 = (bf16[512,768]{1,0:T(8,128)(2,1)}, bf16[512,768]{1,0:T(8,128)(2,1)}) custom-call(s32[2]{0:T(128)} %pad_add_fusion.1.place_ref, bf16[2048,640]{1,0:T(8,128)(2,1)} %collect.1.dense_ref, bf16[768,640]{1,0:T(8,128)(2,1)} %get-tuple-element.92.w_ref, f32[512,768]{1,0:T(8,128)} %get-tuple-element.154.h1_ref), custom_call_target="tpu_custom_call" | custom-call | flops 3000000000 | bytes 9000000 | tf_op jit(solution)/shard_map/spread_grads/pallas_call | solution.py:966
  358.8 17.1 %all-to-all-done.refs_0_ = bf16[8,112,640]{2,1,0:T(8,128)(2,1)S(1)} async-done(((bf16[8,112,640]{2,1,0:T(8,128)(2,1)}), bf16[8,112,640]{2,1,0:T(8,128)(2,1)S(1)}, u32[]{:S(2)}, u32[]{:S(2)}) %all-to-all-start) | async-done | bytes 1146912 | tf_op jit(solution)/shard_map/all_to_all | solution.py:1255
  379.0 3.5 order_quarters.2
  383.9 8.5 %collective-permute-done.52 = bf16[512,768]{1,0:T(8,128)(2,1)} collective-permute-done((bf16[512,768]{1,0:T(8,128)(2,1)S(1)}, bf16[512,768]{1,0:T(8,128)(2,1)}, u32[]{:S(2)}, u32[]{:S(2)}) %collective-permute-start.52) | collective-permute-done | bytes 786464 | tf_op jit(solution)/shard_map/ppermute | solution.py:1161
  (227 shorter events, 127.3 us)
Async XLA Ops:
  7.2 89.4 %all-gather.2.cloned.1.call-start = ((), (), s32[]{:S(2)}) async-start(), calls=%async_computation.2 | async-start | bytes 3317760 | tf_op jit(solution)/shard_map/all_gather | solution.py:1200
  10.5 397.9 %reduce-scatter.2.cloned.1.call-start = ((), (), s32[]{:S(2)}) async-start(), calls=%async_computation.3 | async-start | bytes 3317760 | tf_op jit(solution)/shard_map/reduce_scatter | solution.py:1240
  17.8 15.4 %collective-permute-start.2 = (bf16[96,768]{1,0:T(8,128)(2,1)}, bf16[96,768]{1,0:T(8,128)(2,1)S(1)}, u32[]{:S(2)}, u32[]{:S(2)}) collective-permute-start(bf16[96,768]{1,0:T(8,128)(2,1)} %get-tuple-element.91.refs_0_), channel_id=1, source_target_pairs={{0,12},{4,8},{8,4},{12,0},{16,28},{20,24},{24,20},{28,16},{1,13},{... | collective-permute-start | bytes 442376 | tf_op jit(solution)/shard_map/ppermute | solution.py:1148
  23.6 17.9 %collective-permute-start.5 = (bf16[96,768]{1,0:T(8,128)(2,1)S(1)}, bf16[96,768]{1,0:T(8,128)(2,1)S(1)}, u32[]{:S(2)}, u32[]{:S(2)}) collective-permute-start(bf16[96,768]{1,0:T(8,128)(2,1)S(1)} %collective-permute-done.3.refs_4_), channel_id=1, source_target_pairs={{0,8},{4,12},{8,0},{12,4},{16,24},{20,28},{24,16},{28,20},{1,9},{5... | collective-permute-start | bytes 442376 | tf_op jit(solution)/shard_map/ppermute | solution.py:1148
  24.3 20.5 %collective-permute-start.6 = (bf16[96,768]{1,0:T(8,128)(2,1)S(1)}, bf16[96,768]{1,0:T(8,128)(2,1)S(1)}, u32[]{:S(2)}, u32[]{:S(2)}) collective-permute-start(bf16[96,768]{1,0:T(8,128)(2,1)S(1)} %collective-permute-done.3.refs_4_), channel_id=1, source_target_pairs={{0,12},{4,8},{8,4},{12,0},{16,28},{20,24},{24,20},{28,16},{1,13},{... | collective-permute-start | bytes 442376 | tf_op jit(solution)/shard_map/ppermute | solution.py:1148
  63.3 24.7 %collective-permute-start.8 = (bf16[1168,128]{1,0:T(8,128)(2,1)}, bf16[1168,128]{1,0:T(8,128)(2,1)S(1)}, u32[]{:S(2)}, u32[]{:S(2)}) collective-permute-start(bf16[1168,128]{1,0:T(8,128)(2,1)} %get-tuple-element.96), channel_id=1, source_target_pairs={{0,8},{4,12},{8,0},{12,4},{16,24},{20,28},{24,16},{28,20},{1,9},{5... | collective-permute-start | bytes 897032 | tf_op jit(solution)/shard_map/ppermute | solution.py:1138
  63.3 27.9 %collective-permute-start.7 = (bf16[1168,128]{1,0:T(8,128)(2,1)}, bf16[1168,128]{1,0:T(8,128)(2,1)S(1)}, u32[]{:S(2)}, u32[]{:S(2)}) collective-permute-start(bf16[1168,128]{1,0:T(8,128)(2,1)} %get-tuple-element.95), channel_id=1, source_target_pairs={{0,4},{4,0},{8,12},{12,8},{16,20},{20,16},{24,28},{28,24},{1,5},{5... | collective-permute-start | bytes 897032 | tf_op jit(solution)/shard_map/ppermute | solution.py:1138
  64.9 31.6 %collective-permute-start.10 = (bf16[1168,128]{1,0:T(8,128)(2,1)}, bf16[1168,128]{1,0:T(8,128)(2,1)}, u32[]{:S(2)}, u32[]{:S(2)}) collective-permute-start(bf16[1168,128]{1,0:T(8,128)(2,1)} %get-tuple-element.98), channel_id=1, source_target_pairs={{0,16},{4,20},{8,24},{12,28},{16,0},{20,4},{24,8},{28,12},{1,17},{... | collective-permute-start | bytes 897032 | tf_op jit(solution)/shard_map/ppermute | solution.py:1138
  67.7 36.3 %collective-permute-start.11 = (bf16[1168,128]{1,0:T(8,128)(2,1)}, bf16[1168,128]{1,0:T(8,128)(2,1)S(1)}, u32[]{:S(2)}, u32[]{:S(2)}) collective-permute-start(bf16[1168,128]{1,0:T(8,128)(2,1)} %get-tuple-element.99), channel_id=1, source_target_pairs={{0,20},{4,16},{8,28},{12,24},{16,4},{20,0},{24,12},{28,8},{1,21},{... | collective-permute-start | bytes 897032 | tf_op jit(solution)/shard_map/ppermute | solution.py:1138
  67.8 36.2 %collective-permute-start.9 = (bf16[1168,128]{1,0:T(8,128)(2,1)}, bf16[1168,128]{1,0:T(8,128)(2,1)S(1)}, u32[]{:S(2)}, u32[]{:S(2)}) collective-permute-start(bf16[1168,128]{1,0:T(8,128)(2,1)} %get-tuple-element.97), channel_id=1, source_target_pairs={{0,12},{4,8},{8,4},{12,0},{16,28},{20,24},{24,20},{28,16},{1,13},{... | collective-permute-start | bytes 897032 | tf_op jit(solution)/shard_map/ppermute | solution.py:1138
  88.0 22.8 %collective-permute-start.13 = (bf16[1168,128]{1,0:T(8,128)(2,1)}, bf16[1168,128]{1,0:T(8,128)(2,1)S(1)}, u32[]{:S(2)}, u32[]{:S(2)}) collective-permute-start(bf16[1168,128]{1,0:T(8,128)(2,1)} %get-tuple-element.103), channel_id=1, source_target_pairs={{0,28},{4,24},{8,20},{12,16},{16,12},{20,8},{24,4},{28,0},{1,29},{... | collective-permute-start | bytes 897032 | tf_op jit(solution)/shard_map/ppermute | solution.py:1138
  91.2 24.7 %collective-permute-start.12 = (bf16[1168,128]{1,0:T(8,128)(2,1)}, bf16[1168,128]{1,0:T(8,128)(2,1)S(1)}, u32[]{:S(2)}, u32[]{:S(2)}) collective-permute-start(bf16[1168,128]{1,0:T(8,128)(2,1)} %get-tuple-element.101), channel_id=1, source_target_pairs={{0,24},{4,28},{8,16},{12,20},{16,8},{20,12},{24,0},{28,4},{1,25},{... | collective-permute-start | bytes 897032 | tf_op jit(solution)/shard_map/ppermute | solution.py:1138
  96.6 63.3 %collective-permute-start.25 = (bf16[768,1920]{1,0:T(8,128)(2,1)}, bf16[768,1920]{1,0:T(8,128)(2,1)}, u32[]{:S(2)}, u32[]{:S(2)}) collective-permute-start(bf16[768,1920]{1,0:T(8,128)(2,1)} %all-gather.2.cloned.1.call-done.w0), channel_id=1, source_target_pairs={{0,2},{1,3},{2,0},{3,1},{4,6},{5,7},{6,4},{7,5},{8,10},{9,11},{10,... | collective-permute-start | bytes 8847368 | tf_op jit(solution)/shard_map/ppermute | solution.py:1161
  121.8 15.9 %collective-permute-start.14 = (bf16[384,128]{1,0:T(8,128)(2,1)}, bf16[384,128]{1,0:T(8,128)(2,1)S(1)}, u32[]{:S(2)}, u32[]{:S(2)}) collective-permute-start(bf16[384,128]{1,0:T(8,128)(2,1)} %get-tuple-element.105), channel_id=1, source_target_pairs={{0,4},{4,0},{8,12},{12,8},{16,20},{20,16},{24,28},{28,24},{1,5},{5... | collective-permute-start | bytes 294920 | tf_op jit(solution)/shard_map/ppermute | solution.py:1138
  124.6 15.6 %collective-permute-start.15 = (bf16[384,128]{1,0:T(8,128)(2,1)}, bf16[384,128]{1,0:T(8,128)(2,1)S(1)}, u32[]{:S(2)}, u32[]{:S(2)}) collective-permute-start(bf16[384,128]{1,0:T(8,128)(2,1)} %get-tuple-element.106), channel_id=1, source_target_pairs={{0,8},{4,12},{8,0},{12,4},{16,24},{20,28},{24,16},{28,20},{1,9},{5... | collective-permute-start | bytes 294920 | tf_op jit(solution)/shard_map/ppermute | solution.py:1138
  215.8 19.4 %collective-permute-start.40 = (bf16[1536,1920]{1,0:T(8,128)(2,1)}, bf16[1536,1920]{1,0:T(8,128)(2,1)}, u32[]{:S(2)}, u32[]{:S(2)}) collective-permute-start(bf16[1536,1920]{1,0:T(8,128)(2,1)} %weight_grads.3), channel_id=1, source_target_pairs={{0,1},{1,0},{2,3},{3,2},{4,5},{5,4},{6,7},{7,6},{8,9},{9,8},{10,11... | collective-permute-start | bytes 17694728 | tf_op jit(solution)/shard_map/ppermute | solution.py:1161
  228.6 15.5 %collective-permute-start.32 = (bf16[384,128]{1,0:T(8,128)(2,1)}, bf16[384,128]{1,0:T(8,128)(2,1)S(1)}, u32[]{:S(2)}, u32[]{:S(2)}) collective-permute-start(bf16[384,128]{1,0:T(8,128)(2,1)} %get-tuple-element.128), channel_id=1, source_target_pairs={{0,12},{4,8},{8,4},{12,0},{16,28},{20,24},{24,20},{28,16},{1,13},{... | collective-permute-start | bytes 294920 | tf_op jit(solution)/shard_map/ppermute | solution.py:1138
  228.7 16.9 %collective-permute-start.33 = (bf16[384,128]{1,0:T(8,128)(2,1)}, bf16[384,128]{1,0:T(8,128)(2,1)S(1)}, u32[]{:S(2)}, u32[]{:S(2)}) collective-permute-start(bf16[384,128]{1,0:T(8,128)(2,1)} %get-tuple-element.129), channel_id=1, source_target_pairs={{0,16},{4,20},{8,24},{12,28},{16,0},{20,4},{24,8},{28,12},{1,17},{... | collective-permute-start | bytes 294920 | tf_op jit(solution)/shard_map/ppermute | solution.py:1138
  244.1 64.4 %collective-permute-start.41 = (bf16[768,1920]{1,0:T(8,128)(2,1)}, bf16[768,1920]{1,0:T(8,128)(2,1)S(1)}, u32[]{:S(2)}, u32[]{:S(2)}) collective-permute-start(bf16[768,1920]{1,0:T(8,128)(2,1)} %weight_grads.4), channel_id=1, source_target_pairs={{0,2},{1,3},{2,0},{3,1},{4,6},{5,7},{6,4},{7,5},{8,10},{9,11},{10,... | collective-permute-start | bytes 8847368 | tf_op jit(solution)/shard_map/ppermute | solution.py:1161
  258.3 23.7 %collective-permute-start.38 = (bf16[1152,128]{1,0:T(8,128)(2,1)}, bf16[1152,128]{1,0:T(8,128)(2,1)}, u32[]{:S(2)}, u32[]{:S(2)}) collective-permute-start(bf16[1152,128]{1,0:T(8,128)(2,1)} %get-tuple-element.134), channel_id=1, source_target_pairs={{0,8},{4,12},{8,0},{12,4},{16,24},{20,28},{24,16},{28,20},{1,9},{5... | collective-permute-start | bytes 884744 | tf_op jit(solution)/shard_map/ppermute | solution.py:1138
  262.1 25.3 %collective-permute-start.39 = (bf16[1152,128]{1,0:T(8,128)(2,1)}, bf16[1152,128]{1,0:T(8,128)(2,1)}, u32[]{:S(2)}, u32[]{:S(2)}) collective-permute-start(bf16[1152,128]{1,0:T(8,128)(2,1)} %get-tuple-element.135), channel_id=1, source_target_pairs={{0,12},{4,8},{8,4},{12,0},{16,28},{20,24},{24,20},{28,16},{1,13},{... | collective-permute-start | bytes 884744 | tf_op jit(solution)/shard_map/ppermute | solution.py:1138
  262.8 54.6 %collective-permute-start.45 = (bf16[1152,128]{1,0:T(8,128)(2,1)}, bf16[1152,128]{1,0:T(8,128)(2,1)}, u32[]{:S(2)}, u32[]{:S(2)}) collective-permute-start(bf16[1152,128]{1,0:T(8,128)(2,1)} %get-tuple-element.144), channel_id=1, source_target_pairs={{0,16},{4,20},{8,24},{12,28},{16,0},{20,4},{24,8},{28,12},{1,17},{... | collective-permute-start | bytes 884744 | tf_op jit(solution)/shard_map/ppermute | solution.py:1138
  265.2 52.1 %collective-permute-start.46 = (bf16[1152,128]{1,0:T(8,128)(2,1)}, bf16[1152,128]{1,0:T(8,128)(2,1)}, u32[]{:S(2)}, u32[]{:S(2)}) collective-permute-start(bf16[1152,128]{1,0:T(8,128)(2,1)} %get-tuple-element.145), channel_id=1, source_target_pairs={{0,20},{4,16},{8,28},{12,24},{16,4},{20,0},{24,12},{28,8},{1,21},{... | collective-permute-start | bytes 884744 | tf_op jit(solution)/shard_map/ppermute | solution.py:1138
  282.0 35.4 %collective-permute-start.47 = (bf16[1152,128]{1,0:T(8,128)(2,1)}, bf16[1152,128]{1,0:T(8,128)(2,1)}, u32[]{:S(2)}, u32[]{:S(2)}) collective-permute-start(bf16[1152,128]{1,0:T(8,128)(2,1)} %get-tuple-element.146), channel_id=1, source_target_pairs={{0,24},{4,28},{8,16},{12,20},{16,8},{20,12},{24,0},{28,4},{1,25},{... | collective-permute-start | bytes 884744 | tf_op jit(solution)/shard_map/ppermute | solution.py:1138
  287.4 30.1 %collective-permute-start.48 = (bf16[1152,128]{1,0:T(8,128)(2,1)}, bf16[1152,128]{1,0:T(8,128)(2,1)}, u32[]{:S(2)}, u32[]{:S(2)}) collective-permute-start(bf16[1152,128]{1,0:T(8,128)(2,1)} %get-tuple-element.147), channel_id=1, source_target_pairs={{0,28},{4,24},{8,20},{12,16},{16,12},{20,8},{24,4},{28,0},{1,29},{... | collective-permute-start | bytes 884744 | tf_op jit(solution)/shard_map/ppermute | solution.py:1138
  318.5 23.0 %collective-permute-start.42 = (bf16[512,768]{1,0:T(8,128)(2,1)S(1)}, bf16[512,768]{1,0:T(8,128)(2,1)}, u32[]{:S(2)}, u32[]{:S(2)}) collective-permute-start(bf16[512,768]{1,0:T(8,128)(2,1)S(1)} %copy-done.10), channel_id=1, source_target_pairs={{0,2},{1,3},{2,0},{3,1},{4,6},{5,7},{6,4},{7,5},{8,10},{9,11},{10,... | collective-permute-start | bytes 2359304 | tf_op jit(solution)/shard_map/ppermute | solution.py:1161
  337.9 37.9 %all-to-all-start = ((bf16[8,112,640]{2,1,0:T(8,128)(2,1)}), bf16[8,112,640]{2,1,0:T(8,128)(2,1)S(1)}, u32[]{:S(2)}, u32[]{:S(2)}) async-start(bf16[8,112,640]{2,1,0:T(8,128)(2,1)} %head_grads.1), calls=%async_computation | async-start | bytes 2293760 | tf_op jit(solution)/shard_map/all_to_all | solution.py:1255
  353.2 25.8 %collective-permute-start.43 = (bf16[512,768]{1,0:T(8,128)(2,1)S(1)}, bf16[512,768]{1,0:T(8,128)(2,1)}, u32[]{:S(2)}, u32[]{:S(2)}) collective-permute-start(bf16[512,768]{1,0:T(8,128)(2,1)S(1)} %copy-done.10), channel_id=1, source_target_pairs={{0,1},{1,0},{2,3},{3,2},{4,5},{5,4},{6,7},{7,6},{8,9},{9,8},{10,11... | collective-permute-start | bytes 2359304 | tf_op jit(solution)/shard_map/ppermute | solution.py:1161
  353.3 25.7 %collective-permute-start.44 = (bf16[512,768]{1,0:T(8,128)(2,1)}, bf16[512,768]{1,0:T(8,128)(2,1)}, u32[]{:S(2)}, u32[]{:S(2)}) collective-permute-start(bf16[512,768]{1,0:T(8,128)(2,1)} %collective-permute-done.42.refs_1_), channel_id=1, source_target_pairs={{0,1},{1,0},{2,3},{3,2},{4,5},{5,4},{6,7},{7,6},{8,9},{9,8},{10,11... | collective-permute-start | bytes 2359304 | tf_op jit(solution)/shard_map/ppermute | solution.py:1161
  355.9 26.7 %collective-permute-start.54 = (bf16[512,768]{1,0:T(8,128)(2,1)S(1)}, bf16[512,768]{1,0:T(8,128)(2,1)}, u32[]{:S(2)}, u32[]{:S(2)}) collective-permute-start(bf16[512,768]{1,0:T(8,128)(2,1)S(1)} %add_convert_fusion.1), channel_id=1, source_target_pairs={{0,2},{1,3},{2,0},{3,1},{4,6},{5,7},{6,4},{7,5},{8,10},{9,11},{10,... | collective-permute-start | bytes 2359304 | tf_op jit(solution)/shard_map/ppermute | solution.py:1161
  356.7 35.8 %collective-permute-start.52 = (bf16[512,768]{1,0:T(8,128)(2,1)S(1)}, bf16[512,768]{1,0:T(8,128)(2,1)}, u32[]{:S(2)}, u32[]{:S(2)}) collective-permute-start(bf16[512,768]{1,0:T(8,128)(2,1)S(1)} %add_convert_fusion.3), channel_id=1, source_target_pairs={{0,2},{1,3},{2,0},{3,1},{4,6},{5,7},{6,4},{7,5},{8,10},{9,11},{10,... | collective-permute-start | bytes 2359304 | tf_op jit(solution)/shard_map/ppermute | solution.py:1161
  383.9 19.2 %collective-permute-start.56 = (bf16[512,768]{1,0:T(8,128)(2,1)S(1)}, bf16[512,768]{1,0:T(8,128)(2,1)S(1)}, u32[]{:S(2)}, u32[]{:S(2)}) collective-permute-start(bf16[512,768]{1,0:T(8,128)(2,1)S(1)} %add_convert_fusion.refs_1_), channel_id=1, source_target_pairs={{0,1},{1,0},{2,3},{3,2},{4,5},{5,4},{6,7},{7,6},{8,9},{9,8},{10,11... | collective-permute-start | bytes 2359304 | tf_op jit(solution)/shard_map/ppermute | solution.py:1161
  (75 other events, 740.7 us)
Sparse Core Ops, SparseCore 0:
  10.8 85.1 all-gather.1
  317.6 85.9 reduce-scatter.1

commit v2 on v1

--- a/solution.py
+++ b/solution.py
@@ -849,14 +849,22 @@
             low = lane_iota(256, att.shape[1]) % LANES < HEAD_DIM
             zero = jnp.zeros_like(att)
             both = jnp.concatenate([jnp.where(low, att, zero), jnp.where(low, zero, att)], axis=0)
-            put(slice(2 * D, 2 * D + att.shape[1]), tn(branch_ref[...], both))
+            part = tn(branch_ref[...], both)
+            planes = [part[:, k * LANES : (k + 1) * LANES] for k in range(part.shape[1] // LANES)]
+            planes = [plane + pltpu.roll(plane, HEAD_DIM, 1) for plane in planes]
+            if len(planes) % 2:
+                planes.append(jnp.zeros_like(planes[0]))
+            first = lane_iota(part.shape[0]) < HEAD_DIM
+            for k in range(0, len(planes), 2):
+                at = slice(2 * D + k // 2 * LANES, 2 * D + (k // 2 + 1) * LANES)
+                put(at, jnp.where(first, planes[k], planes[k + 1]))
 
 
 def weight_grads(places, saved, att, first, chunks, adds):
     act, pre, low, ffn_grad, branch_grad = saved
     rows = act.shape[0]
     width = att[0].shape[1]
-    total = 2 * D + width
+    total = 2 * D + -(-width // (2 * LANES)) * LANES
     cut = D // 2
 
     def chunk(s, i, q):
@@ -1073,19 +1081,17 @@
     inner_ref[...] = grad_ref[:, :D].astype(f32)
     outer_ref[...] = grad_ref[:, D : 2 * D].astype(f32)
     rest = grad_ref[:, 2 * D :].astype(f32)
-    planes = [rest[:, i * LANES : (i + 1) * LANES] for i in range(rest.shape[1] // LANES)]
-    folded = [p[:, :HEAD_DIM] + p[:, HEAD_DIM:] for p in planes]
-    output_ref[...] = jnp.concatenate(folded, axis=1).T
-
-
-def finish_middle(grads):
-    depth, total = grads.shape
+    output_ref[...] = rest[:, : output_ref.shape[0]].T
+
+
+def finish_middle(grads, width):
+    depth = grads.shape[0]
     return pl.pallas_call(
         finish_middle_kernel,
         out_shape=[
             jax.ShapeDtypeStruct((depth, D), f32),
             jax.ShapeDtypeStruct((depth, D), f32),
-            jax.ShapeDtypeStruct(((total - 2 * D) // 2, depth), f32),
+            jax.ShapeDtypeStruct((width, depth), f32),
         ],
         name="finish_middle",
         cost_estimate=QUICK,
@@ -1257,8 +1263,8 @@
     else:
         ends = reduce_heads(terms, vec, depth, width)
     small = ends[3] + swap(ends[3], 1)
+    chips[1] = after(chips[1], small, hidden_out)
     small = finish_vectors(small, swap(small, 2), depth)
-    chips[1] = after(chips[1], ends[0], hidden_out)
     ready = [
         (chip.astype(f32) + part.astype(f32)).astype(bf16) for chip, part in zip(chips, others)
     ]
@@ -1269,7 +1275,7 @@
         ready + [swap(part, 1) for part in ready],
     )
 
-    grad_inner, grad_outer, grad_output = finish_middle(reduced)
+    grad_inner, grad_outer, grad_output = finish_middle(reduced, width)
     return (
         hidden_out,
         grad_hidden,

time: 419 us -> 413 us (0.986)
  waiting for transfers between devices: 136 us -> 130 us
    ppermute x22, waiting for transfers between devices: 39.1 us -> 32.4 us  [swap(): return lax.ppermute(rows, 'mp', [(i, i ^ flip) for i in range(4)])]
    unnamed x94 -> x98, local copies, waits for them, and re-layouts: 13.3 us -> 13.8 us
  transfers between devices with their start and end apart: 60 -> 60, of which waited for: 23 -> 24; matrix products, arithmetic and copies ran while one was open for 2% -> 2% of each run, Pallas kernels for 27% -> 28%
where the time goes in v2:
time: 413 us; the launch traced here: 412 us
  Pallas kernels  146 us (35%)
  waiting for transfers between devices  130 us (31%)
  starting transfers between devices  96.3 us (23%)
  local copies, waits for them, and re-layouts  17.9 us (4%)
  between operations  14.5 us (4%)
  other arithmetic  7.26 us (2%)
    ppermute x28, starting transfers between devices, over_rows(): out.append(lax.ppermute(rows, 'dp', [(i, i ^ s) for i in range(lay.peers)]))  66.6 us
    ppermute x28, waiting for transfers between devices, over_rows(): out.append(lax.ppermute(rows, 'dp', [(i, i ^ s) for i in range(lay.peers)]))  60.2 us
    ppermute x22, waiting for transfers between devices, swap(): return lax.ppermute(rows, 'mp', [(i, i ^ flip) for i in range(4)])  32.4 us
    pallas_call x1, Pallas kernels, middle(): pl.pallas_call(middle_kernel, grid_spec=spec, out_shape=[jax.ShapeDtypeSt...  28.7 us
    pallas_call x3, Pallas kernels, weight_grads(): pl.pallas_call(partial(weight_grad_kernel, chunks, len(adds)), grid_spec=...  23.9 us
    ppermute x7, waiting for transfers between devices, flip(): return lax.ppermute(rows, 'dp', [(i, i ^ s) for i in range(lay.peers)])  20 us
    all_to_all x1, waiting for transfers between devices, on_device(): terms = lax.all_to_all(terms, 'dp', split_axis=0, concat_axis=0, tiled=True)  17.1 us
    pallas_call x1, Pallas kernels, project_rows(): pl.pallas_call(partial(project_kernel, lay, steps), grid_spec=spec, out_s...  15.1 us
  transfers between devices with their start and end apart: 60, of which 24 were waited for; matrix products, arithmetic and copies ran while one was open for 2% of the time, Pallas kernels for 28%

profile of v2, /device:TPU:0, one launch (start us, length us, event | category | flops | bytes accessed | tf_op | source)
XLA Modules:
  0.0 412.1 jit_solution(7242981876120468765)
XLA Ops:
  10.6 4.1 collective-permute-start.3
  18.2 3.8 collective-permute-done.3.refs_4_
  28.7 4.4 %collective-permute-done.2.refs_3_ = bf16[96,768]{1,0:T(8,128)(2,1)S(1)} collective-permute-done((bf16[96,768]{1,0:T(8,128)(2,1)}, bf16[96,768]{1,0:T(8,128)(2,1)S(1)}, u32[]{:S(2)}, u32[]{:S(2)}) %collective-permute-start.2) | collective-permute-done | bytes 147488 | tf_op jit(solution)/shard_map/ppermute | solution.py:1154
  33.2 8.3 %collective-permute-done.5.refs_6_ = bf16[96,768]{1,0:T(8,128)(2,1)S(1)} collective-permute-done((bf16[96,768]{1,0:T(8,128)(2,1)S(1)}, bf16[96,768]{1,0:T(8,128)(2,1)S(1)}, u32[]{:S(2)}, u32[]{:S(2)}) %collective-permute-start.5) | collective-permute-done | bytes 147488 | tf_op jit(solution)/shard_map/ppermute | solution.py:1154
  48.2 15.1 %project_rows.1 = (bf16[1168,128]{1,0:T(8,128)(2,1)}, bf16[1168,128]{1,0:T(8,128)(2,1)}, bf16[1168,128]{1,0:T(8,128)(2,1)}, bf16[1168,128]{1,0:T(8,128)(2,1)}, b...) custom-call(s32[2]{0:T(128)} %pad_add_fusion.1.place_ref, ...), custom_call_target="tpu_custom_call" | custom-call | flops 1000000 | bytes 3000 | tf_op jit(solution)/shard_map/project_rows/pallas_call | solution.py:288
  70.7 17.3 %collective-permute-done.8.refs_2_.refs_10_ = bf16[1168,128]{1,0:T(8,128)(2,1)S(1)} collective-permute-done((bf16[1168,128]{1,0:T(8,128)(2,1)}, bf16[1168,128]{1,0:T(8,128)(2,1)S(1)}, u32[]{:S(2)}, u32[]{:S(2)}) %collective-permute-start.8) | collective-permute-done | bytes 299040 | tf_op jit(solution)/shard_map/ppermute | solution.py:1144
  98.5 5.5 %collective-permute-done.11.refs_5_.refs_13_ = bf16[1168,128]{1,0:T(8,128)(2,1)S(1)} collective-permute-done((bf16[1168,128]{1,0:T(8,128)(2,1)}, bf16[1168,128]{1,0:T(8,128)(2,1)S(1)}, u32[]{:S(2)}, u32[]{:S(2)}) %collective-permute-start.11) | collective-permute-done | bytes 299040 | tf_op jit(solution)/shard_map/ppermute | solution.py:1144
  104.0 6.8 %collective-permute-done.13.refs_7_.refs_15_ = bf16[1168,128]{1,0:T(8,128)(2,1)S(1)} collective-permute-done((bf16[1168,128]{1,0:T(8,128)(2,1)}, bf16[1168,128]{1,0:T(8,128)(2,1)S(1)}, u32[]{:S(2)}, u32[]{:S(2)}) %collective-permute-start.13) | collective-permute-done | bytes 299040 | tf_op jit(solution)/shard_map/ppermute | solution.py:1144
  110.8 5.0 %collective-permute-done.12.refs_6_.refs_14_ = bf16[1168,128]{1,0:T(8,128)(2,1)S(1)} collective-permute-done((bf16[1168,128]{1,0:T(8,128)(2,1)}, bf16[1168,128]{1,0:T(8,128)(2,1)S(1)}, u32[]{:S(2)}, u32[]{:S(2)}) %collective-permute-start.12) | collective-permute-done | bytes 299040 | tf_op jit(solution)/shard_map/ppermute | solution.py:1144
  116.6 5.2 %attend.1 = (bf16[384,128]{1,0:T(8,128)(2,1)}, bf16[384,128]{1,0:T(8,128)(2,1)}, bf16[384,128]{1,0:T(8,128)(2,1)}, bf16[384,128]{1,0:T(8,128)(2,1)}, bf16[384,12...) custom-call(bf16[1168,128]{1,0:T(8,128)(2,1)} %get-tuple-element.94.refs_0_.refs_, ...), custom_call_target="tpu_custom_call" | custom-call | flops 46000001024 | bytes 138000000 | tf_op jit(solution)/shard_map/attend/pallas_call | solution.py:363
  124.6 10.5 %collective-permute-start.15 = (bf16[384,128]{1,0:T(8,128)(2,1)}, bf16[384,128]{1,0:T(8,128)(2,1)S(1)}, u32[]{:S(2)}, u32[]{:S(2)}) collective-permute-start(bf16[384,128]{1,0:T(8,128)(2,1)} %get-tuple-element.106), channel_id=1, source_target_pairs={{0,8},{4,12},{8,0},{12,4},{16,24},{20,28},{24,16},{28,20},{1,9},{5... | collective-permute-start | bytes 294920 | tf_op jit(solution)/shard_map/ppermute | solution.py:1144
  145.0 5.4 %collective-permute-done.17.refs_4_ = bf16[384,128]{1,0:T(8,128)(2,1)S(1)} collective-permute-done((bf16[384,128]{1,0:T(8,128)(2,1)}, bf16[384,128]{1,0:T(8,128)(2,1)S(1)}, u32[]{:S(2)}, u32[]{:S(2)}) %collective-permute-start.17) | collective-permute-done | bytes 98336 | tf_op jit(solution)/shard_map/ppermute | solution.py:1144
  153.3 6.6 %unsort_rows.1 = (bf16[256,384]{1,0:T(8,128)(2,1)}, bf16[256,384]{1,0:T(8,128)(2,1)}, bf16[256,384]{1,0:T(8,128)(2,1)}, bf16[256,384]{1,0:T(8,128)(2,1)}) custom-call(s32[2]{0:T(128)} %pad_add_fusion.1.place_ref, bf16[384,128]{1,0:T(8,128)(2,1)} %get-tuple-element.104.refs_0_, bf16[384,128]{1,0:T(8,128)(2,1)} %copy-done.23, bf16[384,128]{1,0:T(8,128)(2,1)} %copy-done.24, ...), custom_call_target="tpu_custom_call" | custom-call | flops 1000000 | bytes 3000 | tf_op jit(solution)/shard_map/unsort_rows/pallas_call | solution.py:448
  162.3 7.7 %collective-permute-done.21.att1.refs_1_ = bf16[256,384]{1,0:T(8,128)(2,1)S(1)} collective-permute-done((bf16[256,384]{1,0:T(8,128)(2,1)}, bf16[256,384]{1,0:T(8,128)(2,1)S(1)}, u32[]{:S(2)}, u32[]{:S(2)}) %collective-permute-start.21) | collective-permute-done | bytes 196640 | tf_op jit(solution)/shard_map/ppermute | solution.py:1167
  175.1 28.7 %middle.1 = (bf16[512,768]{1,0:T(8,128)(2,1)}, bf16[512,3072]{1,0:T(8,128)(2,1)}, bf16[512,3072]{1,0:T(8,128)(2,1)}, bf16[512,768]{1,0:T(8,128)(2,1)}, bf16[512,...) custom-call(s32[2]{0:T(128)} %pad_add_fusion.1.place_ref, ...), custom_call_target="tpu_custom_call" | custom-call | flops 1000000 | bytes 3000 | tf_op jit(solution)/shard_map/middle/pallas_call | solution.py:813
  205.8 10.0 %weight_grads.3 = bf16[1536,1792]{1,0:T(8,128)(2,1)} custom-call(s32[2]{0:T(128)} %pad_add_fusion.1.place_ref, bf16[512,3072]{1,0:T(8,128)(2,1)} %get-tuple-element.141.act_ref, bf16[512,3072]{1,0:T(8,128)(2,1)} %get-tuple-element.137.pre_ref, bf16[512,768]{1,0:T(8,128)(2,1)} %get-tuple-element.138.low_ref, bf16[512,768]{1,0:T(8,128)(2,1)} %get-tuple-element.139.ffn_ref, ...), custom_call_target="tpu_custom_call" | custom-call | flops 1000000 | bytes 3000 | tf_op jit(solution)/shard_map/weight_grads/pallas_call | solution.py:883
  217.2 7.4 %sort_rows.1 = (bf16[384,128]{1,0:T(8,128)(2,1)}, bf16[384,128]{1,0:T(8,128)(2,1)}, bf16[384,128]{1,0:T(8,128)(2,1)}, bf16[384,128]{1,0:T(8,128)(2,1)}, bf16[384...) custom-call(s32[2]{0:T(128)} %pad_add_fusion.1.place_ref, ...), custom_call_target="tpu_custom_call" | custom-call | flops 80000000000 | bytes 240000000 | tf_op jit(solution)/shard_map/sort_rows/pallas_call | solution.py:487
  237.7 6.5 %weight_grads.4 = bf16[768,1792]{1,0:T(8,128)(2,1)} custom-call(s32[2]{0:T(128)} %pad_add_fusion.1.place_ref, bf16[512,3072]{1,0:T(8,128)(2,1)} %get-tuple-element.141.act_ref, bf16[512,3072]{1,0:T(8,128)(2,1)} %get-tuple-element.137.pre_ref, bf16[512,768]{1,0:T(8,128)(2,1)} %get-tuple-element.138.low_ref, bf16[512,768]{1,0:T(8,128)(2,1)} %get-tuple-element.139.ffn_ref, ...), custom_call_target="tpu_custom_call" | custom-call | flops 1000000 | bytes 3000 | tf_op jit(solution)/shard_map/weight_grads/pallas_call | solution.py:883
  247.1 10.6 %attend_back.1 = (bf16[1152,128]{1,0:T(8,128)(2,1)}, bf16[1152,128]{1,0:T(8,128)(2,1)}, bf16[1152,128]{1,0:T(8,128)(2,1)}, bf16[1152,128]{1,0:T(8,128)(2,1)}, bf...) custom-call(bf16[1168,128]{1,0:T(8,128)(2,1)} %get-tuple-element.94., ...), custom_call_target="tpu_custom_call" | custom-call | flops 40000000000 | bytes 120000000 | tf_op jit(solution)/shard_map/attend_back/pallas_call | solution.py:404
  265.5 6.3 %collective-permute-start.46 = (bf16[1152,128]{1,0:T(8,128)(2,1)}, bf16[1152,128]{1,0:T(8,128)(2,1)}, u32[]{:S(2)}, u32[]{:S(2)}) collective-permute-start(bf16[1152,128]{1,0:T(8,128)(2,1)} %get-tuple-element.145), channel_id=1, source_target_pairs={{0,20},{4,16},{8,28},{12,24},{16,4},{20,0},{24,12},{28,8},{1,21},{... | collective-permute-start | bytes 884744 | tf_op jit(solution)/shard_map/ppermute | solution.py:1144
  271.8 10.1 %collective-permute-done.38.refs_2_ = bf16[1152,128]{1,0:T(8,128)(2,1)S(1)} collective-permute-done((bf16[1152,128]{1,0:T(8,128)(2,1)}, bf16[1152,128]{1,0:T(8,128)(2,1)S(1)}, u32[]{:S(2)}, u32[]{:S(2)}) %collective-permute-start.38) | collective-permute-done | bytes 294944 | tf_op jit(solution)/shard_map/ppermute | solution.py:1144
  283.8 3.5 collective-permute-done.39.refs_3_
  291.6 12.8 %collective-permute-done.41.refs_2_ = bf16[768,1792]{1,0:T(8,128)(2,1)S(1)} collective-permute-done((bf16[768,1792]{1,0:T(8,128)(2,1)}, bf16[768,1792]{1,0:T(8,128)(2,1)S(1)}, u32[]{:S(2)}, u32[]{:S(2)}) %collective-permute-start.41) | collective-permute-done | bytes 2752544 | tf_op jit(solution)/shard_map/ppermute | solution.py:1167
  305.9 7.4 %weight_grads.5 = bf16[768,1792]{1,0:T(8,128)(2,1)} custom-call(s32[2]{0:T(128)} %pad_add_fusion.1.place_ref, bf16[512,3072]{1,0:T(8,128)(2,1)} %get-tuple-element.141.act_ref, bf16[512,3072]{1,0:T(8,128)(2,1)} %get-tuple-element.137.pre_ref, bf16[512,768]{1,0:T(8,128)(2,1)} %get-tuple-element.138.low_ref, bf16[512,768]{1,0:T(8,128)(2,1)} %get-tuple-element.139.ffn_ref, ...), custom_call_target="tpu_custom_call" | custom-call | flops 1000000 | bytes 3000 | tf_op jit(solution)/shard_map/weight_grads/pallas_call | solution.py:883
  316.1 10.9 %collect.1.dense_ref = bf16[2048,640]{1,0:T(8,128)(2,1)} custom-call(s32[2]{0:T(128)} %pad_add_fusion.1.place_ref, bf16[1152,128]{1,0:T(8,128)(2,1)} %get-tuple-element.143.refs_0_, bf16[1152,128]{1,0:T(8,128)(2,1)} %copy-done.38, bf16[1152,128]{1,0:T(8,128)(2,1)} %copy-done.39, bf16[1152,128]{1,0:T(8,128)(2,1)} %collective-permute-done.39.refs_3_, ...), custom_call_target="tpu_custom_call" | custom-call | flops 30000001024 | bytes 90000000 | tf_op jit(solution)/shard_map/collect/pallas_call | solution.py:932
  326.9 7.0 %head_grads.1 = bf16[8,112,640]{2,1,0:T(8,128)(2,1)} custom-call(s32[2]{0:T(128)} %pad_add_fusion.1.place_ref, bf16[2048,768]{1,0:T(8,128)(2,1)} %x_ref.3, bf16[2048,640]{1,0:T(8,128)(2,1)} %collect.1.dense_ref, f32[8,16,128]{2,1,0:T(8,128)} %select_maximum_fusion.vec_ref), custom_call_target="tpu_custom_call" | custom-call | flops 4000000000 | bytes 12000000 | tf_op jit(solution)/shard_map/head_grads/pallas_call | solution.py:1027
  334.0 4.6 %all-to-all-start = ((bf16[8,112,640]{2,1,0:T(8,128)(2,1)}), bf16[8,112,640]{2,1,0:T(8,128)(2,1)S(1)}, u32[]{:S(2)}, u32[]{:S(2)}) async-start(bf16[8,112,640]{2,1,0:T(8,128)(2,1)} %head_grads.1), calls=%async_computation | async-start | bytes 2293760 | tf_op jit(solution)/shard_map/all_to_all | solution.py:1261
  338.6 5.6 %spread_grads.3 = (bf16[512,768]{1,0:T(8,128)(2,1)}, bf16[512,768]{1,0:T(8,128)(2,1)}) custom-call(s32[2]{0:T(128)} %pad_add_fusion.1.place_ref, bf16[2048,640]{1,0:T(8,128)(2,1)} %collect.1.dense_ref, bf16[768,640]{1,0:T(8,128)(2,1)} %get-tuple-element.92.w_ref, f32[512,768]{1,0:T(8,128)} %get-tuple-element.154.h1_ref), custom_call_target="tpu_custom_call" | custom-call | flops 3000000000 | bytes 9000000 | tf_op jit(solution)/shard_map/spread_grads/pallas_call | solution.py:974
  344.2 5.7 %spread_grads.2 = (bf16[512,768]{1,0:T(8,128)(2,1)}, bf16[512,768]{1,0:T(8,128)(2,1)}) custom-call(s32[2]{0:T(128)} %pad_add_fusion.1.place_ref, bf16[2048,640]{1,0:T(8,128)(2,1)} %collect.1.dense_ref, bf16[768,640]{1,0:T(8,128)(2,1)} %get-tuple-element.92.w_ref, f32[512,768]{1,0:T(8,128)} %get-tuple-element.154.h1_ref), custom_call_target="tpu_custom_call" | custom-call | flops 3000000000 | bytes 9000000 | tf_op jit(solution)/shard_map/spread_grads/pallas_call | solution.py:974
  355.3 17.1 %all-to-all-done.refs_0_ = bf16[8,112,640]{2,1,0:T(8,128)(2,1)S(1)} async-done(((bf16[8,112,640]{2,1,0:T(8,128)(2,1)}), bf16[8,112,640]{2,1,0:T(8,128)(2,1)S(1)}, u32[]{:S(2)}, u32[]{:S(2)}) %all-to-all-start) | async-done | bytes 1146912 | tf_op jit(solution)/shard_map/all_to_all | solution.py:1261
  377.6 3.5 order_quarters.2
  382.7 6.9 %collective-permute-done.52 = bf16[512,768]{1,0:T(8,128)(2,1)} collective-permute-done((bf16[512,768]{1,0:T(8,128)(2,1)S(1)}, bf16[512,768]{1,0:T(8,128)(2,1)}, u32[]{:S(2)}, u32[]{:S(2)}) %collective-permute-start.52) | collective-permute-done | bytes 786464 | tf_op jit(solution)/shard_map/ppermute | solution.py:1167
  (231 shorter events, 126.9 us)
Async XLA Ops:
  7.2 89.4 %all-gather.2.cloned.1.call-start = ((), (), s32[]{:S(2)}) async-start(), calls=%async_computation.2 | async-start | bytes 3317760 | tf_op jit(solution)/shard_map/all_gather | solution.py:1206
  10.5 392.9 %reduce-scatter.2.cloned.1.call-start = ((), (), s32[]{:S(2)}) async-start(), calls=%async_computation.3 | async-start | bytes 3096576 | tf_op jit(solution)/shard_map/reduce_scatter | solution.py:1246
  17.8 15.4 %collective-permute-start.2 = (bf16[96,768]{1,0:T(8,128)(2,1)}, bf16[96,768]{1,0:T(8,128)(2,1)S(1)}, u32[]{:S(2)}, u32[]{:S(2)}) collective-permute-start(bf16[96,768]{1,0:T(8,128)(2,1)} %get-tuple-element.91.refs_0_), channel_id=1, source_target_pairs={{0,12},{4,8},{8,4},{12,0},{16,28},{20,24},{24,20},{28,16},{1,13},{... | collective-permute-start | bytes 442376 | tf_op jit(solution)/shard_map/ppermute | solution.py:1154
  23.6 17.9 %collective-permute-start.5 = (bf16[96,768]{1,0:T(8,128)(2,1)S(1)}, bf16[96,768]{1,0:T(8,128)(2,1)S(1)}, u32[]{:S(2)}, u32[]{:S(2)}) collective-permute-start(bf16[96,768]{1,0:T(8,128)(2,1)S(1)} %collective-permute-done.3.refs_4_), channel_id=1, source_target_pairs={{0,8},{4,12},{8,0},{12,4},{16,24},{20,28},{24,16},{28,20},{1,9},{5... | collective-permute-start | bytes 442376 | tf_op jit(solution)/shard_map/ppermute | solution.py:1154
  24.3 20.5 %collective-permute-start.6 = (bf16[96,768]{1,0:T(8,128)(2,1)S(1)}, bf16[96,768]{1,0:T(8,128)(2,1)S(1)}, u32[]{:S(2)}, u32[]{:S(2)}) collective-permute-start(bf16[96,768]{1,0:T(8,128)(2,1)S(1)} %collective-permute-done.3.refs_4_), channel_id=1, source_target_pairs={{0,12},{4,8},{8,4},{12,0},{16,28},{20,24},{24,20},{28,16},{1,13},{... | collective-permute-start | bytes 442376 | tf_op jit(solution)/shard_map/ppermute | solution.py:1154
  63.3 24.7 %collective-permute-start.8 = (bf16[1168,128]{1,0:T(8,128)(2,1)}, bf16[1168,128]{1,0:T(8,128)(2,1)S(1)}, u32[]{:S(2)}, u32[]{:S(2)}) collective-permute-start(bf16[1168,128]{1,0:T(8,128)(2,1)} %get-tuple-element.96), channel_id=1, source_target_pairs={{0,8},{4,12},{8,0},{12,4},{16,24},{20,28},{24,16},{28,20},{1,9},{5... | collective-permute-start | bytes 897032 | tf_op jit(solution)/shard_map/ppermute | solution.py:1144
  63.3 27.9 %collective-permute-start.7 = (bf16[1168,128]{1,0:T(8,128)(2,1)}, bf16[1168,128]{1,0:T(8,128)(2,1)S(1)}, u32[]{:S(2)}, u32[]{:S(2)}) collective-permute-start(bf16[1168,128]{1,0:T(8,128)(2,1)} %get-tuple-element.95), channel_id=1, source_target_pairs={{0,4},{4,0},{8,12},{12,8},{16,20},{20,16},{24,28},{28,24},{1,5},{5... | collective-permute-start | bytes 897032 | tf_op jit(solution)/shard_map/ppermute | solution.py:1144
  64.9 31.6 %collective-permute-start.10 = (bf16[1168,128]{1,0:T(8,128)(2,1)}, bf16[1168,128]{1,0:T(8,128)(2,1)}, u32[]{:S(2)}, u32[]{:S(2)}) collective-permute-start(bf16[1168,128]{1,0:T(8,128)(2,1)} %get-tuple-element.98), channel_id=1, source_target_pairs={{0,16},{4,20},{8,24},{12,28},{16,0},{20,4},{24,8},{28,12},{1,17},{... | collective-permute-start | bytes 897032 | tf_op jit(solution)/shard_map/ppermute | solution.py:1144
  67.7 36.3 %collective-permute-start.11 = (bf16[1168,128]{1,0:T(8,128)(2,1)}, bf16[1168,128]{1,0:T(8,128)(2,1)S(1)}, u32[]{:S(2)}, u32[]{:S(2)}) collective-permute-start(bf16[1168,128]{1,0:T(8,128)(2,1)} %get-tuple-element.99), channel_id=1, source_target_pairs={{0,20},{4,16},{8,28},{12,24},{16,4},{20,0},{24,12},{28,8},{1,21},{... | collective-permute-start | bytes 897032 | tf_op jit(solution)/shard_map/ppermute | solution.py:1144
  67.7 36.3 %collective-permute-start.9 = (bf16[1168,128]{1,0:T(8,128)(2,1)}, bf16[1168,128]{1,0:T(8,128)(2,1)S(1)}, u32[]{:S(2)}, u32[]{:S(2)}) collective-permute-start(bf16[1168,128]{1,0:T(8,128)(2,1)} %get-tuple-element.97), channel_id=1, source_target_pairs={{0,12},{4,8},{8,4},{12,0},{16,28},{20,24},{24,20},{28,16},{1,13},{... | collective-permute-start | bytes 897032 | tf_op jit(solution)/shard_map/ppermute | solution.py:1144
  88.0 22.8 %collective-permute-start.13 = (bf16[1168,128]{1,0:T(8,128)(2,1)}, bf16[1168,128]{1,0:T(8,128)(2,1)S(1)}, u32[]{:S(2)}, u32[]{:S(2)}) collective-permute-start(bf16[1168,128]{1,0:T(8,128)(2,1)} %get-tuple-element.103), channel_id=1, source_target_pairs={{0,28},{4,24},{8,20},{12,16},{16,12},{20,8},{24,4},{28,0},{1,29},{... | collective-permute-start | bytes 897032 | tf_op jit(solution)/shard_map/ppermute | solution.py:1144
  91.2 24.7 %collective-permute-start.12 = (bf16[1168,128]{1,0:T(8,128)(2,1)}, bf16[1168,128]{1,0:T(8,128)(2,1)S(1)}, u32[]{:S(2)}, u32[]{:S(2)}) collective-permute-start(bf16[1168,128]{1,0:T(8,128)(2,1)} %get-tuple-element.101), channel_id=1, source_target_pairs={{0,24},{4,28},{8,16},{12,20},{16,8},{20,12},{24,0},{28,4},{1,25},{... | collective-permute-start | bytes 897032 | tf_op jit(solution)/shard_map/ppermute | solution.py:1144
  96.6 63.4 %collective-permute-start.25 = (bf16[768,1920]{1,0:T(8,128)(2,1)}, bf16[768,1920]{1,0:T(8,128)(2,1)}, u32[]{:S(2)}, u32[]{:S(2)}) collective-permute-start(bf16[768,1920]{1,0:T(8,128)(2,1)} %all-gather.2.cloned.1.call-done.w0), channel_id=1, source_target_pairs={{0,2},{1,3},{2,0},{3,1},{4,6},{5,7},{6,4},{7,5},{8,10},{9,11},{10,... | collective-permute-start | bytes 8847368 | tf_op jit(solution)/shard_map/ppermute | solution.py:1167
  121.8 15.9 %collective-permute-start.14 = (bf16[384,128]{1,0:T(8,128)(2,1)}, bf16[384,128]{1,0:T(8,128)(2,1)S(1)}, u32[]{:S(2)}, u32[]{:S(2)}) collective-permute-start(bf16[384,128]{1,0:T(8,128)(2,1)} %get-tuple-element.105), channel_id=1, source_target_pairs={{0,4},{4,0},{8,12},{12,8},{16,20},{20,16},{24,28},{28,24},{1,5},{5... | collective-permute-start | bytes 294920 | tf_op jit(solution)/shard_map/ppermute | solution.py:1144
  124.6 15.7 %collective-permute-start.15 = (bf16[384,128]{1,0:T(8,128)(2,1)}, bf16[384,128]{1,0:T(8,128)(2,1)S(1)}, u32[]{:S(2)}, u32[]{:S(2)}) collective-permute-start(bf16[384,128]{1,0:T(8,128)(2,1)} %get-tuple-element.106), channel_id=1, source_target_pairs={{0,8},{4,12},{8,0},{12,4},{16,24},{20,28},{24,16},{28,20},{1,9},{5... | collective-permute-start | bytes 294920 | tf_op jit(solution)/shard_map/ppermute | solution.py:1144
  215.8 19.4 %collective-permute-start.40 = (bf16[1536,1792]{1,0:T(8,128)(2,1)}, bf16[1536,1792]{1,0:T(8,128)(2,1)}, u32[]{:S(2)}, u32[]{:S(2)}) collective-permute-start(bf16[1536,1792]{1,0:T(8,128)(2,1)} %weight_grads.3), channel_id=1, source_target_pairs={{0,1},{1,0},{2,3},{3,2},{4,5},{5,4},{6,7},{7,6},{8,9},{9,8},{10,11... | collective-permute-start | bytes 16515080 | tf_op jit(solution)/shard_map/ppermute | solution.py:1167
  228.5 15.7 %collective-permute-start.32 = (bf16[384,128]{1,0:T(8,128)(2,1)}, bf16[384,128]{1,0:T(8,128)(2,1)S(1)}, u32[]{:S(2)}, u32[]{:S(2)}) collective-permute-start(bf16[384,128]{1,0:T(8,128)(2,1)} %get-tuple-element.128), channel_id=1, source_target_pairs={{0,12},{4,8},{8,4},{12,0},{16,28},{20,24},{24,20},{28,16},{1,13},{... | collective-permute-start | bytes 294920 | tf_op jit(solution)/shard_map/ppermute | solution.py:1144
  228.7 17.1 %collective-permute-start.33 = (bf16[384,128]{1,0:T(8,128)(2,1)}, bf16[384,128]{1,0:T(8,128)(2,1)S(1)}, u32[]{:S(2)}, u32[]{:S(2)}) collective-permute-start(bf16[384,128]{1,0:T(8,128)(2,1)} %get-tuple-element.129), channel_id=1, source_target_pairs={{0,16},{4,20},{8,24},{12,28},{16,0},{20,4},{24,8},{28,12},{1,17},{... | collective-permute-start | bytes 294920 | tf_op jit(solution)/shard_map/ppermute | solution.py:1144
  244.2 60.2 %collective-permute-start.41 = (bf16[768,1792]{1,0:T(8,128)(2,1)}, bf16[768,1792]{1,0:T(8,128)(2,1)S(1)}, u32[]{:S(2)}, u32[]{:S(2)}) collective-permute-start(bf16[768,1792]{1,0:T(8,128)(2,1)} %weight_grads.4), channel_id=1, source_target_pairs={{0,2},{1,3},{2,0},{3,1},{4,6},{5,7},{6,4},{7,5},{8,10},{9,11},{10,... | collective-permute-start | bytes 8257544 | tf_op jit(solution)/shard_map/ppermute | solution.py:1167
  258.7 23.2 %collective-permute-start.38 = (bf16[1152,128]{1,0:T(8,128)(2,1)}, bf16[1152,128]{1,0:T(8,128)(2,1)S(1)}, u32[]{:S(2)}, u32[]{:S(2)}) collective-permute-start(bf16[1152,128]{1,0:T(8,128)(2,1)} %get-tuple-element.134), channel_id=1, source_target_pairs={{0,8},{4,12},{8,0},{12,4},{16,24},{20,28},{24,16},{28,20},{1,9},{5... | collective-permute-start | bytes 884744 | tf_op jit(solution)/shard_map/ppermute | solution.py:1144
  262.1 25.3 %collective-permute-start.39 = (bf16[1152,128]{1,0:T(8,128)(2,1)}, bf16[1152,128]{1,0:T(8,128)(2,1)}, u32[]{:S(2)}, u32[]{:S(2)}) collective-permute-start(bf16[1152,128]{1,0:T(8,128)(2,1)} %get-tuple-element.135), channel_id=1, source_target_pairs={{0,12},{4,8},{8,4},{12,0},{16,28},{20,24},{24,20},{28,16},{1,13},{... | collective-permute-start | bytes 884744 | tf_op jit(solution)/shard_map/ppermute | solution.py:1144
  262.8 50.6 %collective-permute-start.45 = (bf16[1152,128]{1,0:T(8,128)(2,1)}, bf16[1152,128]{1,0:T(8,128)(2,1)}, u32[]{:S(2)}, u32[]{:S(2)}) collective-permute-start(bf16[1152,128]{1,0:T(8,128)(2,1)} %get-tuple-element.144), channel_id=1, source_target_pairs={{0,16},{4,20},{8,24},{12,28},{16,0},{20,4},{24,8},{28,12},{1,17},{... | collective-permute-start | bytes 884744 | tf_op jit(solution)/shard_map/ppermute | solution.py:1144
  265.5 47.9 %collective-permute-start.46 = (bf16[1152,128]{1,0:T(8,128)(2,1)}, bf16[1152,128]{1,0:T(8,128)(2,1)}, u32[]{:S(2)}, u32[]{:S(2)}) collective-permute-start(bf16[1152,128]{1,0:T(8,128)(2,1)} %get-tuple-element.145), channel_id=1, source_target_pairs={{0,20},{4,16},{8,28},{12,24},{16,4},{20,0},{24,12},{28,8},{1,21},{... | collective-permute-start | bytes 884744 | tf_op jit(solution)/shard_map/ppermute | solution.py:1144
  281.9 31.5 %collective-permute-start.47 = (bf16[1152,128]{1,0:T(8,128)(2,1)}, bf16[1152,128]{1,0:T(8,128)(2,1)}, u32[]{:S(2)}, u32[]{:S(2)}) collective-permute-start(bf16[1152,128]{1,0:T(8,128)(2,1)} %get-tuple-element.146), channel_id=1, source_target_pairs={{0,24},{4,28},{8,16},{12,20},{16,8},{20,12},{24,0},{28,4},{1,25},{... | collective-permute-start | bytes 884744 | tf_op jit(solution)/shard_map/ppermute | solution.py:1144
  287.4 26.1 %collective-permute-start.48 = (bf16[1152,128]{1,0:T(8,128)(2,1)}, bf16[1152,128]{1,0:T(8,128)(2,1)}, u32[]{:S(2)}, u32[]{:S(2)}) collective-permute-start(bf16[1152,128]{1,0:T(8,128)(2,1)} %get-tuple-element.147), channel_id=1, source_target_pairs={{0,28},{4,24},{8,20},{12,16},{16,12},{20,8},{24,4},{28,0},{1,29},{... | collective-permute-start | bytes 884744 | tf_op jit(solution)/shard_map/ppermute | solution.py:1144
  314.5 24.1 %collective-permute-start.42 = (bf16[512,768]{1,0:T(8,128)(2,1)S(1)}, bf16[512,768]{1,0:T(8,128)(2,1)}, u32[]{:S(2)}, u32[]{:S(2)}) collective-permute-start(bf16[512,768]{1,0:T(8,128)(2,1)S(1)} %copy-done.10), channel_id=1, source_target_pairs={{0,2},{1,3},{2,0},{3,1},{4,6},{5,7},{6,4},{7,5},{8,10},{9,11},{10,... | collective-permute-start | bytes 2359304 | tf_op jit(solution)/shard_map/ppermute | solution.py:1167
  334.0 38.4 %all-to-all-start = ((bf16[8,112,640]{2,1,0:T(8,128)(2,1)}), bf16[8,112,640]{2,1,0:T(8,128)(2,1)S(1)}, u32[]{:S(2)}, u32[]{:S(2)}) async-start(bf16[8,112,640]{2,1,0:T(8,128)(2,1)} %head_grads.1), calls=%async_computation | async-start | bytes 2293760 | tf_op jit(solution)/shard_map/all_to_all | solution.py:1261
  350.3 27.4 %collective-permute-start.43 = (bf16[512,768]{1,0:T(8,128)(2,1)S(1)}, bf16[512,768]{1,0:T(8,128)(2,1)}, u32[]{:S(2)}, u32[]{:S(2)}) collective-permute-start(bf16[512,768]{1,0:T(8,128)(2,1)S(1)} %copy-done.10), channel_id=1, source_target_pairs={{0,1},{1,0},{2,3},{3,2},{4,5},{5,4},{6,7},{7,6},{8,9},{9,8},{10,11... | collective-permute-start | bytes 2359304 | tf_op jit(solution)/shard_map/ppermute | solution.py:1167
  350.4 27.2 %collective-permute-start.44 = (bf16[512,768]{1,0:T(8,128)(2,1)}, bf16[512,768]{1,0:T(8,128)(2,1)}, u32[]{:S(2)}, u32[]{:S(2)}) collective-permute-start(bf16[512,768]{1,0:T(8,128)(2,1)} %collective-permute-done.42.refs_1_), channel_id=1, source_target_pairs={{0,1},{1,0},{2,3},{3,2},{4,5},{5,4},{6,7},{7,6},{8,9},{9,8},{10,11... | collective-permute-start | bytes 2359304 | tf_op jit(solution)/shard_map/ppermute | solution.py:1167
  353.0 28.2 %collective-permute-start.54 = (bf16[512,768]{1,0:T(8,128)(2,1)S(1)}, bf16[512,768]{1,0:T(8,128)(2,1)}, u32[]{:S(2)}, u32[]{:S(2)}) collective-permute-start(bf16[512,768]{1,0:T(8,128)(2,1)S(1)} %add_convert_fusion.1), channel_id=1, source_target_pairs={{0,2},{1,3},{2,0},{3,1},{4,6},{5,7},{6,4},{7,5},{8,10},{9,11},{10,... | collective-permute-start | bytes 2359304 | tf_op jit(solution)/shard_map/ppermute | solution.py:1167
  353.8 35.8 %collective-permute-start.52 = (bf16[512,768]{1,0:T(8,128)(2,1)S(1)}, bf16[512,768]{1,0:T(8,128)(2,1)}, u32[]{:S(2)}, u32[]{:S(2)}) collective-permute-start(bf16[512,768]{1,0:T(8,128)(2,1)S(1)} %add_convert_fusion.3), channel_id=1, source_target_pairs={{0,2},{1,3},{2,0},{3,1},{4,6},{5,7},{6,4},{7,5},{8,10},{9,11},{10,... | collective-permute-start | bytes 2359304 | tf_op jit(solution)/shard_map/ppermute | solution.py:1167
  382.5 15.5 %collective-permute-start.56 = (bf16[512,768]{1,0:T(8,128)(2,1)S(1)}, bf16[512,768]{1,0:T(8,128)(2,1)S(1)}, u32[]{:S(2)}, u32[]{:S(2)}) collective-permute-start(bf16[512,768]{1,0:T(8,128)(2,1)S(1)} %add_convert_fusion.refs_1_), channel_id=1, source_target_pairs={{0,1},{1,0},{2,3},{3,2},{4,5},{5,4},{6,7},{7,6},{8,9},{9,8},{10,11... | collective-permute-start | bytes 2359304 | tf_op jit(solution)/shard_map/ppermute | solution.py:1167
  (77 other events, 757.7 us)
Sparse Core Ops, SparseCore 0:
  10.8 85.2 all-gather.1
  313.6 85.6 reduce-scatter.1

commit v3 on v2

--- a/solution.py
+++ b/solution.py
@@ -521,9 +521,10 @@
     shard_ref[:, :D] = inner_ref[...]
     turned = output_ref[...].astype(f32).T
     shard_ref[:, D : 2 * D] = outer_ref[...]
-    shard_ref[:, 2 * D :] = jnp.concatenate(
-        [turned[:, at] for at in cut for _ in range(2)], axis=1
-    ).astype(bf16)
+    fill = -width % (2 * LANES)
+    if fill:
+        turned = jnp.concatenate([turned, jnp.zeros((depth, fill), f32)], axis=1)
+    shard_ref[:, 2 * D :] = turned.astype(bf16)
 
 
 def pack_weights(*arrays):
@@ -533,7 +534,7 @@
         pack_kernel,
         out_shape=[
             jax.ShapeDtypeStruct((max(depth, 16), columns + LANES), bf16),
-            jax.ShapeDtypeStruct((depth, 2 * D + 2 * width), bf16),
+            jax.ShapeDtypeStruct((depth, 2 * D + width + -width % (2 * LANES)), bf16),
         ],
         name="pack_weights",
         cost_estimate=QUICK,
@@ -646,15 +647,14 @@
     sum_ref,
     h2_ref,
     weight_ref,
+    double_ref,
     sems,
 ):
     step = pl.program_id(0)
     place = place_ref[1]
-    project = slice(2 * D, None)
 
     def fetch(t, part):
-        width = att0.shape[1]
-        at = (pl.ds(2 * D, width), pl.ds(0, 2 * D))[part]
+        at = (pl.ds(2 * D, weight_ref.shape[2] - 2 * D), pl.ds(0, 2 * D))[part]
         source = (w0, w1, w2, w3)[t]
         return pltpu.make_async_copy(source.at[:, at], weight_ref.at[t, :, at], sems.at[part, t])
 
@@ -672,6 +672,17 @@
             fetch(t, 1).start()
         for t in range(4):
             fetch(t, 0).wait()
+
+        @loop(4)
+        def _(t):
+            low = lane_iota(D) < HEAD_DIM
+            for k in range(double_ref.shape[2] // LANES):
+                tile = weight_ref[t, :, 2 * D + k // 2 * LANES : 2 * D + (k // 2 + 1) * LANES]
+                tile = tile.astype(f32)
+                turned = pltpu.roll(tile, HEAD_DIM, 1)
+                both = jnp.where(low, tile, turned) if k % 2 == 0 else jnp.where(low, turned, tile)
+                double_ref[t, :, k * LANES : (k + 1) * LANES] = both.astype(bf16)
+
         vec_ref[...] = jnp.zeros_like(vec_ref)
 
         @loop(2)
@@ -681,7 +692,7 @@
                 att = att_ref[...]
                 lane = lane_iota(256, att.shape[1]) % LANES
                 own = (lane >= HEAD_DIM).astype(i32) == side
-                branch = branch + nt(jnp.where(own, att, jnp.zeros_like(att)), weight_ref[t, :, project])
+                branch = branch + nt(jnp.where(own, att, jnp.zeros_like(att)), double_ref[t])
             at = pl.ds(pl.multiple_of(side * 256, 256), 256)
             rows = hidden_ref[at, :].astype(f32) + (branch + par_ref[2:3, :])
             normed, inv = norm_forward(rows)
@@ -758,7 +769,7 @@
             vec_ref[6:7, :] += jnp.sum(grad_first, axis=0, keepdims=True)
 
         for t, grad_ref in enumerate((grad0, grad1, grad2, grad3)):
-            both = nn(branch_grad_ref[...], weight_ref[t, :, project])
+            both = nn(branch_grad_ref[...], double_ref[t])
             lane = lane_iota(256, both.shape[1]) % LANES
             grad_ref[...] = jnp.where(lane < HEAD_DIM, both[:256], both[256:]).astype(bf16)
 
@@ -806,7 +817,8 @@
             pltpu.VMEM((4, rows, D), f32),
             pltpu.VMEM((rows, D), f32),
             pltpu.VMEM((rows, D), f32),
-            pltpu.VMEM((4, D, 2 * D + width), bf16),
+            pltpu.VMEM((4,) + weights[0].shape, bf16),
+            pltpu.VMEM((4, D, width), bf16),
             pltpu.SemaphoreType.DMA((2, 4)),
         ],
     )

time: 413 us -> 412 us (level)
    unnamed x98 -> x100, local copies, waits for them, and re-layouts: 13.8 us -> 14.4 us
  transfers between devices with their start and end apart: 60 -> 60, of which waited for: 24 -> 22; matrix products, arithmetic and copies ran while one was open for 2% -> 2% of each run, Pallas kernels for 28% -> 28%
where the time goes in v3:
time: 412 us; the launch traced here: 411 us
  Pallas kernels  147 us (36%)
  waiting for transfers between devices  130 us (32%)
  starting transfers between devices  93 us (23%)
  local copies, waits for them, and re-layouts  18.5 us (4%)
  between operations  14.5 us (4%)
  other arithmetic  7.33 us (2%)
    ppermute x28, starting transfers between devices, over_rows(): out.append(lax.ppermute(rows, 'dp', [(i, i ^ s) for i in range(lay.peers)]))  63.5 us
    ppermute x28, waiting for transfers between devices, over_rows(): out.append(lax.ppermute(rows, 'dp', [(i, i ^ s) for i in range(lay.peers)]))  62.1 us
    ppermute x22, waiting for transfers between devices, swap(): return lax.ppermute(rows, 'mp', [(i, i ^ flip) for i in range(4)])  32.2 us
    pallas_call x1, Pallas kernels, middle(): pl.pallas_call(middle_kernel, grid_spec=spec, out_shape=[jax.ShapeDtypeSt...  29.4 us
    pallas_call x3, Pallas kernels, weight_grads(): pl.pallas_call(partial(weight_grad_kernel, chunks, len(adds)), grid_spec=...  23.9 us
    ppermute x7, waiting for transfers between devices, flip(): return lax.ppermute(rows, 'dp', [(i, i ^ s) for i in range(lay.peers)])  19.1 us
    all_to_all x1, waiting for transfers between devices, on_device(): terms = lax.all_to_all(terms, 'dp', split_axis=0, concat_axis=0, tiled=True)  17 us
    pallas_call x1, Pallas kernels, project_rows(): pl.pallas_call(partial(project_kernel, lay, steps), grid_spec=spec, out_s...  15.2 us
  transfers between devices with their start and end apart: 60, of which 22 were waited for; matrix products, arithmetic and copies ran while one was open for 2% of the time, Pallas kernels for 28%

profile of v3, /device:TPU:0, one launch (start us, length us, event | category | flops | bytes accessed | tf_op | source)
XLA Modules:
  0.0 411.1 jit_solution(7022036236292986555)
XLA Ops:
  10.5 4.1 collective-permute-start.3
  18.1 3.8 collective-permute-done.3.refs_4_
  28.7 3.9 collective-permute-done.2.refs_3_
  32.6 8.3 %collective-permute-done.5.refs_6_ = bf16[96,768]{1,0:T(8,128)(2,1)S(1)} collective-permute-done((bf16[96,768]{1,0:T(8,128)(2,1)S(1)}, bf16[96,768]{1,0:T(8,128)(2,1)S(1)}, u32[]{:S(2)}, u32[]{:S(2)}) %collective-permute-start.5) | collective-permute-done | bytes 147488 | tf_op jit(solution)/shard_map/ppermute | solution.py:1166
  47.3 15.2 %project_rows.1 = (bf16[1168,128]{1,0:T(8,128)(2,1)}, bf16[1168,128]{1,0:T(8,128)(2,1)}, bf16[1168,128]{1,0:T(8,128)(2,1)}, bf16[1168,128]{1,0:T(8,128)(2,1)}, b...) custom-call(s32[2]{0:T(128)} %pad_add_fusion.1.place_ref, ...), custom_call_target="tpu_custom_call" | custom-call | flops 1000000 | bytes 3000 | tf_op jit(solution)/shard_map/project_rows/pallas_call | solution.py:288
  69.9 16.5 %collective-permute-done.8.refs_2_.refs_10_ = bf16[1168,128]{1,0:T(8,128)(2,1)S(1)} collective-permute-done((bf16[1168,128]{1,0:T(8,128)(2,1)}, bf16[1168,128]{1,0:T(8,128)(2,1)S(1)}, u32[]{:S(2)}, u32[]{:S(2)}) %collective-permute-start.8) | collective-permute-done | bytes 299040 | tf_op jit(solution)/shard_map/ppermute | solution.py:1156
  91.7 3.9 collective-permute-done.10.refs_4_.refs_12_
  97.1 17.4 %collective-permute-done.11.refs_5_.refs_13_ = bf16[1168,128]{1,0:T(8,128)(2,1)S(1)} collective-permute-done((bf16[1168,128]{1,0:T(8,128)(2,1)}, bf16[1168,128]{1,0:T(8,128)(2,1)S(1)}, u32[]{:S(2)}, u32[]{:S(2)}) %collective-permute-start.11) | collective-permute-done | bytes 299040 | tf_op jit(solution)/shard_map/ppermute | solution.py:1156
  116.2 5.2 %attend.1 = (bf16[384,128]{1,0:T(8,128)(2,1)}, bf16[384,128]{1,0:T(8,128)(2,1)}, bf16[384,128]{1,0:T(8,128)(2,1)}, bf16[384,128]{1,0:T(8,128)(2,1)}, bf16[384,12...) custom-call(bf16[1168,128]{1,0:T(8,128)(2,1)} %get-tuple-element.94.refs_0_.refs_, ...), custom_call_target="tpu_custom_call" | custom-call | flops 46000001024 | bytes 138000000 | tf_op jit(solution)/shard_map/attend/pallas_call | solution.py:363
  123.1 10.0 %collective-permute-start.15 = (bf16[384,128]{1,0:T(8,128)(2,1)}, bf16[384,128]{1,0:T(8,128)(2,1)S(1)}, u32[]{:S(2)}, u32[]{:S(2)}) collective-permute-start(bf16[384,128]{1,0:T(8,128)(2,1)} %get-tuple-element.106), channel_id=1, source_target_pairs={{0,8},{4,12},{8,0},{12,4},{16,24},{20,28},{24,16},{28,20},{1,9},{5... | collective-permute-start | bytes 294920 | tf_op jit(solution)/shard_map/ppermute | solution.py:1156
  142.9 5.5 %collective-permute-done.17.refs_4_ = bf16[384,128]{1,0:T(8,128)(2,1)S(1)} collective-permute-done((bf16[384,128]{1,0:T(8,128)(2,1)}, bf16[384,128]{1,0:T(8,128)(2,1)S(1)}, u32[]{:S(2)}, u32[]{:S(2)}) %collective-permute-start.17) | collective-permute-done | bytes 98336 | tf_op jit(solution)/shard_map/ppermute | solution.py:1156
  151.3 6.6 %unsort_rows.1 = (bf16[256,384]{1,0:T(8,128)(2,1)}, bf16[256,384]{1,0:T(8,128)(2,1)}, bf16[256,384]{1,0:T(8,128)(2,1)}, bf16[256,384]{1,0:T(8,128)(2,1)}) custom-call(s32[2]{0:T(128)} %pad_add_fusion.1.place_ref, bf16[384,128]{1,0:T(8,128)(2,1)} %get-tuple-element.104.refs_0_, bf16[384,128]{1,0:T(8,128)(2,1)} %copy-done.23, bf16[384,128]{1,0:T(8,128)(2,1)} %copy-done.24, ...), custom_call_target="tpu_custom_call" | custom-call | flops 1000000 | bytes 3000 | tf_op jit(solution)/shard_map/unsort_rows/pallas_call | solution.py:448
  160.4 7.1 %collective-permute-done.21.att1.refs_1_ = bf16[256,384]{1,0:T(8,128)(2,1)S(1)} collective-permute-done((bf16[256,384]{1,0:T(8,128)(2,1)}, bf16[256,384]{1,0:T(8,128)(2,1)S(1)}, u32[]{:S(2)}, u32[]{:S(2)}) %collective-permute-start.21) | collective-permute-done | bytes 196640 | tf_op jit(solution)/shard_map/ppermute | solution.py:1179
  173.0 29.4 %middle.1 = (bf16[512,768]{1,0:T(8,128)(2,1)}, bf16[512,3072]{1,0:T(8,128)(2,1)}, bf16[512,3072]{1,0:T(8,128)(2,1)}, bf16[512,768]{1,0:T(8,128)(2,1)}, bf16[512,...) custom-call(s32[2]{0:T(128)} %pad_add_fusion.1.place_ref, ...), custom_call_target="tpu_custom_call" | custom-call | flops 1000000 | bytes 3000 | tf_op jit(solution)/shard_map/middle/pallas_call | solution.py:825
  204.3 10.0 %weight_grads.3 = bf16[1536,1792]{1,0:T(8,128)(2,1)} custom-call(s32[2]{0:T(128)} %pad_add_fusion.1.place_ref, bf16[512,3072]{1,0:T(8,128)(2,1)} %get-tuple-element.141.act_ref, bf16[512,3072]{1,0:T(8,128)(2,1)} %get-tuple-element.137.pre_ref, bf16[512,768]{1,0:T(8,128)(2,1)} %get-tuple-element.138.low_ref, bf16[512,768]{1,0:T(8,128)(2,1)} %get-tuple-element.139.ffn_ref, ...), custom_call_target="tpu_custom_call" | custom-call | flops 1000000 | bytes 3000 | tf_op jit(solution)/shard_map/weight_grads/pallas_call | solution.py:895
  215.7 7.4 %sort_rows.1 = (bf16[384,128]{1,0:T(8,128)(2,1)}, bf16[384,128]{1,0:T(8,128)(2,1)}, bf16[384,128]{1,0:T(8,128)(2,1)}, bf16[384,128]{1,0:T(8,128)(2,1)}, bf16[384...) custom-call(s32[2]{0:T(128)} %pad_add_fusion.1.place_ref, ...), custom_call_target="tpu_custom_call" | custom-call | flops 80000000000 | bytes 240000000 | tf_op jit(solution)/shard_map/sort_rows/pallas_call | solution.py:487
  236.4 6.5 %weight_grads.4 = bf16[768,1792]{1,0:T(8,128)(2,1)} custom-call(s32[2]{0:T(128)} %pad_add_fusion.1.place_ref, bf16[512,3072]{1,0:T(8,128)(2,1)} %get-tuple-element.141.act_ref, bf16[512,3072]{1,0:T(8,128)(2,1)} %get-tuple-element.137.pre_ref, bf16[512,768]{1,0:T(8,128)(2,1)} %get-tuple-element.138.low_ref, bf16[512,768]{1,0:T(8,128)(2,1)} %get-tuple-element.139.ffn_ref, ...), custom_call_target="tpu_custom_call" | custom-call | flops 1000000 | bytes 3000 | tf_op jit(solution)/shard_map/weight_grads/pallas_call | solution.py:895
  245.8 10.7 %attend_back.1 = (bf16[1152,128]{1,0:T(8,128)(2,1)}, bf16[1152,128]{1,0:T(8,128)(2,1)}, bf16[1152,128]{1,0:T(8,128)(2,1)}, bf16[1152,128]{1,0:T(8,128)(2,1)}, bf...) custom-call(bf16[1168,128]{1,0:T(8,128)(2,1)} %get-tuple-element.94., ...), custom_call_target="tpu_custom_call" | custom-call | flops 40000000000 | bytes 120000000 | tf_op jit(solution)/shard_map/attend_back/pallas_call | solution.py:404
  264.6 5.8 %collective-permute-start.46 = (bf16[1152,128]{1,0:T(8,128)(2,1)}, bf16[1152,128]{1,0:T(8,128)(2,1)}, u32[]{:S(2)}, u32[]{:S(2)}) collective-permute-start(bf16[1152,128]{1,0:T(8,128)(2,1)} %get-tuple-element.145), channel_id=1, source_target_pairs={{0,20},{4,16},{8,28},{12,24},{16,4},{20,0},{24,12},{28,8},{1,21},{... | collective-permute-start | bytes 884744 | tf_op jit(solution)/shard_map/ppermute | solution.py:1156
  270.4 10.5 %collective-permute-done.38.refs_2_ = bf16[1152,128]{1,0:T(8,128)(2,1)S(1)} collective-permute-done((bf16[1152,128]{1,0:T(8,128)(2,1)}, bf16[1152,128]{1,0:T(8,128)(2,1)S(1)}, u32[]{:S(2)}, u32[]{:S(2)}) %collective-permute-start.38) | collective-permute-done | bytes 294944 | tf_op jit(solution)/shard_map/ppermute | solution.py:1156
  282.5 3.9 collective-permute-done.39.refs_3_
  290.6 12.5 %collective-permute-done.41.refs_2_ = bf16[768,1792]{1,0:T(8,128)(2,1)S(1)} collective-permute-done((bf16[768,1792]{1,0:T(8,128)(2,1)}, bf16[768,1792]{1,0:T(8,128)(2,1)S(1)}, u32[]{:S(2)}, u32[]{:S(2)}) %collective-permute-start.41) | collective-permute-done | bytes 2752544 | tf_op jit(solution)/shard_map/ppermute | solution.py:1179
  304.7 7.4 %weight_grads.5 = bf16[768,1792]{1,0:T(8,128)(2,1)} custom-call(s32[2]{0:T(128)} %pad_add_fusion.1.place_ref, bf16[512,3072]{1,0:T(8,128)(2,1)} %get-tuple-element.141.act_ref, bf16[512,3072]{1,0:T(8,128)(2,1)} %get-tuple-element.137.pre_ref, bf16[512,768]{1,0:T(8,128)(2,1)} %get-tuple-element.138.low_ref, bf16[512,768]{1,0:T(8,128)(2,1)} %get-tuple-element.139.ffn_ref, ...), custom_call_target="tpu_custom_call" | custom-call | flops 1000000 | bytes 3000 | tf_op jit(solution)/shard_map/weight_grads/pallas_call | solution.py:895
  314.7 10.9 %collect.1.dense_ref = bf16[2048,640]{1,0:T(8,128)(2,1)} custom-call(s32[2]{0:T(128)} %pad_add_fusion.1.place_ref, bf16[1152,128]{1,0:T(8,128)(2,1)} %get-tuple-element.143.refs_0_, bf16[1152,128]{1,0:T(8,128)(2,1)} %copy-done.39, bf16[1152,128]{1,0:T(8,128)(2,1)} %copy-done.40, bf16[1152,128]{1,0:T(8,128)(2,1)} %collective-permute-done.39.refs_3_, ...), custom_call_target="tpu_custom_call" | custom-call | flops 30000001024 | bytes 90000000 | tf_op jit(solution)/shard_map/collect/pallas_call | solution.py:944
  325.5 7.0 %head_grads.1 = bf16[8,112,640]{2,1,0:T(8,128)(2,1)} custom-call(s32[2]{0:T(128)} %pad_add_fusion.1.place_ref, bf16[2048,768]{1,0:T(8,128)(2,1)} %x_ref.3, bf16[2048,640]{1,0:T(8,128)(2,1)} %collect.1.dense_ref, f32[8,16,128]{2,1,0:T(8,128)} %select_maximum_fusion.vec_ref), custom_call_target="tpu_custom_call" | custom-call | flops 4000000000 | bytes 12000000 | tf_op jit(solution)/shard_map/head_grads/pallas_call | solution.py:1039
  332.6 5.1 %all-to-all-start = ((bf16[8,112,640]{2,1,0:T(8,128)(2,1)}), bf16[8,112,640]{2,1,0:T(8,128)(2,1)S(1)}, u32[]{:S(2)}, u32[]{:S(2)}) async-start(bf16[8,112,640]{2,1,0:T(8,128)(2,1)} %head_grads.1), calls=%async_computation | async-start | bytes 2293760 | tf_op jit(solution)/shard_map/all_to_all | solution.py:1273
  337.7 5.6 %spread_grads.3 = (bf16[512,768]{1,0:T(8,128)(2,1)}, bf16[512,768]{1,0:T(8,128)(2,1)}) custom-call(s32[2]{0:T(128)} %pad_add_fusion.1.place_ref, bf16[2048,640]{1,0:T(8,128)(2,1)} %collect.1.dense_ref, bf16[768,640]{1,0:T(8,128)(2,1)} %get-tuple-element.92.w_ref, f32[512,768]{1,0:T(8,128)} %get-tuple-element.154.h1_ref), custom_call_target="tpu_custom_call" | custom-call | flops 3000000000 | bytes 9000000 | tf_op jit(solution)/shard_map/spread_grads/pallas_call | solution.py:986
  343.3 5.7 %spread_grads.2 = (bf16[512,768]{1,0:T(8,128)(2,1)}, bf16[512,768]{1,0:T(8,128)(2,1)}) custom-call(s32[2]{0:T(128)} %pad_add_fusion.1.place_ref, bf16[2048,640]{1,0:T(8,128)(2,1)} %collect.1.dense_ref, bf16[768,640]{1,0:T(8,128)(2,1)} %get-tuple-element.92.w_ref, f32[512,768]{1,0:T(8,128)} %get-tuple-element.154.h1_ref), custom_call_target="tpu_custom_call" | custom-call | flops 3000000000 | bytes 9000000 | tf_op jit(solution)/shard_map/spread_grads/pallas_call | solution.py:986
  354.4 17.0 %all-to-all-done.refs_0_ = bf16[8,112,640]{2,1,0:T(8,128)(2,1)S(1)} async-done(((bf16[8,112,640]{2,1,0:T(8,128)(2,1)}), bf16[8,112,640]{2,1,0:T(8,128)(2,1)S(1)}, u32[]{:S(2)}, u32[]{:S(2)}) %all-to-all-start) | async-done | bytes 1146912 | tf_op jit(solution)/shard_map/all_to_all | solution.py:1273
  376.6 3.5 order_quarters.2
  381.7 6.9 %collective-permute-done.52 = bf16[512,768]{1,0:T(8,128)(2,1)} collective-permute-done((bf16[512,768]{1,0:T(8,128)(2,1)S(1)}, bf16[512,768]{1,0:T(8,128)(2,1)}, u32[]{:S(2)}, u32[]{:S(2)}) %collective-permute-start.52) | collective-permute-done | bytes 786464 | tf_op jit(solution)/shard_map/ppermute | solution.py:1179
  398.9 3.5 order_quarters.3
  (233 shorter events, 119.3 us)
Async XLA Ops:
  7.2 88.4 %all-gather.2.cloned.1.call-start = ((), (), s32[]{:S(2)}) async-start(), calls=%async_computation.2 | async-start | bytes 3096576 | tf_op jit(solution)/shard_map/all_gather | solution.py:1218
  10.5 392.0 %reduce-scatter.2.cloned.1.call-start = ((), (), s32[]{:S(2)}) async-start(), calls=%async_computation.3 | async-start | bytes 3096576 | tf_op jit(solution)/shard_map/reduce_scatter | solution.py:1258
  17.7 14.9 %collective-permute-start.2 = (bf16[96,768]{1,0:T(8,128)(2,1)}, bf16[96,768]{1,0:T(8,128)(2,1)S(1)}, u32[]{:S(2)}, u32[]{:S(2)}) collective-permute-start(bf16[96,768]{1,0:T(8,128)(2,1)} %get-tuple-element.91.refs_0_), channel_id=1, source_target_pairs={{0,12},{4,8},{8,4},{12,0},{16,28},{20,24},{24,20},{28,16},{1,13},{... | collective-permute-start | bytes 442376 | tf_op jit(solution)/shard_map/ppermute | solution.py:1166
  23.5 17.4 %collective-permute-start.5 = (bf16[96,768]{1,0:T(8,128)(2,1)S(1)}, bf16[96,768]{1,0:T(8,128)(2,1)S(1)}, u32[]{:S(2)}, u32[]{:S(2)}) collective-permute-start(bf16[96,768]{1,0:T(8,128)(2,1)S(1)} %collective-permute-done.3.refs_4_), channel_id=1, source_target_pairs={{0,8},{4,12},{8,0},{12,4},{16,24},{20,28},{24,16},{28,20},{1,9},{5... | collective-permute-start | bytes 442376 | tf_op jit(solution)/shard_map/ppermute | solution.py:1166
  24.2 19.7 %collective-permute-start.6 = (bf16[96,768]{1,0:T(8,128)(2,1)S(1)}, bf16[96,768]{1,0:T(8,128)(2,1)S(1)}, u32[]{:S(2)}, u32[]{:S(2)}) collective-permute-start(bf16[96,768]{1,0:T(8,128)(2,1)S(1)} %collective-permute-done.3.refs_4_), channel_id=1, source_target_pairs={{0,12},{4,8},{8,4},{12,0},{16,28},{20,24},{24,20},{28,16},{1,13},{... | collective-permute-start | bytes 442376 | tf_op jit(solution)/shard_map/ppermute | solution.py:1166
  62.5 24.0 %collective-permute-start.8 = (bf16[1168,128]{1,0:T(8,128)(2,1)}, bf16[1168,128]{1,0:T(8,128)(2,1)S(1)}, u32[]{:S(2)}, u32[]{:S(2)}) collective-permute-start(bf16[1168,128]{1,0:T(8,128)(2,1)} %get-tuple-element.96), channel_id=1, source_target_pairs={{0,8},{4,12},{8,0},{12,4},{16,24},{20,28},{24,16},{28,20},{1,9},{5... | collective-permute-start | bytes 897032 | tf_op jit(solution)/shard_map/ppermute | solution.py:1156
  62.5 26.4 %collective-permute-start.7 = (bf16[1168,128]{1,0:T(8,128)(2,1)}, bf16[1168,128]{1,0:T(8,128)(2,1)S(1)}, u32[]{:S(2)}, u32[]{:S(2)}) collective-permute-start(bf16[1168,128]{1,0:T(8,128)(2,1)} %get-tuple-element.95), channel_id=1, source_target_pairs={{0,4},{4,0},{8,12},{12,8},{16,20},{20,16},{24,28},{28,24},{1,5},{5... | collective-permute-start | bytes 897032 | tf_op jit(solution)/shard_map/ppermute | solution.py:1156
  64.2 31.4 %collective-permute-start.10 = (bf16[1168,128]{1,0:T(8,128)(2,1)}, bf16[1168,128]{1,0:T(8,128)(2,1)}, u32[]{:S(2)}, u32[]{:S(2)}) collective-permute-start(bf16[1168,128]{1,0:T(8,128)(2,1)} %get-tuple-element.98), channel_id=1, source_target_pairs={{0,16},{4,20},{8,24},{12,28},{16,0},{20,4},{24,8},{28,12},{1,17},{... | collective-permute-start | bytes 897032 | tf_op jit(solution)/shard_map/ppermute | solution.py:1156
  66.8 47.7 %collective-permute-start.11 = (bf16[1168,128]{1,0:T(8,128)(2,1)}, bf16[1168,128]{1,0:T(8,128)(2,1)S(1)}, u32[]{:S(2)}, u32[]{:S(2)}) collective-permute-start(bf16[1168,128]{1,0:T(8,128)(2,1)} %get-tuple-element.99), channel_id=1, source_target_pairs={{0,20},{4,16},{8,28},{12,24},{16,4},{20,0},{24,12},{28,8},{1,21},{... | collective-permute-start | bytes 897032 | tf_op jit(solution)/shard_map/ppermute | solution.py:1156
  66.9 47.6 %collective-permute-start.9 = (bf16[1168,128]{1,0:T(8,128)(2,1)}, bf16[1168,128]{1,0:T(8,128)(2,1)S(1)}, u32[]{:S(2)}, u32[]{:S(2)}) collective-permute-start(bf16[1168,128]{1,0:T(8,128)(2,1)} %get-tuple-element.97), channel_id=1, source_target_pairs={{0,12},{4,8},{8,4},{12,0},{16,28},{20,24},{24,20},{28,16},{1,13},{... | collective-permute-start | bytes 897032 | tf_op jit(solution)/shard_map/ppermute | solution.py:1156
  86.4 28.1 %collective-permute-start.13 = (bf16[1168,128]{1,0:T(8,128)(2,1)}, bf16[1168,128]{1,0:T(8,128)(2,1)S(1)}, u32[]{:S(2)}, u32[]{:S(2)}) collective-permute-start(bf16[1168,128]{1,0:T(8,128)(2,1)} %get-tuple-element.103), channel_id=1, source_target_pairs={{0,28},{4,24},{8,20},{12,16},{16,12},{20,8},{24,4},{28,0},{1,29},{... | collective-permute-start | bytes 897032 | tf_op jit(solution)/shard_map/ppermute | solution.py:1156
  88.8 25.8 %collective-permute-start.12 = (bf16[1168,128]{1,0:T(8,128)(2,1)}, bf16[1168,128]{1,0:T(8,128)(2,1)S(1)}, u32[]{:S(2)}, u32[]{:S(2)}) collective-permute-start(bf16[1168,128]{1,0:T(8,128)(2,1)} %get-tuple-element.101), channel_id=1, source_target_pairs={{0,24},{4,28},{8,16},{12,20},{16,8},{20,12},{24,0},{28,4},{1,25},{... | collective-permute-start | bytes 897032 | tf_op jit(solution)/shard_map/ppermute | solution.py:1156
  95.6 62.4 %collective-permute-start.25 = (bf16[768,1792]{1,0:T(8,128)(2,1)}, bf16[768,1792]{1,0:T(8,128)(2,1)}, u32[]{:S(2)}, u32[]{:S(2)}) collective-permute-start(bf16[768,1792]{1,0:T(8,128)(2,1)} %all-gather.2.cloned.1.call-done.w0), channel_id=1, source_target_pairs={{0,2},{1,3},{2,0},{3,1},{4,6},{5,7},{6,4},{7,5},{8,10},{9,11},{10,... | collective-permute-start | bytes 8257544 | tf_op jit(solution)/shard_map/ppermute | solution.py:1179
  123.1 15.9 %collective-permute-start.15 = (bf16[384,128]{1,0:T(8,128)(2,1)}, bf16[384,128]{1,0:T(8,128)(2,1)S(1)}, u32[]{:S(2)}, u32[]{:S(2)}) collective-permute-start(bf16[384,128]{1,0:T(8,128)(2,1)} %get-tuple-element.106), channel_id=1, source_target_pairs={{0,8},{4,12},{8,0},{12,4},{16,24},{20,28},{24,16},{28,20},{1,9},{5... | collective-permute-start | bytes 294920 | tf_op jit(solution)/shard_map/ppermute | solution.py:1156
  214.3 19.7 %collective-permute-start.40 = (bf16[1536,1792]{1,0:T(8,128)(2,1)}, bf16[1536,1792]{1,0:T(8,128)(2,1)}, u32[]{:S(2)}, u32[]{:S(2)}) collective-permute-start(bf16[1536,1792]{1,0:T(8,128)(2,1)} %weight_grads.3), channel_id=1, source_target_pairs={{0,1},{1,0},{2,3},{3,2},{4,5},{5,4},{6,7},{7,6},{8,9},{9,8},{10,11... | collective-permute-start | bytes 16515080 | tf_op jit(solution)/shard_map/ppermute | solution.py:1179
  227.3 15.6 %collective-permute-start.32 = (bf16[384,128]{1,0:T(8,128)(2,1)}, bf16[384,128]{1,0:T(8,128)(2,1)S(1)}, u32[]{:S(2)}, u32[]{:S(2)}) collective-permute-start(bf16[384,128]{1,0:T(8,128)(2,1)} %get-tuple-element.128), channel_id=1, source_target_pairs={{0,12},{4,8},{8,4},{12,0},{16,28},{20,24},{24,20},{28,16},{1,13},{... | collective-permute-start | bytes 294920 | tf_op jit(solution)/shard_map/ppermute | solution.py:1156
  227.7 16.7 %collective-permute-start.33 = (bf16[384,128]{1,0:T(8,128)(2,1)}, bf16[384,128]{1,0:T(8,128)(2,1)S(1)}, u32[]{:S(2)}, u32[]{:S(2)}) collective-permute-start(bf16[384,128]{1,0:T(8,128)(2,1)} %get-tuple-element.129), channel_id=1, source_target_pairs={{0,16},{4,20},{8,24},{12,28},{16,0},{20,4},{24,8},{28,12},{1,17},{... | collective-permute-start | bytes 294920 | tf_op jit(solution)/shard_map/ppermute | solution.py:1156
  230.3 14.8 %collective-permute-start.34 = (bf16[384,128]{1,0:T(8,128)(2,1)}, bf16[384,128]{1,0:T(8,128)(2,1)S(1)}, u32[]{:S(2)}, u32[]{:S(2)}) collective-permute-start(bf16[384,128]{1,0:T(8,128)(2,1)} %get-tuple-element.130), channel_id=1, source_target_pairs={{0,20},{4,16},{8,28},{12,24},{16,4},{20,0},{24,12},{28,8},{1,21},{... | collective-permute-start | bytes 294920 | tf_op jit(solution)/shard_map/ppermute | solution.py:1156
  243.0 60.2 %collective-permute-start.41 = (bf16[768,1792]{1,0:T(8,128)(2,1)}, bf16[768,1792]{1,0:T(8,128)(2,1)S(1)}, u32[]{:S(2)}, u32[]{:S(2)}) collective-permute-start(bf16[768,1792]{1,0:T(8,128)(2,1)} %weight_grads.4), channel_id=1, source_target_pairs={{0,2},{1,3},{2,0},{3,1},{4,6},{5,7},{6,4},{7,5},{8,10},{9,11},{10,... | collective-permute-start | bytes 8257544 | tf_op jit(solution)/shard_map/ppermute | solution.py:1179
  257.7 23.2 %collective-permute-start.38 = (bf16[1152,128]{1,0:T(8,128)(2,1)}, bf16[1152,128]{1,0:T(8,128)(2,1)S(1)}, u32[]{:S(2)}, u32[]{:S(2)}) collective-permute-start(bf16[1152,128]{1,0:T(8,128)(2,1)} %get-tuple-element.134), channel_id=1, source_target_pairs={{0,8},{4,12},{8,0},{12,4},{16,24},{20,28},{24,16},{28,20},{1,9},{5... | collective-permute-start | bytes 884744 | tf_op jit(solution)/shard_map/ppermute | solution.py:1156
  261.1 25.3 %collective-permute-start.39 = (bf16[1152,128]{1,0:T(8,128)(2,1)}, bf16[1152,128]{1,0:T(8,128)(2,1)}, u32[]{:S(2)}, u32[]{:S(2)}) collective-permute-start(bf16[1152,128]{1,0:T(8,128)(2,1)} %get-tuple-element.135), channel_id=1, source_target_pairs={{0,12},{4,8},{8,4},{12,0},{16,28},{20,24},{24,20},{28,16},{1,13},{... | collective-permute-start | bytes 884744 | tf_op jit(solution)/shard_map/ppermute | solution.py:1156
  261.7 50.5 %collective-permute-start.45 = (bf16[1152,128]{1,0:T(8,128)(2,1)}, bf16[1152,128]{1,0:T(8,128)(2,1)}, u32[]{:S(2)}, u32[]{:S(2)}) collective-permute-start(bf16[1152,128]{1,0:T(8,128)(2,1)} %get-tuple-element.144), channel_id=1, source_target_pairs={{0,16},{4,20},{8,24},{12,28},{16,0},{20,4},{24,8},{28,12},{1,17},{... | collective-permute-start | bytes 884744 | tf_op jit(solution)/shard_map/ppermute | solution.py:1156
  264.6 47.6 %collective-permute-start.46 = (bf16[1152,128]{1,0:T(8,128)(2,1)}, bf16[1152,128]{1,0:T(8,128)(2,1)}, u32[]{:S(2)}, u32[]{:S(2)}) collective-permute-start(bf16[1152,128]{1,0:T(8,128)(2,1)} %get-tuple-element.145), channel_id=1, source_target_pairs={{0,20},{4,16},{8,28},{12,24},{16,4},{20,0},{24,12},{28,8},{1,21},{... | collective-permute-start | bytes 884744 | tf_op jit(solution)/shard_map/ppermute | solution.py:1156
  280.9 31.3 %collective-permute-start.47 = (bf16[1152,128]{1,0:T(8,128)(2,1)}, bf16[1152,128]{1,0:T(8,128)(2,1)}, u32[]{:S(2)}, u32[]{:S(2)}) collective-permute-start(bf16[1152,128]{1,0:T(8,128)(2,1)} %get-tuple-element.146), channel_id=1, source_target_pairs={{0,24},{4,28},{8,16},{12,20},{16,8},{20,12},{24,0},{28,4},{1,25},{... | collective-permute-start | bytes 884744 | tf_op jit(solution)/shard_map/ppermute | solution.py:1156
  286.5 25.7 %collective-permute-start.48 = (bf16[1152,128]{1,0:T(8,128)(2,1)}, bf16[1152,128]{1,0:T(8,128)(2,1)}, u32[]{:S(2)}, u32[]{:S(2)}) collective-permute-start(bf16[1152,128]{1,0:T(8,128)(2,1)} %get-tuple-element.147), channel_id=1, source_target_pairs={{0,28},{4,24},{8,20},{12,16},{16,12},{20,8},{24,4},{28,0},{1,29},{... | collective-permute-start | bytes 884744 | tf_op jit(solution)/shard_map/ppermute | solution.py:1156
  313.2 24.4 %collective-permute-start.42 = (bf16[512,768]{1,0:T(8,128)(2,1)S(1)}, bf16[512,768]{1,0:T(8,128)(2,1)}, u32[]{:S(2)}, u32[]{:S(2)}) collective-permute-start(bf16[512,768]{1,0:T(8,128)(2,1)S(1)} %copy-done.10), channel_id=1, source_target_pairs={{0,2},{1,3},{2,0},{3,1},{4,6},{5,7},{6,4},{7,5},{8,10},{9,11},{10,... | collective-permute-start | bytes 2359304 | tf_op jit(solution)/shard_map/ppermute | solution.py:1179
  332.6 38.8 %all-to-all-start = ((bf16[8,112,640]{2,1,0:T(8,128)(2,1)}), bf16[8,112,640]{2,1,0:T(8,128)(2,1)S(1)}, u32[]{:S(2)}, u32[]{:S(2)}) async-start(bf16[8,112,640]{2,1,0:T(8,128)(2,1)} %head_grads.1), calls=%async_computation | async-start | bytes 2293760 | tf_op jit(solution)/shard_map/all_to_all | solution.py:1273
  349.3 27.3 %collective-permute-start.43 = (bf16[512,768]{1,0:T(8,128)(2,1)S(1)}, bf16[512,768]{1,0:T(8,128)(2,1)}, u32[]{:S(2)}, u32[]{:S(2)}) collective-permute-start(bf16[512,768]{1,0:T(8,128)(2,1)S(1)} %copy-done.10), channel_id=1, source_target_pairs={{0,1},{1,0},{2,3},{3,2},{4,5},{5,4},{6,7},{7,6},{8,9},{9,8},{10,11... | collective-permute-start | bytes 2359304 | tf_op jit(solution)/shard_map/ppermute | solution.py:1179
  349.5 27.1 %collective-permute-start.44 = (bf16[512,768]{1,0:T(8,128)(2,1)}, bf16[512,768]{1,0:T(8,128)(2,1)}, u32[]{:S(2)}, u32[]{:S(2)}) collective-permute-start(bf16[512,768]{1,0:T(8,128)(2,1)} %collective-permute-done.42.refs_1_), channel_id=1, source_target_pairs={{0,1},{1,0},{2,3},{3,2},{4,5},{5,4},{6,7},{7,6},{8,9},{9,8},{10,11... | collective-permute-start | bytes 2359304 | tf_op jit(solution)/shard_map/ppermute | solution.py:1179
  352.0 28.1 %collective-permute-start.54 = (bf16[512,768]{1,0:T(8,128)(2,1)S(1)}, bf16[512,768]{1,0:T(8,128)(2,1)}, u32[]{:S(2)}, u32[]{:S(2)}) collective-permute-start(bf16[512,768]{1,0:T(8,128)(2,1)S(1)} %add_convert_fusion.1), channel_id=1, source_target_pairs={{0,2},{1,3},{2,0},{3,1},{4,6},{5,7},{6,4},{7,5},{8,10},{9,11},{10,... | collective-permute-start | bytes 2359304 | tf_op jit(solution)/shard_map/ppermute | solution.py:1179
  352.9 35.8 %collective-permute-start.52 = (bf16[512,768]{1,0:T(8,128)(2,1)S(1)}, bf16[512,768]{1,0:T(8,128)(2,1)}, u32[]{:S(2)}, u32[]{:S(2)}) collective-permute-start(bf16[512,768]{1,0:T(8,128)(2,1)S(1)} %add_convert_fusion.3), channel_id=1, source_target_pairs={{0,2},{1,3},{2,0},{3,1},{4,6},{5,7},{6,4},{7,5},{8,10},{9,11},{10,... | collective-permute-start | bytes 2359304 | tf_op jit(solution)/shard_map/ppermute | solution.py:1179
  381.5 15.6 %collective-permute-start.56 = (bf16[512,768]{1,0:T(8,128)(2,1)S(1)}, bf16[512,768]{1,0:T(8,128)(2,1)S(1)}, u32[]{:S(2)}, u32[]{:S(2)}) collective-permute-start(bf16[512,768]{1,0:T(8,128)(2,1)S(1)} %add_convert_fusion.refs_1_), channel_id=1, source_target_pairs={{0,1},{1,0},{2,3},{3,2},{4,5},{5,4},{6,7},{7,6},{8,9},{9,8},{10,11... | collective-permute-start | bytes 2359304 | tf_op jit(solution)/shard_map/ppermute | solution.py:1179
  (78 other events, 726.8 us)
Sparse Core Ops, SparseCore 0:
  10.8 75.0 all-gather.1
  312.3 86.0 reduce-scatter.1

commit v4 on v3

--- a/solution.py
+++ b/solution.py
@@ -508,7 +508,7 @@
         columns.append(jnp.zeros((depth, fill), f32))
     columns = jnp.concatenate(columns, axis=1).astype(bf16)
     piece_ref[:depth, : have + fill] = columns
-    inner_bias = inner_bias_ref[...].astype(f32)
+    inner_bias = inner_bias_ref[...].astype(f32).reshape(1, -1)
     vectors = jnp.concatenate(
         [ref[...].astype(f32) for ref in (bias_ref, gain_ref, shift_ref)]
         + [inner_bias[:, i * depth : (i + 1) * depth] for i in range(4)]
@@ -1213,7 +1213,7 @@
 
     piece, shard = pack_weights(
         w_query, w_key, w_value, w_output, w_inner, w_outer.T,
-        biases, gains, shifts, inner_bias.reshape(1, -1),
+        biases, gains, shifts, inner_bias,
     )
     own_w = lax.all_gather(shard, "dp", axis=0, tiled=True)
     far_w = swap(own_w, 2)

time: 412 us -> 412 us (level)
  transfers between devices with their start and end apart: 60 -> 60, of which waited for: 22 -> 23; matrix products, arithmetic and copies ran while one was open for 2% -> 2% of each run, Pallas kernels for 28% -> 28%
where the time goes in v4:
time: 412 us; the launch traced here: 411 us
  Pallas kernels  147 us (36%)
  waiting for transfers between devices  130 us (32%)
  starting transfers between devices  94.9 us (23%)
  local copies, waits for them, and re-layouts  16.5 us (4%)
  between operations  14.6 us (4%)
  other arithmetic  7.33 us (2%)
    ppermute x28, starting transfers between devices, over_rows(): out.append(lax.ppermute(rows, 'dp', [(i, i ^ s) for i in range(lay.peers)]))  65.2 us
    ppermute x28, waiting for transfers between devices, over_rows(): out.append(lax.ppermute(rows, 'dp', [(i, i ^ s) for i in range(lay.peers)]))  63.5 us
    ppermute x22, waiting for transfers between devices, swap(): return lax.ppermute(rows, 'mp', [(i, i ^ flip) for i in range(4)])  32.1 us
    pallas_call x1, Pallas kernels, middle(): pl.pallas_call(middle_kernel, grid_spec=spec, out_shape=[jax.ShapeDtypeSt...  29.4 us
    pallas_call x3, Pallas kernels, weight_grads(): pl.pallas_call(partial(weight_grad_kernel, chunks, len(adds)), grid_spec=...  23.9 us
    ppermute x7, waiting for transfers between devices, flip(): return lax.ppermute(rows, 'dp', [(i, i ^ s) for i in range(lay.peers)])  17.8 us
    all_to_all x1, waiting for transfers between devices, on_device(): terms = lax.all_to_all(terms, 'dp', split_axis=0, concat_axis=0, tiled=True)  17 us
    pallas_call x1, Pallas kernels, project_rows(): pl.pallas_call(partial(project_kernel, lay, steps), grid_spec=spec, out_s...  15 us
  transfers between devices with their start and end apart: 60, of which 23 were waited for; matrix products, arithmetic and copies ran while one was open for 2% of the time, Pallas kernels for 28%

profile of v4, /device:TPU:0, one launch (start us, length us, event | category | flops | bytes accessed | tf_op | source)
XLA Modules:
  0.0 410.8 jit_solution(2939590770031033982)
XLA Ops:
  9.3 4.1 collective-permute-start.3
  16.9 3.8 collective-permute-done.3.refs_4_
  31.2 6.4 %collective-permute-done.5.refs_6_ = bf16[96,768]{1,0:T(8,128)(2,1)S(1)} collective-permute-done((bf16[96,768]{1,0:T(8,128)(2,1)S(1)}, bf16[96,768]{1,0:T(8,128)(2,1)S(1)}, u32[]{:S(2)}, u32[]{:S(2)}) %collective-permute-start.5) | collective-permute-done | bytes 147488 | tf_op jit(solution)/shard_map/ppermute | solution.py:1166
  37.6 3.8 collective-permute-done.6.refs_7_
  44.7 15.0 %project_rows.1 = (bf16[1168,128]{1,0:T(8,128)(2,1)}, bf16[1168,128]{1,0:T(8,128)(2,1)}, bf16[1168,128]{1,0:T(8,128)(2,1)}, bf16[1168,128]{1,0:T(8,128)(2,1)}, b...) custom-call(s32[2]{0:T(128)} %pad_add_fusion.1.place_ref, ...), custom_call_target="tpu_custom_call" | custom-call | flops 1000000 | bytes 3000 | tf_op jit(solution)/shard_map/project_rows/pallas_call | solution.py:288
  61.7 3.9 collective-permute-start.10
  67.5 17.8 %collective-permute-done.8.refs_2_.refs_10_ = bf16[1168,128]{1,0:T(8,128)(2,1)S(1)} collective-permute-done((bf16[1168,128]{1,0:T(8,128)(2,1)}, bf16[1168,128]{1,0:T(8,128)(2,1)S(1)}, u32[]{:S(2)}, u32[]{:S(2)}) %collective-permute-start.8) | collective-permute-done | bytes 299040 | tf_op jit(solution)/shard_map/ppermute | solution.py:1156
  94.8 18.4 %collective-permute-done.11.refs_5_.refs_13_ = bf16[1168,128]{1,0:T(8,128)(2,1)S(1)} collective-permute-done((bf16[1168,128]{1,0:T(8,128)(2,1)}, bf16[1168,128]{1,0:T(8,128)(2,1)S(1)}, u32[]{:S(2)}, u32[]{:S(2)}) %collective-permute-start.11) | collective-permute-done | bytes 299040 | tf_op jit(solution)/shard_map/ppermute | solution.py:1156
  114.9 5.2 %attend.1 = (bf16[384,128]{1,0:T(8,128)(2,1)}, bf16[384,128]{1,0:T(8,128)(2,1)}, bf16[384,128]{1,0:T(8,128)(2,1)}, bf16[384,128]{1,0:T(8,128)(2,1)}, bf16[384,12...) custom-call(bf16[1168,128]{1,0:T(8,128)(2,1)} %get-tuple-element.94.refs_0_.refs_, ...), custom_call_target="tpu_custom_call" | custom-call | flops 46000001024 | bytes 138000000 | tf_op jit(solution)/shard_map/attend/pallas_call | solution.py:363
  120.2 12.1 %collective-permute-start.15 = (bf16[384,128]{1,0:T(8,128)(2,1)}, bf16[384,128]{1,0:T(8,128)(2,1)S(1)}, u32[]{:S(2)}, u32[]{:S(2)}) collective-permute-start(bf16[384,128]{1,0:T(8,128)(2,1)} %get-tuple-element.106), channel_id=1, source_target_pairs={{0,8},{4,12},{8,0},{12,4},{16,24},{20,28},{24,16},{28,20},{1,9},{5... | collective-permute-start | bytes 294920 | tf_op jit(solution)/shard_map/ppermute | solution.py:1156
  142.4 5.2 %collective-permute-done.17.refs_4_ = bf16[384,128]{1,0:T(8,128)(2,1)S(1)} collective-permute-done((bf16[384,128]{1,0:T(8,128)(2,1)}, bf16[384,128]{1,0:T(8,128)(2,1)S(1)}, u32[]{:S(2)}, u32[]{:S(2)}) %collective-permute-start.17) | collective-permute-done | bytes 98336 | tf_op jit(solution)/shard_map/ppermute | solution.py:1156
  150.7 6.6 %unsort_rows.1 = (bf16[256,384]{1,0:T(8,128)(2,1)}, bf16[256,384]{1,0:T(8,128)(2,1)}, bf16[256,384]{1,0:T(8,128)(2,1)}, bf16[256,384]{1,0:T(8,128)(2,1)}) custom-call(s32[2]{0:T(128)} %pad_add_fusion.1.place_ref, bf16[384,128]{1,0:T(8,128)(2,1)} %get-tuple-element.104.refs_0_, bf16[384,128]{1,0:T(8,128)(2,1)} %copy-done.23, bf16[384,128]{1,0:T(8,128)(2,1)} %copy-done.24, ...), custom_call_target="tpu_custom_call" | custom-call | flops 1000000 | bytes 3000 | tf_op jit(solution)/shard_map/unsort_rows/pallas_call | solution.py:448
  159.8 7.1 %collective-permute-done.21.att1.refs_1_ = bf16[256,384]{1,0:T(8,128)(2,1)S(1)} collective-permute-done((bf16[256,384]{1,0:T(8,128)(2,1)}, bf16[256,384]{1,0:T(8,128)(2,1)S(1)}, u32[]{:S(2)}, u32[]{:S(2)}) %collective-permute-start.21) | collective-permute-done | bytes 196640 | tf_op jit(solution)/shard_map/ppermute | solution.py:1179
  172.4 29.4 %middle.1 = (bf16[512,768]{1,0:T(8,128)(2,1)}, bf16[512,3072]{1,0:T(8,128)(2,1)}, bf16[512,3072]{1,0:T(8,128)(2,1)}, bf16[512,768]{1,0:T(8,128)(2,1)}, bf16[512,...) custom-call(s32[2]{0:T(128)} %pad_add_fusion.1.place_ref, ...), custom_call_target="tpu_custom_call" | custom-call | flops 1000000 | bytes 3000 | tf_op jit(solution)/shard_map/middle/pallas_call | solution.py:825
  203.7 10.0 %weight_grads.3 = bf16[1536,1792]{1,0:T(8,128)(2,1)} custom-call(s32[2]{0:T(128)} %pad_add_fusion.1.place_ref, bf16[512,3072]{1,0:T(8,128)(2,1)} %get-tuple-element.141.act_ref, bf16[512,3072]{1,0:T(8,128)(2,1)} %get-tuple-element.137.pre_ref, bf16[512,768]{1,0:T(8,128)(2,1)} %get-tuple-element.138.low_ref, bf16[512,768]{1,0:T(8,128)(2,1)} %get-tuple-element.139.ffn_ref, ...), custom_call_target="tpu_custom_call" | custom-call | flops 1000000 | bytes 3000 | tf_op jit(solution)/shard_map/weight_grads/pallas_call | solution.py:895
  215.1 7.4 %sort_rows.1 = (bf16[384,128]{1,0:T(8,128)(2,1)}, bf16[384,128]{1,0:T(8,128)(2,1)}, bf16[384,128]{1,0:T(8,128)(2,1)}, bf16[384,128]{1,0:T(8,128)(2,1)}, bf16[384...) custom-call(s32[2]{0:T(128)} %pad_add_fusion.1.place_ref, ...), custom_call_target="tpu_custom_call" | custom-call | flops 80000000000 | bytes 240000000 | tf_op jit(solution)/shard_map/sort_rows/pallas_call | solution.py:487
  223.8 3.5 collective-permute-start.31
  236.4 6.5 %weight_grads.4 = bf16[768,1792]{1,0:T(8,128)(2,1)} custom-call(s32[2]{0:T(128)} %pad_add_fusion.1.place_ref, bf16[512,3072]{1,0:T(8,128)(2,1)} %get-tuple-element.141.act_ref, bf16[512,3072]{1,0:T(8,128)(2,1)} %get-tuple-element.137.pre_ref, bf16[512,768]{1,0:T(8,128)(2,1)} %get-tuple-element.138.low_ref, bf16[512,768]{1,0:T(8,128)(2,1)} %get-tuple-element.139.ffn_ref, ...), custom_call_target="tpu_custom_call" | custom-call | flops 1000000 | bytes 3000 | tf_op jit(solution)/shard_map/weight_grads/pallas_call | solution.py:895
  245.7 10.7 %attend_back.1 = (bf16[1152,128]{1,0:T(8,128)(2,1)}, bf16[1152,128]{1,0:T(8,128)(2,1)}, bf16[1152,128]{1,0:T(8,128)(2,1)}, bf16[1152,128]{1,0:T(8,128)(2,1)}, bf...) custom-call(bf16[1168,128]{1,0:T(8,128)(2,1)} %get-tuple-element.94., ...), custom_call_target="tpu_custom_call" | custom-call | flops 40000000000 | bytes 120000000 | tf_op jit(solution)/shard_map/attend_back/pallas_call | solution.py:404
  264.6 5.7 %collective-permute-start.46 = (bf16[1152,128]{1,0:T(8,128)(2,1)}, bf16[1152,128]{1,0:T(8,128)(2,1)}, u32[]{:S(2)}, u32[]{:S(2)}) collective-permute-start(bf16[1152,128]{1,0:T(8,128)(2,1)} %get-tuple-element.145), channel_id=1, source_target_pairs={{0,20},{4,16},{8,28},{12,24},{16,4},{20,0},{24,12},{28,8},{1,21},{... | collective-permute-start | bytes 884744 | tf_op jit(solution)/shard_map/ppermute | solution.py:1156
  270.3 10.1 %collective-permute-done.38.refs_2_ = bf16[1152,128]{1,0:T(8,128)(2,1)S(1)} collective-permute-done((bf16[1152,128]{1,0:T(8,128)(2,1)}, bf16[1152,128]{1,0:T(8,128)(2,1)S(1)}, u32[]{:S(2)}, u32[]{:S(2)}) %collective-permute-start.38) | collective-permute-done | bytes 294944 | tf_op jit(solution)/shard_map/ppermute | solution.py:1156
  282.5 3.9 collective-permute-done.39.refs_3_
  290.5 12.6 %collective-permute-done.41.refs_2_ = bf16[768,1792]{1,0:T(8,128)(2,1)S(1)} collective-permute-done((bf16[768,1792]{1,0:T(8,128)(2,1)}, bf16[768,1792]{1,0:T(8,128)(2,1)S(1)}, u32[]{:S(2)}, u32[]{:S(2)}) %collective-permute-start.41) | collective-permute-done | bytes 2752544 | tf_op jit(solution)/shard_map/ppermute | solution.py:1179
  304.6 7.4 %weight_grads.5 = bf16[768,1792]{1,0:T(8,128)(2,1)} custom-call(s32[2]{0:T(128)} %pad_add_fusion.1.place_ref, bf16[512,3072]{1,0:T(8,128)(2,1)} %get-tuple-element.141.act_ref, bf16[512,3072]{1,0:T(8,128)(2,1)} %get-tuple-element.137.pre_ref, bf16[512,768]{1,0:T(8,128)(2,1)} %get-tuple-element.138.low_ref, bf16[512,768]{1,0:T(8,128)(2,1)} %get-tuple-element.139.ffn_ref, ...), custom_call_target="tpu_custom_call" | custom-call | flops 1000000 | bytes 3000 | tf_op jit(solution)/shard_map/weight_grads/pallas_call | solution.py:895
  314.6 10.9 %collect.1.dense_ref = bf16[2048,640]{1,0:T(8,128)(2,1)} custom-call(s32[2]{0:T(128)} %pad_add_fusion.1.place_ref, bf16[1152,128]{1,0:T(8,128)(2,1)} %get-tuple-element.143.refs_0_, bf16[1152,128]{1,0:T(8,128)(2,1)} %copy-done.39, bf16[1152,128]{1,0:T(8,128)(2,1)} %copy-done.40, bf16[1152,128]{1,0:T(8,128)(2,1)} %collective-permute-done.39.refs_3_, ...), custom_call_target="tpu_custom_call" | custom-call | flops 30000001024 | bytes 90000000 | tf_op jit(solution)/shard_map/collect/pallas_call | solution.py:944
  325.5 7.1 %head_grads.1 = bf16[8,112,640]{2,1,0:T(8,128)(2,1)} custom-call(s32[2]{0:T(128)} %pad_add_fusion.1.place_ref, bf16[2048,768]{1,0:T(8,128)(2,1)} %x_ref.3, bf16[2048,640]{1,0:T(8,128)(2,1)} %collect.1.dense_ref, f32[8,16,128]{2,1,0:T(8,128)} %select_maximum_fusion.vec_ref), custom_call_target="tpu_custom_call" | custom-call | flops 4000000000 | bytes 12000000 | tf_op jit(solution)/shard_map/head_grads/pallas_call | solution.py:1039
  332.6 4.8 %all-to-all-start = ((bf16[8,112,640]{2,1,0:T(8,128)(2,1)}), bf16[8,112,640]{2,1,0:T(8,128)(2,1)S(1)}, u32[]{:S(2)}, u32[]{:S(2)}) async-start(bf16[8,112,640]{2,1,0:T(8,128)(2,1)} %head_grads.1), calls=%async_computation | async-start | bytes 2293760 | tf_op jit(solution)/shard_map/all_to_all | solution.py:1273
  337.4 5.6 %spread_grads.3 = (bf16[512,768]{1,0:T(8,128)(2,1)}, bf16[512,768]{1,0:T(8,128)(2,1)}) custom-call(s32[2]{0:T(128)} %pad_add_fusion.1.place_ref, bf16[2048,640]{1,0:T(8,128)(2,1)} %collect.1.dense_ref, bf16[768,640]{1,0:T(8,128)(2,1)} %get-tuple-element.92.w_ref, f32[512,768]{1,0:T(8,128)} %get-tuple-element.154.h1_ref), custom_call_target="tpu_custom_call" | custom-call | flops 3000000000 | bytes 9000000 | tf_op jit(solution)/shard_map/spread_grads/pallas_call | solution.py:986
  343.0 5.7 %spread_grads.2 = (bf16[512,768]{1,0:T(8,128)(2,1)}, bf16[512,768]{1,0:T(8,128)(2,1)}) custom-call(s32[2]{0:T(128)} %pad_add_fusion.1.place_ref, bf16[2048,640]{1,0:T(8,128)(2,1)} %collect.1.dense_ref, bf16[768,640]{1,0:T(8,128)(2,1)} %get-tuple-element.92.w_ref, f32[512,768]{1,0:T(8,128)} %get-tuple-element.154.h1_ref), custom_call_target="tpu_custom_call" | custom-call | flops 3000000000 | bytes 9000000 | tf_op jit(solution)/shard_map/spread_grads/pallas_call | solution.py:986
  354.1 17.0 %all-to-all-done.refs_0_ = bf16[8,112,640]{2,1,0:T(8,128)(2,1)S(1)} async-done(((bf16[8,112,640]{2,1,0:T(8,128)(2,1)}), bf16[8,112,640]{2,1,0:T(8,128)(2,1)S(1)}, u32[]{:S(2)}, u32[]{:S(2)}) %all-to-all-start) | async-done | bytes 1146912 | tf_op jit(solution)/shard_map/all_to_all | solution.py:1273
  376.3 3.5 order_quarters.2
  381.4 6.9 %collective-permute-done.52 = bf16[512,768]{1,0:T(8,128)(2,1)} collective-permute-done((bf16[512,768]{1,0:T(8,128)(2,1)S(1)}, bf16[512,768]{1,0:T(8,128)(2,1)}, u32[]{:S(2)}, u32[]{:S(2)}) %collective-permute-start.52) | collective-permute-done | bytes 786464 | tf_op jit(solution)/shard_map/ppermute | solution.py:1179
  (232 shorter events, 117.8 us)
Async XLA Ops:
  7.2 85.9 %all-gather.2.cloned.1.call-start = ((), (), s32[]{:S(2)}) async-start(), calls=%async_computation.2 | async-start | bytes 3096576 | tf_op jit(solution)/shard_map/all_gather | solution.py:1218
  9.2 392.9 %reduce-scatter.2.cloned.1.call-start = ((), (), s32[]{:S(2)}) async-start(), calls=%async_computation.3 | async-start | bytes 3096576 | tf_op jit(solution)/shard_map/reduce_scatter | solution.py:1258
  22.3 15.3 %collective-permute-start.5 = (bf16[96,768]{1,0:T(8,128)(2,1)S(1)}, bf16[96,768]{1,0:T(8,128)(2,1)S(1)}, u32[]{:S(2)}, u32[]{:S(2)}) collective-permute-start(bf16[96,768]{1,0:T(8,128)(2,1)S(1)} %collective-permute-done.3.refs_4_), channel_id=1, source_target_pairs={{0,8},{4,12},{8,0},{12,4},{16,24},{20,28},{24,16},{28,20},{1,9},{5... | collective-permute-start | bytes 442376 | tf_op jit(solution)/shard_map/ppermute | solution.py:1166
  23.0 18.4 %collective-permute-start.6 = (bf16[96,768]{1,0:T(8,128)(2,1)S(1)}, bf16[96,768]{1,0:T(8,128)(2,1)S(1)}, u32[]{:S(2)}, u32[]{:S(2)}) collective-permute-start(bf16[96,768]{1,0:T(8,128)(2,1)S(1)} %collective-permute-done.3.refs_4_), channel_id=1, source_target_pairs={{0,12},{4,8},{8,4},{12,0},{16,28},{20,24},{24,20},{28,16},{1,13},{... | collective-permute-start | bytes 442376 | tf_op jit(solution)/shard_map/ppermute | solution.py:1166
  59.8 25.6 %collective-permute-start.8 = (bf16[1168,128]{1,0:T(8,128)(2,1)}, bf16[1168,128]{1,0:T(8,128)(2,1)S(1)}, u32[]{:S(2)}, u32[]{:S(2)}) collective-permute-start(bf16[1168,128]{1,0:T(8,128)(2,1)} %get-tuple-element.96), channel_id=1, source_target_pairs={{0,8},{4,12},{8,0},{12,4},{16,24},{20,28},{24,16},{28,20},{1,9},{5... | collective-permute-start | bytes 897032 | tf_op jit(solution)/shard_map/ppermute | solution.py:1156
  59.8 27.6 %collective-permute-start.7 = (bf16[1168,128]{1,0:T(8,128)(2,1)}, bf16[1168,128]{1,0:T(8,128)(2,1)S(1)}, u32[]{:S(2)}, u32[]{:S(2)}) collective-permute-start(bf16[1168,128]{1,0:T(8,128)(2,1)} %get-tuple-element.95), channel_id=1, source_target_pairs={{0,4},{4,0},{8,12},{12,8},{16,20},{20,16},{24,28},{28,24},{1,5},{5... | collective-permute-start | bytes 897032 | tf_op jit(solution)/shard_map/ppermute | solution.py:1156
  61.7 31.4 %collective-permute-start.10 = (bf16[1168,128]{1,0:T(8,128)(2,1)}, bf16[1168,128]{1,0:T(8,128)(2,1)}, u32[]{:S(2)}, u32[]{:S(2)}) collective-permute-start(bf16[1168,128]{1,0:T(8,128)(2,1)} %get-tuple-element.98), channel_id=1, source_target_pairs={{0,16},{4,20},{8,24},{12,28},{16,0},{20,4},{24,8},{28,12},{1,17},{... | collective-permute-start | bytes 897032 | tf_op jit(solution)/shard_map/ppermute | solution.py:1156
  65.6 47.7 %collective-permute-start.11 = (bf16[1168,128]{1,0:T(8,128)(2,1)}, bf16[1168,128]{1,0:T(8,128)(2,1)S(1)}, u32[]{:S(2)}, u32[]{:S(2)}) collective-permute-start(bf16[1168,128]{1,0:T(8,128)(2,1)} %get-tuple-element.99), channel_id=1, source_target_pairs={{0,20},{4,16},{8,28},{12,24},{16,4},{20,0},{24,12},{28,8},{1,21},{... | collective-permute-start | bytes 897032 | tf_op jit(solution)/shard_map/ppermute | solution.py:1156
  65.6 47.7 %collective-permute-start.9 = (bf16[1168,128]{1,0:T(8,128)(2,1)}, bf16[1168,128]{1,0:T(8,128)(2,1)S(1)}, u32[]{:S(2)}, u32[]{:S(2)}) collective-permute-start(bf16[1168,128]{1,0:T(8,128)(2,1)} %get-tuple-element.97), channel_id=1, source_target_pairs={{0,12},{4,8},{8,4},{12,0},{16,28},{20,24},{24,20},{28,16},{1,13},{... | collective-permute-start | bytes 897032 | tf_op jit(solution)/shard_map/ppermute | solution.py:1156
  85.3 27.9 %collective-permute-start.13 = (bf16[1168,128]{1,0:T(8,128)(2,1)}, bf16[1168,128]{1,0:T(8,128)(2,1)S(1)}, u32[]{:S(2)}, u32[]{:S(2)}) collective-permute-start(bf16[1168,128]{1,0:T(8,128)(2,1)} %get-tuple-element.103), channel_id=1, source_target_pairs={{0,28},{4,24},{8,20},{12,16},{16,12},{20,8},{24,4},{28,0},{1,29},{... | collective-permute-start | bytes 897032 | tf_op jit(solution)/shard_map/ppermute | solution.py:1156
  87.3 26.8 %collective-permute-start.12 = (bf16[1168,128]{1,0:T(8,128)(2,1)}, bf16[1168,128]{1,0:T(8,128)(2,1)S(1)}, u32[]{:S(2)}, u32[]{:S(2)}) collective-permute-start(bf16[1168,128]{1,0:T(8,128)(2,1)} %get-tuple-element.101), channel_id=1, source_target_pairs={{0,24},{4,28},{8,16},{12,20},{16,8},{20,12},{24,0},{28,4},{1,25},{... | collective-permute-start | bytes 897032 | tf_op jit(solution)/shard_map/ppermute | solution.py:1156
  93.1 64.3 %collective-permute-start.25 = (bf16[768,1792]{1,0:T(8,128)(2,1)}, bf16[768,1792]{1,0:T(8,128)(2,1)}, u32[]{:S(2)}, u32[]{:S(2)}) collective-permute-start(bf16[768,1792]{1,0:T(8,128)(2,1)} %all-gather.2.cloned.1.call-done.w0), channel_id=1, source_target_pairs={{0,2},{1,3},{2,0},{3,1},{4,6},{5,7},{6,4},{7,5},{8,10},{9,11},{10,... | collective-permute-start | bytes 8257544 | tf_op jit(solution)/shard_map/ppermute | solution.py:1179
  120.1 14.9 %collective-permute-start.14 = (bf16[384,128]{1,0:T(8,128)(2,1)}, bf16[384,128]{1,0:T(8,128)(2,1)S(1)}, u32[]{:S(2)}, u32[]{:S(2)}) collective-permute-start(bf16[384,128]{1,0:T(8,128)(2,1)} %get-tuple-element.105), channel_id=1, source_target_pairs={{0,4},{4,0},{8,12},{12,8},{16,20},{20,16},{24,28},{28,24},{1,5},{5... | collective-permute-start | bytes 294920 | tf_op jit(solution)/shard_map/ppermute | solution.py:1156
  120.2 18.0 %collective-permute-start.15 = (bf16[384,128]{1,0:T(8,128)(2,1)}, bf16[384,128]{1,0:T(8,128)(2,1)S(1)}, u32[]{:S(2)}, u32[]{:S(2)}) collective-permute-start(bf16[384,128]{1,0:T(8,128)(2,1)} %get-tuple-element.106), channel_id=1, source_target_pairs={{0,8},{4,12},{8,0},{12,4},{16,24},{20,28},{24,16},{28,20},{1,9},{5... | collective-permute-start | bytes 294920 | tf_op jit(solution)/shard_map/ppermute | solution.py:1156
  135.0 15.0 %collective-permute-start.18 = (bf16[384,128]{1,0:T(8,128)(2,1)}, bf16[384,128]{1,0:T(8,128)(2,1)S(1)}, u32[]{:S(2)}, u32[]{:S(2)}) collective-permute-start(bf16[384,128]{1,0:T(8,128)(2,1)} %get-tuple-element.109), channel_id=1, source_target_pairs={{0,20},{4,16},{8,28},{12,24},{16,4},{20,0},{24,12},{28,8},{1,21},{... | collective-permute-start | bytes 294920 | tf_op jit(solution)/shard_map/ppermute | solution.py:1156
  213.8 20.3 %collective-permute-start.40 = (bf16[1536,1792]{1,0:T(8,128)(2,1)}, bf16[1536,1792]{1,0:T(8,128)(2,1)}, u32[]{:S(2)}, u32[]{:S(2)}) collective-permute-start(bf16[1536,1792]{1,0:T(8,128)(2,1)} %weight_grads.3), channel_id=1, source_target_pairs={{0,1},{1,0},{2,3},{3,2},{4,5},{5,4},{6,7},{7,6},{8,9},{9,8},{10,11... | collective-permute-start | bytes 16515080 | tf_op jit(solution)/shard_map/ppermute | solution.py:1179
  227.3 15.6 %collective-permute-start.32 = (bf16[384,128]{1,0:T(8,128)(2,1)}, bf16[384,128]{1,0:T(8,128)(2,1)S(1)}, u32[]{:S(2)}, u32[]{:S(2)}) collective-permute-start(bf16[384,128]{1,0:T(8,128)(2,1)} %get-tuple-element.128), channel_id=1, source_target_pairs={{0,12},{4,8},{8,4},{12,0},{16,28},{20,24},{24,20},{28,16},{1,13},{... | collective-permute-start | bytes 294920 | tf_op jit(solution)/shard_map/ppermute | solution.py:1156
  227.4 17.0 %collective-permute-start.33 = (bf16[384,128]{1,0:T(8,128)(2,1)}, bf16[384,128]{1,0:T(8,128)(2,1)S(1)}, u32[]{:S(2)}, u32[]{:S(2)}) collective-permute-start(bf16[384,128]{1,0:T(8,128)(2,1)} %get-tuple-element.129), channel_id=1, source_target_pairs={{0,16},{4,20},{8,24},{12,28},{16,0},{20,4},{24,8},{28,12},{1,17},{... | collective-permute-start | bytes 294920 | tf_op jit(solution)/shard_map/ppermute | solution.py:1156
  242.9 60.2 %collective-permute-start.41 = (bf16[768,1792]{1,0:T(8,128)(2,1)}, bf16[768,1792]{1,0:T(8,128)(2,1)S(1)}, u32[]{:S(2)}, u32[]{:S(2)}) collective-permute-start(bf16[768,1792]{1,0:T(8,128)(2,1)} %weight_grads.4), channel_id=1, source_target_pairs={{0,2},{1,3},{2,0},{3,1},{4,6},{5,7},{6,4},{7,5},{8,10},{9,11},{10,... | collective-permute-start | bytes 8257544 | tf_op jit(solution)/shard_map/ppermute | solution.py:1179
  257.4 23.1 %collective-permute-start.38 = (bf16[1152,128]{1,0:T(8,128)(2,1)}, bf16[1152,128]{1,0:T(8,128)(2,1)S(1)}, u32[]{:S(2)}, u32[]{:S(2)}) collective-permute-start(bf16[1152,128]{1,0:T(8,128)(2,1)} %get-tuple-element.134), channel_id=1, source_target_pairs={{0,8},{4,12},{8,0},{12,4},{16,24},{20,28},{24,16},{28,20},{1,9},{5... | collective-permute-start | bytes 884744 | tf_op jit(solution)/shard_map/ppermute | solution.py:1156
  260.9 25.5 %collective-permute-start.39 = (bf16[1152,128]{1,0:T(8,128)(2,1)}, bf16[1152,128]{1,0:T(8,128)(2,1)}, u32[]{:S(2)}, u32[]{:S(2)}) collective-permute-start(bf16[1152,128]{1,0:T(8,128)(2,1)} %get-tuple-element.135), channel_id=1, source_target_pairs={{0,12},{4,8},{8,4},{12,0},{16,28},{20,24},{24,20},{28,16},{1,13},{... | collective-permute-start | bytes 884744 | tf_op jit(solution)/shard_map/ppermute | solution.py:1156
  261.6 50.4 %collective-permute-start.45 = (bf16[1152,128]{1,0:T(8,128)(2,1)}, bf16[1152,128]{1,0:T(8,128)(2,1)}, u32[]{:S(2)}, u32[]{:S(2)}) collective-permute-start(bf16[1152,128]{1,0:T(8,128)(2,1)} %get-tuple-element.144), channel_id=1, source_target_pairs={{0,16},{4,20},{8,24},{12,28},{16,0},{20,4},{24,8},{28,12},{1,17},{... | collective-permute-start | bytes 884744 | tf_op jit(solution)/shard_map/ppermute | solution.py:1156
  264.6 47.5 %collective-permute-start.46 = (bf16[1152,128]{1,0:T(8,128)(2,1)}, bf16[1152,128]{1,0:T(8,128)(2,1)}, u32[]{:S(2)}, u32[]{:S(2)}) collective-permute-start(bf16[1152,128]{1,0:T(8,128)(2,1)} %get-tuple-element.145), channel_id=1, source_target_pairs={{0,20},{4,16},{8,28},{12,24},{16,4},{20,0},{24,12},{28,8},{1,21},{... | collective-permute-start | bytes 884744 | tf_op jit(solution)/shard_map/ppermute | solution.py:1156
  280.4 31.6 %collective-permute-start.47 = (bf16[1152,128]{1,0:T(8,128)(2,1)}, bf16[1152,128]{1,0:T(8,128)(2,1)}, u32[]{:S(2)}, u32[]{:S(2)}) collective-permute-start(bf16[1152,128]{1,0:T(8,128)(2,1)} %get-tuple-element.146), channel_id=1, source_target_pairs={{0,24},{4,28},{8,16},{12,20},{16,8},{20,12},{24,0},{28,4},{1,25},{... | collective-permute-start | bytes 884744 | tf_op jit(solution)/shard_map/ppermute | solution.py:1156
  286.4 25.7 %collective-permute-start.48 = (bf16[1152,128]{1,0:T(8,128)(2,1)}, bf16[1152,128]{1,0:T(8,128)(2,1)}, u32[]{:S(2)}, u32[]{:S(2)}) collective-permute-start(bf16[1152,128]{1,0:T(8,128)(2,1)} %get-tuple-element.147), channel_id=1, source_target_pairs={{0,28},{4,24},{8,20},{12,16},{16,12},{20,8},{24,4},{28,0},{1,29},{... | collective-permute-start | bytes 884744 | tf_op jit(solution)/shard_map/ppermute | solution.py:1156
  313.2 24.2 %collective-permute-start.42 = (bf16[512,768]{1,0:T(8,128)(2,1)S(1)}, bf16[512,768]{1,0:T(8,128)(2,1)}, u32[]{:S(2)}, u32[]{:S(2)}) collective-permute-start(bf16[512,768]{1,0:T(8,128)(2,1)S(1)} %copy-done.10), channel_id=1, source_target_pairs={{0,2},{1,3},{2,0},{3,1},{4,6},{5,7},{6,4},{7,5},{8,10},{9,11},{10,... | collective-permute-start | bytes 2359304 | tf_op jit(solution)/shard_map/ppermute | solution.py:1179
  332.6 38.6 %all-to-all-start = ((bf16[8,112,640]{2,1,0:T(8,128)(2,1)}), bf16[8,112,640]{2,1,0:T(8,128)(2,1)S(1)}, u32[]{:S(2)}, u32[]{:S(2)}) async-start(bf16[8,112,640]{2,1,0:T(8,128)(2,1)} %head_grads.1), calls=%async_computation | async-start | bytes 2293760 | tf_op jit(solution)/shard_map/all_to_all | solution.py:1273
  349.0 27.3 %collective-permute-start.43 = (bf16[512,768]{1,0:T(8,128)(2,1)S(1)}, bf16[512,768]{1,0:T(8,128)(2,1)}, u32[]{:S(2)}, u32[]{:S(2)}) collective-permute-start(bf16[512,768]{1,0:T(8,128)(2,1)S(1)} %copy-done.10), channel_id=1, source_target_pairs={{0,1},{1,0},{2,3},{3,2},{4,5},{5,4},{6,7},{7,6},{8,9},{9,8},{10,11... | collective-permute-start | bytes 2359304 | tf_op jit(solution)/shard_map/ppermute | solution.py:1179
  349.2 27.2 %collective-permute-start.44 = (bf16[512,768]{1,0:T(8,128)(2,1)}, bf16[512,768]{1,0:T(8,128)(2,1)}, u32[]{:S(2)}, u32[]{:S(2)}) collective-permute-start(bf16[512,768]{1,0:T(8,128)(2,1)} %collective-permute-done.42.refs_1_), channel_id=1, source_target_pairs={{0,1},{1,0},{2,3},{3,2},{4,5},{5,4},{6,7},{7,6},{8,9},{9,8},{10,11... | collective-permute-start | bytes 2359304 | tf_op jit(solution)/shard_map/ppermute | solution.py:1179
  351.8 28.1 %collective-permute-start.54 = (bf16[512,768]{1,0:T(8,128)(2,1)S(1)}, bf16[512,768]{1,0:T(8,128)(2,1)}, u32[]{:S(2)}, u32[]{:S(2)}) collective-permute-start(bf16[512,768]{1,0:T(8,128)(2,1)S(1)} %add_convert_fusion.1), channel_id=1, source_target_pairs={{0,2},{1,3},{2,0},{3,1},{4,6},{5,7},{6,4},{7,5},{8,10},{9,11},{10,... | collective-permute-start | bytes 2359304 | tf_op jit(solution)/shard_map/ppermute | solution.py:1179
  352.6 35.7 %collective-permute-start.52 = (bf16[512,768]{1,0:T(8,128)(2,1)S(1)}, bf16[512,768]{1,0:T(8,128)(2,1)}, u32[]{:S(2)}, u32[]{:S(2)}) collective-permute-start(bf16[512,768]{1,0:T(8,128)(2,1)S(1)} %add_convert_fusion.3), channel_id=1, source_target_pairs={{0,2},{1,3},{2,0},{3,1},{4,6},{5,7},{6,4},{7,5},{8,10},{9,11},{10,... | collective-permute-start | bytes 2359304 | tf_op jit(solution)/shard_map/ppermute | solution.py:1179
  381.2 15.6 %collective-permute-start.56 = (bf16[512,768]{1,0:T(8,128)(2,1)S(1)}, bf16[512,768]{1,0:T(8,128)(2,1)S(1)}, u32[]{:S(2)}, u32[]{:S(2)}) collective-permute-start(bf16[512,768]{1,0:T(8,128)(2,1)S(1)} %add_convert_fusion.refs_1_), channel_id=1, source_target_pairs={{0,1},{1,0},{2,3},{3,2},{4,5},{5,4},{6,7},{7,6},{8,9},{9,8},{10,11... | collective-permute-start | bytes 2359304 | tf_op jit(solution)/shard_map/ppermute | solution.py:1179
  (78 other events, 725.5 us)
Sparse Core Ops, SparseCore 0:
  10.8 73.5 all-gather.1
  312.2 86.1 reduce-scatter.1
